TPU v7x, 32 devices: a whole 2x2x4 slice. The times are simulated.
32 devices in a mesh: groups: 2 (over y), space: 4 (over z), dp: 2 (over x), ysp: 2 (over core).
Axes of the slice: x: 2, y: 2, z: 4, core: 2. Of those that a mesh axis runs over, the one named last changes fastest.
Arguments:
- inputs: bfloat16 [4, 8, 16, 2048], P(('groups', 'dp'), 'space', 'ysp'), parts along dimension 0, may hold values from -6 to 6
- w_first: float32 [864, 64], replicated, may hold values from -0.21875 to 0.21875
- b_first: float32 [64], replicated, may hold values from -2 to 2
- w_second: float32 [1728, 64], replicated, may hold values from -0.15625 to 0.15625
- b_second: float32 [64], replicated, may hold values from -2 to 2
- cotangent: bfloat16 [4, 8, 16, 4096], P(('groups', 'dp'), 'space', 'ysp'), parts along dimension 0, may hold values from -16 to 16
Outputs:
- output: bfloat16 [4, 8, 16, 4096], P(('groups', 'dp'), 'space', 'ysp'), parts along dimension 0
- input_grad: bfloat16 [4, 8, 16, 2048], P(('groups', 'dp'), 'space', 'ysp'), parts along dimension 0
- grad_w_first: float32 [1728, 64], P('groups'), parts along dimension 0
- grad_b_first: float32 [128], P('groups'), parts along dimension 0
- grad_w_second: float32 [3456, 64], P('groups'), parts along dimension 0
- grad_b_second: float32 [128], P('groups'), parts along dimension 0
There are 2 independent parts, one for each index of `groups`. A program takes and returns all parts, laid end to end along the dimension named above; an argument that names none is the same for every part. Nothing has to cross between parts.
All inputs are finite; a program needn't handle non-finite values.
Results may differ from a plain program's by a relative error of at most 0.0075.
Values may be sent and summed in bfloat16 or wider, within the bound.
No kernel may reach another device: no remote copies, remote signals or barrier semaphores. Data moves between devices by JAX's collectives and lax.ppermute only.
A program may use at most 64 MiB of HBM per device.

v0:
```python
import jax
import jax.numpy as jnp
from jax import lax
from jax.sharding import PartitionSpec as P

C_IN = 32
C_MID = 64
DEPTH = 64


def padded_2(cells, sides, width):
    for axis, dim in sides:
        count = lax.axis_size(axis)
        ends = count - 1
        head = lax.slice_in_dim(cells, 0, width, axis=dim)
        tail = lax.slice_in_dim(cells, cells.shape[dim] - width, cells.shape[dim], axis=dim)
        cells = jnp.concatenate(
            [
                lax.ppermute(tail, axis, [(i, (i + 1) % count) for i in range(ends)]),
                cells,
                lax.ppermute(head, axis, [((i + 1) % count, i) for i in range(ends)]),
            ],
            axis=dim,
        )
    return cells


def columns(padded, chans):
    batch = padded.shape[0]
    wide_x = padded.shape[1] - 2
    wide_y = padded.shape[2] - 2
    cells = padded.reshape(batch, wide_x + 2, wide_y + 2, DEPTH, chans)
    cells = jnp.pad(cells, ((0, 0), (0, 0), (0, 0), (1, 1), (0, 0)))
    pieces = []
    for first in range(3):
        for second in range(3):
            for third in range(3):
                pieces.append(
                    cells[
                        :,
                        first : first + wide_x,
                        second : second + wide_y,
                        third : third + DEPTH,
                        :,
                    ]
                )
    return jnp.concatenate(pieces, axis=-1).reshape(-1, 27 * chans)


def flipped(weights, chans_in, chans_out):
    cube = weights.reshape(3, 3, 3, chans_in, chans_out)[::-1, ::-1, ::-1]
    return jnp.transpose(cube, (0, 1, 2, 4, 3)).reshape(27 * chans_out, chans_in)


def silu_grad(value):
    sig = jax.nn.sigmoid(value)
    return sig * (1.0 + value * (1.0 - sig))


def weight_term(patches, grads):
    return lax.dot_general(
        patches, grads, (((0,), (0,)), ((), ())), preferred_element_type=jnp.float32
    )


def on_device(inputs, w_first, b_first, w_second, b_second, cotangent):
    batch, cells_x, cells_y = (inputs.shape[0], inputs.shape[1], inputs.shape[2])
    w1_round = w_first.astype(jnp.bfloat16)
    w2_round = w_second.astype(jnp.bfloat16)
    in_padded = padded_2(inputs, (("space", 1), ("ysp", 2)), 1)
    first_cols = columns(in_padded, C_IN)
    y_first = jnp.dot(first_cols, w1_round, preferred_element_type=jnp.float32) + b_first
    act_first = (
        jax.nn.silu(y_first).astype(jnp.bfloat16).reshape(batch, cells_x, cells_y, DEPTH * C_MID)
    )
    mid_padded = padded_2(act_first, (("space", 1), ("ysp", 2)), 1)
    second_cols = columns(mid_padded, C_MID)
    y_second = jnp.dot(second_cols, w2_round, preferred_element_type=jnp.float32) + b_second
    output = (
        jax.nn.silu(y_second).astype(jnp.bfloat16).reshape(batch, cells_x, cells_y, DEPTH * C_MID)
    )
    g_second = (cotangent.reshape(-1, C_MID).astype(jnp.float32) * silu_grad(y_second)).astype(
        jnp.bfloat16
    )
    grad_w2 = weight_term(second_cols, g_second)
    grad_b2 = jnp.sum(g_second.astype(jnp.float32), axis=0)
    g2_padded = padded_2(
        g_second.reshape(batch, cells_x, cells_y, DEPTH * C_MID), (("space", 1), ("ysp", 2)), 1
    )
    d_first = jnp.dot(
        columns(g2_padded, C_MID),
        flipped(w2_round, C_MID, C_MID),
        preferred_element_type=jnp.float32,
    )
    g_first = (d_first * silu_grad(y_first)).astype(jnp.bfloat16)
    grad_w1 = weight_term(first_cols, g_first)
    grad_b1 = jnp.sum(g_first.astype(jnp.float32), axis=0)
    g1_padded = padded_2(
        g_first.reshape(batch, cells_x, cells_y, DEPTH * C_MID), (("space", 1), ("ysp", 2)), 1
    )
    d_input = jnp.dot(
        columns(g1_padded, C_MID),
        flipped(w1_round, C_IN, C_MID),
        preferred_element_type=jnp.float32,
    )
    input_grad = d_input.astype(jnp.bfloat16).reshape(batch, cells_x, cells_y, DEPTH * C_IN)
    grad_w1, grad_b1, grad_w2, grad_b2 = lax.psum(
        (grad_w1, grad_b1, grad_w2, grad_b2), ("space", "dp", "ysp")
    )
    return (output, input_grad, grad_w1, grad_b1, grad_w2, grad_b2)


def solution(mesh):
    placed = (
        P(("groups", "dp"), "space", "ysp", None),
        P(),
        P(),
        P(),
        P(),
        P(("groups", "dp"), "space", "ysp", None),
    )
    return jax.shard_map(
        on_device,
        mesh=mesh,
        in_specs=placed,
        out_specs=(
            P(("groups", "dp"), "space", "ysp", None),
            P(("groups", "dp"), "space", "ysp", None),
            P("groups", None),
            P("groups"),
            P("groups", None),
            P("groups"),
        ),
        check_vma=False,
    )
```

profile of v0, /device:TPU:0, one launch (start us, length us, event | category | flops | bytes accessed | tf_op | source)
XLA Modules:
  0.0 233.7 jit_solution(10804659027833530314)
XLA Ops:
  8.0 4.9 %collective-permute-start = (bf16[1,1,8,2048]{3,2,1,0:T(8,128)(2,1)S(1)}, bf16[1,1,8,2048]{3,2,1,0:T(8,128)(2,1)S(1)}, u32[]{:S(2)}, u32[]{:S(2)}) collective-permute-start(bf16[1,1,8,2048]{3,2,1,0:T(8,128)(2,1)S(1)} %get-tuple-element.136), channel_id=1, source_target_pairs={{0,4},{4,8},{8,12},{1,5},{5,9},{9,13},{2,6},{6,10},{10,14},{3,7},{... | collective-permute-start | bytes 98312 | tf_op jit(solution)/shard_map/ppermute | solution.py:19
  12.9 1.3 collective-permute-start.1
  15.3 3.4 %collective-permute-done.1 = bf16[1,1,8,2048]{3,2,1,0:T(8,128)(2,1)S(1)} collective-permute-done((bf16[1,1,8,2048]{3,2,1,0:T(8,128)(2,1)S(1)}, bf16[1,1,8,2048]{3,2,1,0:T(8,128)(2,1)S(1)}, u32[]{:S(2)}, u32[]{:S(2)}) %collective-permute-start.1) | collective-permute-done | bytes 32800 | tf_op jit(solution)/shard_map/ppermute | solution.py:21
  18.8 1.3 collective-permute-start.2
  20.1 1.3 collective-permute-start.3
  21.4 1.8 copy.27
  24.2 1.6 pad_slice_fusion.54
  25.8 1.8 pad_slice_fusion.55
  27.5 8.3 %concatenate.38 = bf16[1,2,8,64,864]{4,3,1,2,0:T(8,128)(2,1)} concatenate(bf16[1,2,8,64,32]{4,3,1,2,0:T(8,128)(2,1)S(1)} %get-tuple-element.119, bf16[1,2,8,64,32]{4,3,1,2,0:T(8,128)(2,1)S(1)} %get-tuple-element.118, bf16[1,2,8,64,32]{4,3,1,2,0:T(8,128)(2,1)S(1)} %get-tuple-element.94, bf16[1,2,8,64,32]{4,3,1,2,0:T(8,128)(2,1)S(1)} %get-tuple-element.95, ...), dimensions={4} | concatenate | bytes 3538944 | tf_op jit(solution)/shard_map/concatenate | solution.py:47
  35.9 1.7 copy.26
  37.7 1.4 multiply_convert_fusion.2
  39.6 3.5 %collective-permute-start.4 = (bf16[1,1,8,4096]{3,2,1,0:T(8,128)(2,1)S(1)}, bf16[1,1,8,4096]{3,2,1,0:T(8,128)(2,1)S(1)}, u32[]{:S(2)}, u32[]{:S(2)}) collective-permute-start(bf16[1,1,8,4096]{3,2,1,0:T(8,128)(2,1)S(1)} %get-tuple-element.132), channel_id=1, source_target_pairs={{0,4},{4,8},{8,12},{1,5},{5,9},{9,13},{2,6},{6,10},{10,14},{3,7},{... | collective-permute-start | bytes 196616 | tf_op jit(solution)/shard_map/ppermute | solution.py:19
  43.1 1.3 collective-permute-start.5
  45.4 4.4 %collective-permute-done.5 = bf16[1,1,8,4096]{3,2,1,0:T(8,128)(2,1)S(1)} collective-permute-done((bf16[1,1,8,4096]{3,2,1,0:T(8,128)(2,1)S(1)}, bf16[1,1,8,4096]{3,2,1,0:T(8,128)(2,1)S(1)}, u32[]{:S(2)}, u32[]{:S(2)}) %collective-permute-start.5) | collective-permute-done | bytes 65568 | tf_op jit(solution)/shard_map/ppermute | solution.py:21
  49.9 1.9 collective-permute-start.6
  51.8 1.3 collective-permute-start.7
  56.0 1.2 fusion.3
  57.2 1.9 pad_slice_fusion.36
  59.0 1.8 pad_slice_fusion.37
  60.8 8.8 %concatenate.41 = bf16[1,2,8,64,1728]{4,3,1,2,0:T(8,128)(2,1)} concatenate(bf16[1,2,8,64,64]{4,3,1,2,0:T(8,128)(2,1)} %get-tuple-element.92, bf16[1,2,8,64,64]{4,3,1,2,0:T(8,128)(2,1)} %get-tuple-element.91, bf16[1,2,8,64,64]{4,3,1,2,0:T(8,128)(2,1)} %get-tuple-element.67, bf16[1,2,8,64,64]{4,3,1,2,0:T(8,128)(2,1)} %get-tuple-element.68, ...), dimensions={4} | concatenate | bytes 7077888 | tf_op jit(solution)/shard_map/concatenate | solution.py:47
  69.7 2.4 %copy.30 = bf16[1,2,8,64,1728]{4,3,2,1,0:T(8,128)(2,1)S(1)} copy(bf16[1,2,8,64,1728]{4,3,1,2,0:T(8,128)(2,1)} %concatenate.41) | data formatting | bytes 7077888 | tf_op jit(solution)/shard_map/concatenate | solution.py:47
  72.2 2.0 convert_reduce_fusion
  75.4 3.5 %collective-permute-start.8 = (bf16[1,1,8,4096]{3,2,1,0:T(8,128)(2,1)S(1)}, bf16[1,1,8,4096]{3,2,1,0:T(8,128)(2,1)S(1)}, u32[]{:S(2)}, u32[]{:S(2)}) collective-permute-start(bf16[1,1,8,4096]{3,2,1,0:T(8,128)(2,1)S(1)} %get-tuple-element.130), channel_id=1, source_target_pairs={{0,4},{4,8},{8,12},{1,5},{5,9},{9,13},{2,6},{6,10},{10,14},{3,7},{... | collective-permute-start | bytes 196616 | tf_op jit(solution)/shard_map/ppermute | solution.py:19
  78.8 1.3 collective-permute-start.9
  81.2 4.4 %collective-permute-done.9 = bf16[1,1,8,4096]{3,2,1,0:T(8,128)(2,1)S(1)} collective-permute-done((bf16[1,1,8,4096]{3,2,1,0:T(8,128)(2,1)S(1)}, bf16[1,1,8,4096]{3,2,1,0:T(8,128)(2,1)S(1)}, u32[]{:S(2)}, u32[]{:S(2)}) %collective-permute-start.9) | collective-permute-done | bytes 65568 | tf_op jit(solution)/shard_map/ppermute | solution.py:21
  86.3 1.9 collective-permute-start.10
  88.2 1.5 collective-permute-start.11
  91.1 1.7 rev.6
  96.0 1.2 fusion.2
  97.2 1.8 pad_slice_fusion.18
  99.1 1.8 pad_slice_fusion.19
  100.8 8.8 %concatenate.44 = bf16[1,2,8,64,1728]{4,3,1,2,0:T(8,128)(2,1)} concatenate(bf16[1,2,8,64,64]{4,3,1,2,0:T(8,128)(2,1)} %get-tuple-element.65, bf16[1,2,8,64,64]{4,3,1,2,0:T(8,128)(2,1)} %get-tuple-element.64, bf16[1,2,8,64,64]{4,3,1,2,0:T(8,128)(2,1)} %get-tuple-element.40, bf16[1,2,8,64,64]{4,3,1,2,0:T(8,128)(2,1)} %get-tuple-element.41, ...), dimensions={4} | concatenate | bytes 7077888 | tf_op jit(solution)/shard_map/concatenate | solution.py:47
  109.7 2.4 %copy.35 = bf16[1,2,8,64,1728]{4,3,2,1,0:T(8,128)(2,1)S(1)} copy(bf16[1,2,8,64,1728]{4,3,1,2,0:T(8,128)(2,1)} %concatenate.44) | data formatting | bytes 7077888 | tf_op jit(solution)/shard_map/concatenate | solution.py:47
  112.2 1.3 convert_reduce_fusion.1
  114.0 2.3 collective-permute-start.12
  116.3 3.6 %fusion.14 = f32[1728,64]{0,1:T(8,128)} fusion(bf16[1024,64]{0,1:T(8,128)(2,1)S(1)} %copy-done.5, bf16[1024,1728]{1,0:T(8,128)(2,1)} %bitcast.38), kind=kOutput, calls=%fused_computation.114 | convolution fusion | flops 226492416 | bytes 4112384 | tf_op jit(solution)/shard_map/dot_general | solution.py:61
  121.0 1.3 collective-permute-start.13
  122.3 5.4 %collective-permute-done.13 = bf16[1,1,8,4096]{3,2,1,0:T(8,128)(2,1)S(1)} collective-permute-done((bf16[1,1,8,4096]{3,2,1,0:T(8,128)(2,1)S(1)}, bf16[1,1,8,4096]{3,2,1,0:T(8,128)(2,1)S(1)}, u32[]{:S(2)}, u32[]{:S(2)}) %collective-permute-start.13) | collective-permute-done | bytes 65568 | tf_op jit(solution)/shard_map/ppermute | solution.py:21
  127.8 1.9 collective-permute-start.14
  129.7 1.3 collective-permute-start.15
  132.1 31.3 %all-reduce.4 = (f32[64]{0:T(128)}, f32[64]{0:T(128)}) all-reduce(f32[64]{0:T(128)S(1)} %get-tuple-element.139, f32[64]{0:T(128)S(1)} %get-tuple-element.10), channel_id=1, replica_groups=mesh['groups'=2,'space'=4,'dp'=2,'ysp'=2] {'space','dp','ysp'}, use_global_device_ids=true, to_apply=%region_2.3 | all-reduce | flops 128 | bytes 1024 | tf_op jit(solution)/shard_map/psum | solution.py:107
  165.2 1.7 pad_slice_fusion.1
  167.0 1.3 fusion.1
  168.3 9.0 %concatenate.47 = bf16[1,2,8,64,1728]{4,3,1,2,0:T(8,128)(2,1)} concatenate(bf16[1,2,8,64,64]{4,3,1,2,0:T(8,128)(2,1)} %get-tuple-element.38, bf16[1,2,8,64,64]{4,3,1,2,0:T(8,128)(2,1)} %get-tuple-element.37, bf16[1,2,8,64,64]{4,3,1,2,0:T(8,128)(2,1)S(1)} %get-tuple-element.13, bf16[1,2,8,64,64]{4,3,1,2,0:T(8,128)(2,1)S(1)} %get-tuple-element.14, ...), dimensions={4} | concatenate | bytes 7077888 | tf_op jit(solution)/shard_map/concatenate | solution.py:47
  177.3 2.4 %copy.39 = bf16[1,2,8,64,1728]{4,3,2,1,0:T(8,128)(2,1)S(1)} copy(bf16[1,2,8,64,1728]{4,3,1,2,0:T(8,128)(2,1)} %concatenate.47) | data formatting | bytes 7077888 | tf_op jit(solution)/shard_map/concatenate | solution.py:47
  181.9 41.4 %all-reduce.8.cloned.1.call-done = (f32[864,64]{0,1:T(8,128)}, f32[1728,64]{0,1:T(8,128)}) async-done(((f32[864,64]{0,1:T(8,128)}, f32[1728,64]{0,1:T(8,128)}), (f32[864,64]{0,1:T(8,128)}, f32[1728,64]{0,1:T(8,128)})) %all-reduce.8.cloned.1.call-update) | async-done | bytes 663568 | tf_op jit(solution)/shard_map/psum | solution.py:107
  223.4 1.6 copy.52
  225.0 1.8 copy.53
  (99 shorter events, 21.8 us)
Async XLA Ops:
  7.2 216.2 %all-reduce.8.cloned.1.call-start = ((), (), s32[]{:S(2)}) async-start(), calls=%async_computation | async-start | bytes 1376256 | tf_op jit(solution)/shard_map/psum | solution.py:107
  8.0 6.5 %collective-permute-start = (bf16[1,1,8,2048]{3,2,1,0:T(8,128)(2,1)S(1)}, bf16[1,1,8,2048]{3,2,1,0:T(8,128)(2,1)S(1)}, u32[]{:S(2)}, u32[]{:S(2)}) collective-permute-start(bf16[1,1,8,2048]{3,2,1,0:T(8,128)(2,1)S(1)} %get-tuple-element.136), channel_id=1, source_target_pairs={{0,4},{4,8},{8,12},{1,5},{5,9},{9,13},{2,6},{6,10},{10,14},{3,7},{... | collective-permute-start | bytes 98312 | tf_op jit(solution)/shard_map/ppermute | solution.py:19
  12.9 5.8 %collective-permute-start.1 = (bf16[1,1,8,2048]{3,2,1,0:T(8,128)(2,1)S(1)}, bf16[1,1,8,2048]{3,2,1,0:T(8,128)(2,1)S(1)}, u32[]{:S(2)}, u32[]{:S(2)}) collective-permute-start(bf16[1,1,8,2048]{3,2,1,0:T(8,128)(2,1)S(1)} %get-tuple-element.135), channel_id=1, source_target_pairs={{4,0},{8,4},{12,8},{5,1},{9,5},{13,9},{6,2},{10,6},{14,10},{7,3},{... | collective-permute-start | bytes 98312 | tf_op jit(solution)/shard_map/ppermute | solution.py:21
  18.8 4.4 %collective-permute-start.2 = (bf16[1,4,1,2048]{3,2,1,0:T(2,128)(2,1)S(1)}, bf16[1,4,1,2048]{3,2,1,0:T(2,128)(2,1)S(1)}, u32[]{:S(2)}, u32[]{:S(2)}) collective-permute-start(bf16[1,4,1,2048]{3,2,1,0:T(2,128)(2,1)S(1)} %get-tuple-element.133), channel_id=1, source_target_pairs={{0,1},{2,3},{4,5},{6,7},{8,9},{10,11},{12,13},{14,15},{16,17},{18,... | collective-permute-start | bytes 49160 | tf_op jit(solution)/shard_map/ppermute | solution.py:19
  20.1 3.1 %collective-permute-start.3 = (bf16[1,4,1,2048]{3,2,1,0:T(2,128)(2,1)S(1)}, bf16[1,4,1,2048]{3,2,1,0:T(2,128)(2,1)S(1)}, u32[]{:S(2)}, u32[]{:S(2)}) collective-permute-start(bf16[1,4,1,2048]{3,2,1,0:T(2,128)(2,1)S(1)} %get-tuple-element.134), channel_id=1, source_target_pairs={{1,0},{3,2},{5,4},{7,6},{9,8},{11,10},{13,12},{15,14},{17,16},{19,... | collective-permute-start | bytes 49160 | tf_op jit(solution)/shard_map/ppermute | solution.py:21
  35.9 1.8 copy-start.2
  35.9 1.8 copy-start.12
  35.9 17.2 %copy-start.6 = (f32[1728,64]{0,1:T(8,128)S(1)}, f32[1728,64]{0,1:T(8,128)}, u32[]{:S(2)}) copy-start(f32[1728,64]{0,1:T(8,128)} %param.9) | copy-start | bytes 1327108
  35.9 17.9 %copy-start.10 = (bf16[1,2,8,4096]{3,2,1,0:T(8,128)(2,1)S(1)}, bf16[1,2,8,4096]{3,2,1,0:T(8,128)(2,1)}, u32[]{:S(2)}) copy-start(bf16[1,2,8,4096]{3,2,1,0:T(8,128)(2,1)} %param.11) | copy-start | bytes 393220
  39.6 5.8 %collective-permute-start.4 = (bf16[1,1,8,4096]{3,2,1,0:T(8,128)(2,1)S(1)}, bf16[1,1,8,4096]{3,2,1,0:T(8,128)(2,1)S(1)}, u32[]{:S(2)}, u32[]{:S(2)}) collective-permute-start(bf16[1,1,8,4096]{3,2,1,0:T(8,128)(2,1)S(1)} %get-tuple-element.132), channel_id=1, source_target_pairs={{0,4},{4,8},{8,12},{1,5},{5,9},{9,13},{2,6},{6,10},{10,14},{3,7},{... | collective-permute-start | bytes 196616 | tf_op jit(solution)/shard_map/ppermute | solution.py:19
  43.1 6.7 %collective-permute-start.5 = (bf16[1,1,8,4096]{3,2,1,0:T(8,128)(2,1)S(1)}, bf16[1,1,8,4096]{3,2,1,0:T(8,128)(2,1)S(1)}, u32[]{:S(2)}, u32[]{:S(2)}) collective-permute-start(bf16[1,1,8,4096]{3,2,1,0:T(8,128)(2,1)S(1)} %get-tuple-element.131), channel_id=1, source_target_pairs={{4,0},{8,4},{12,8},{5,1},{9,5},{13,9},{6,2},{10,6},{14,10},{7,3},{... | collective-permute-start | bytes 196616 | tf_op jit(solution)/shard_map/ppermute | solution.py:21
  49.9 5.0 %collective-permute-start.6 = (bf16[1,4,1,4096]{3,2,1,0:T(2,128)(2,1)S(1)}, bf16[1,4,1,4096]{3,2,1,0:T(2,128)(2,1)S(1)}, u32[]{:S(2)}, u32[]{:S(2)}) collective-permute-start(bf16[1,4,1,4096]{3,2,1,0:T(2,128)(2,1)S(1)} %get-tuple-element.125), channel_id=1, source_target_pairs={{0,1},{2,3},{4,5},{6,7},{8,9},{10,11},{12,13},{14,15},{16,17},{18,... | collective-permute-start | bytes 98312 | tf_op jit(solution)/shard_map/ppermute | solution.py:19
  51.8 3.1 %collective-permute-start.7 = (bf16[1,4,1,4096]{3,2,1,0:T(2,128)(2,1)S(1)}, bf16[1,4,1,4096]{3,2,1,0:T(2,128)(2,1)S(1)}, u32[]{:S(2)}, u32[]{:S(2)}) collective-permute-start(bf16[1,4,1,4096]{3,2,1,0:T(2,128)(2,1)S(1)} %get-tuple-element.126), channel_id=1, source_target_pairs={{1,0},{3,2},{5,4},{7,6},{9,8},{11,10},{13,12},{15,14},{17,16},{19,... | collective-permute-start | bytes 98312 | tf_op jit(solution)/shard_map/ppermute | solution.py:21
  69.7 2.5 %copy-start.1 = (bf16[1728,64]{0,1:T(8,128)(2,1)S(1)}, bf16[1728,64]{0,1:T(8,128)(2,1)}, u32[]{:S(2)}) copy-start(bf16[1728,64]{0,1:T(8,128)(2,1)} %convert_element_type.41) | copy-start | bytes 663556
  69.7 2.5 %copy-start.8 = (f32[1024,64]{0,1:T(8,128)S(1)}, f32[1024,64]{0,1:T(8,128)}, u32[]{:S(2)}) copy-start(f32[1024,64]{0,1:T(8,128)} %copy.32) | copy-start | bytes 786436
  69.7 2.5 %copy-start.13 = (f32[64]{0:T(128)S(1)}, f32[64]{0:T(128)}, u32[]{:S(2)}) copy-start(f32[64]{0:T(128)} %param.10) | copy-start | bytes 772
  72.1 2.1 copy-start
  72.2 17.5 %copy-start.3 = (bf16[864,64]{1,0:T(8,128)(2,1)S(1)}, bf16[864,64]{1,0:T(8,128)(2,1)}, u32[]{:S(2)}) copy-start(bf16[864,64]{1,0:T(8,128)(2,1)} %copy.27) | copy-start | bytes 331780
  74.2 0.7 copy-start.4
  75.4 5.8 %collective-permute-start.8 = (bf16[1,1,8,4096]{3,2,1,0:T(8,128)(2,1)S(1)}, bf16[1,1,8,4096]{3,2,1,0:T(8,128)(2,1)S(1)}, u32[]{:S(2)}, u32[]{:S(2)}) collective-permute-start(bf16[1,1,8,4096]{3,2,1,0:T(8,128)(2,1)S(1)} %get-tuple-element.130), channel_id=1, source_target_pairs={{0,4},{4,8},{8,12},{1,5},{5,9},{9,13},{2,6},{6,10},{10,14},{3,7},{... | collective-permute-start | bytes 196616 | tf_op jit(solution)/shard_map/ppermute | solution.py:19
  78.8 6.7 %collective-permute-start.9 = (bf16[1,1,8,4096]{3,2,1,0:T(8,128)(2,1)S(1)}, bf16[1,1,8,4096]{3,2,1,0:T(8,128)(2,1)S(1)}, u32[]{:S(2)}, u32[]{:S(2)}) collective-permute-start(bf16[1,1,8,4096]{3,2,1,0:T(8,128)(2,1)S(1)} %get-tuple-element.129), channel_id=1, source_target_pairs={{4,0},{8,4},{12,8},{5,1},{9,5},{13,9},{6,2},{10,6},{14,10},{7,3},{... | collective-permute-start | bytes 196616 | tf_op jit(solution)/shard_map/ppermute | solution.py:21
  86.3 8.7 %collective-permute-start.10 = (bf16[1,4,1,4096]{3,2,1,0:T(2,128)(2,1)}, bf16[1,4,1,4096]{3,2,1,0:T(2,128)(2,1)S(1)}, u32[]{:S(2)}, u32[]{:S(2)}) collective-permute-start(bf16[1,4,1,4096]{3,2,1,0:T(2,128)(2,1)} %get-tuple-element.122), channel_id=1, source_target_pairs={{0,1},{2,3},{4,5},{6,7},{8,9},{10,11},{12,13},{14,15},{16,17},{18,... | collective-permute-start | bytes 98312 | tf_op jit(solution)/shard_map/ppermute | solution.py:19
  88.2 6.8 %collective-permute-start.11 = (bf16[1,4,1,4096]{3,2,1,0:T(2,128)(2,1)S(1)}, bf16[1,4,1,4096]{3,2,1,0:T(2,128)(2,1)S(1)}, u32[]{:S(2)}, u32[]{:S(2)}) collective-permute-start(bf16[1,4,1,4096]{3,2,1,0:T(2,128)(2,1)S(1)} %get-tuple-element.123), channel_id=1, source_target_pairs={{1,0},{3,2},{5,4},{7,6},{9,8},{11,10},{13,12},{15,14},{17,16},{19,... | collective-permute-start | bytes 98312 | tf_op jit(solution)/shard_map/ppermute | solution.py:21
  109.7 2.5 %copy-start.9 = (bf16[1728,64]{0,1:T(8,128)(2,1)S(1)}, bf16[1728,64]{0,1:T(8,128)(2,1)}, u32[]{:S(2)}) copy-start(bf16[1728,64]{0,1:T(8,128)(2,1)} %reshape.78) | copy-start | bytes 663556
  109.7 2.5 %copy-start.14 = (f32[1024,64]{0,1:T(8,128)S(1)}, f32[1024,64]{0,1:T(8,128)}, u32[]{:S(2)}) copy-start(f32[1024,64]{0,1:T(8,128)} %get-tuple-element.138) | copy-start | bytes 786436
  112.1 4.2 %copy-start.5 = (bf16[1024,64]{0,1:T(8,128)(2,1)S(1)}, bf16[1024,64]{0,1:T(8,128)(2,1)}, u32[]{:S(2)}) copy-start(bf16[1024,64]{0,1:T(8,128)(2,1)} %copy-done.4) | copy-start | bytes 393220
  113.5 6.4 %copy-start.11 = (bf16[1024,64]{0,1:T(8,128)(2,1)S(1)}, bf16[1024,64]{0,1:T(8,128)(2,1)}, u32[]{:S(2)}) copy-start(bf16[1024,64]{0,1:T(8,128)(2,1)} %get-tuple-element.124) | copy-start | bytes 393220
  114.0 8.3 %collective-permute-start.12 = (bf16[1,1,8,4096]{3,2,1,0:T(8,128)(2,1)S(1)}, bf16[1,1,8,4096]{3,2,1,0:T(8,128)(2,1)S(1)}, u32[]{:S(2)}, u32[]{:S(2)}) collective-permute-start(bf16[1,1,8,4096]{3,2,1,0:T(8,128)(2,1)S(1)} %get-tuple-element.128), channel_id=1, source_target_pairs={{0,4},{4,8},{8,12},{1,5},{5,9},{9,13},{2,6},{6,10},{10,14},{3,7},{... | collective-permute-start | bytes 196616 | tf_op jit(solution)/shard_map/ppermute | solution.py:19
  121.0 6.7 %collective-permute-start.13 = (bf16[1,1,8,4096]{3,2,1,0:T(8,128)(2,1)S(1)}, bf16[1,1,8,4096]{3,2,1,0:T(8,128)(2,1)S(1)}, u32[]{:S(2)}, u32[]{:S(2)}) collective-permute-start(bf16[1,1,8,4096]{3,2,1,0:T(8,128)(2,1)S(1)} %get-tuple-element.127), channel_id=1, source_target_pairs={{4,0},{8,4},{12,8},{5,1},{9,5},{13,9},{6,2},{10,6},{14,10},{7,3},{... | collective-permute-start | bytes 196616 | tf_op jit(solution)/shard_map/ppermute | solution.py:21
  127.8 35.6 %collective-permute-start.14 = (bf16[1,4,1,4096]{3,2,1,0:T(2,128)(2,1)S(1)}, bf16[1,4,1,4096]{3,2,1,0:T(2,128)(2,1)S(1)}, u32[]{:S(2)}, u32[]{:S(2)}) collective-permute-start(bf16[1,4,1,4096]{3,2,1,0:T(2,128)(2,1)S(1)} %get-tuple-element.120), channel_id=1, source_target_pairs={{0,1},{2,3},{4,5},{6,7},{8,9},{10,11},{12,13},{14,15},{16,17},{18,... | collective-permute-start | bytes 98312 | tf_op jit(solution)/shard_map/ppermute | solution.py:19
  129.7 33.7 %collective-permute-start.15 = (bf16[1,4,1,4096]{3,2,1,0:T(2,128)(2,1)S(1)}, bf16[1,4,1,4096]{3,2,1,0:T(2,128)(2,1)S(1)}, u32[]{:S(2)}, u32[]{:S(2)}) collective-permute-start(bf16[1,4,1,4096]{3,2,1,0:T(2,128)(2,1)S(1)} %get-tuple-element.121), channel_id=1, source_target_pairs={{1,0},{3,2},{5,4},{7,6},{9,8},{11,10},{13,12},{15,14},{17,16},{19,... | collective-permute-start | bytes 98312 | tf_op jit(solution)/shard_map/ppermute | solution.py:21
  177.2 2.4 %copy-start.7 = (bf16[1728,32]{0,1:T(8,128)(2,1)S(1)}, bf16[1728,32]{0,1:T(8,128)(2,1)}, u32[]{:S(2)}) copy-start(bf16[1728,32]{0,1:T(8,128)(2,1)} %reshape.83) | copy-start | bytes 331780
Sparse Core Ops, SparseCore 0:
  132.2 91.0 all-reduce.7
where the time goes:
time: 237 us; the launch traced here: 234 us
  local copies, waits for them, and re-layouts  82.5 us (35%)
  waiting for transfers between devices  61.4 us (26%)
  starting transfers between devices  31.7 us (13%)
  blocking collectives  31.3 us (13%)
  between operations  14.7 us (6%)
  matrix products  10.6 us (4%)
    concatenate x8, local copies, waits for them, and re-layouts, columns(): return jnp.concatenate(pieces, axis=-1).reshape(-1, 27 * chans)  44 us
    psum x1, waiting for transfers between devices, on_device(): lax.psum((grad_w1, grad_b1, grad_w2, grad_b2), ('space', 'dp', 'ysp'))  41.4 us
    psum x1, blocking collectives, on_device(): lax.psum((grad_w1, grad_b1, grad_w2, grad_b2), ('space', 'dp', 'ysp'))  31.3 us
    ppermute x8, starting transfers between devices, padded_2(): lax.ppermute(tail, axis, [(i, (i + 1) % count) for i in range(ends)])  21.1 us
    ppermute x8, waiting for transfers between devices, padded_2(): lax.ppermute(head, axis, [((i + 1) % count, i) for i in range(ends)])  17.6 us
    slice x12, local copies, waits for them, and re-layouts, columns(): cells[:, first:first + wide_x, second:second + wide_y, third:third + DEPT...  17.1 us
    ppermute x8, starting transfers between devices, padded_2(): lax.ppermute(head, axis, [((i + 1) % count, i) for i in range(ends)])  10.5 us
    unnamed x41, local copies, waits for them, and re-layouts  6.87 us
  transfers between devices with their start and end apart: 17, of which 8 were waited for; matrix products, arithmetic and copies ran while one was open for 15% of the time, Pallas kernels for 0%

commit v1 on v0

v1 whole, which is shorter than its diff:
```python
import jax
import jax.numpy as jnp
from jax import lax
from jax.experimental import pallas as pl
from jax.experimental.pallas import tpu as pltpu
from jax.sharding import PartitionSpec as P

C_IN = 32
C_MID = 64
DEPTH = 64
BF = jnp.bfloat16
F32 = jnp.float32
GROUP = 4
ROWS = DEPTH // GROUP
IN_L = GROUP * C_IN
MID_L = GROUP * C_MID
TAP1 = 3 * C_IN
TAP2 = 3 * C_MID
W1_L = 9 * TAP1
W2_L = 9 * TAP2
PACK2 = 1792
PACK1 = 896
NT = (((1,), (1,)), ((), ()))
NN = (((1,), (0,)), ((), ()))


def call(body, outs, scratch=(), vmem=40 << 20, cost=None):
    return pl.pallas_call(
        body,
        out_shape=[jax.ShapeDtypeStruct(shape, kind) for shape, kind in outs],
        scratch_shapes=list(scratch),
        compiler_params=pltpu.CompilerParams(vmem_limit_bytes=vmem),
        cost_estimate=cost,
    )


def dot(a, b, dims):
    return lax.dot_general(a, b, dims, preferred_element_type=F32)


def window(ref, start, width):
    frame = 256 if width <= 128 else 384
    at = start // 128 * 128
    value = ref[:, at : at + frame]
    if start != at:
        value = pltpu.roll(value, frame - (start - at), 1)
    lane = lax.broadcasted_iota(jnp.int32, value.shape, 1)
    return jnp.where(lane < width, value, 0.0)


def banded_body(w1_ref, w2_ref, f1_ref, f2_ref, r2_ref, r1_ref, pad1, pad2):
    pad1[...] = jnp.zeros(pad1.shape, F32)
    pad2[...] = jnp.zeros(pad2.shape, F32)
    pad1[:, :W1_L] = w1_ref[...]
    pad2[:, :W2_L] = w2_ref[...]
    for tap in range(9):
        one = window(pad1, tap * TAP1, TAP1)
        two = window(pad2, tap * TAP2, TAP2)
        for m in range(-1, 5):
            at = (m % 6) * C_MID
            s1 = pltpu.roll(one, ((m - 1) * C_IN) % 256, 1) if m != 1 else one
            s2 = pltpu.roll(two, ((m - 1) * C_MID) % 384, 1) if m != 1 else two
            s1 = s1.astype(BF)
            s2 = s2.astype(BF)
            if 0 <= m < 4:
                f1_ref[tap, m * C_MID : (m + 1) * C_MID, :] = s1
                f2_ref[tap, m * C_MID : (m + 1) * C_MID, :] = s2
            r1_ref[tap, at : at + C_MID, :] = s1[:, :IN_L]
            r2_ref[tap, at : at + C_MID, :] = s2[:, :MID_L]


def edges(value, low, high):
    count = value.shape[0]
    row = lax.broadcasted_iota(jnp.int32, (count, 128), 0) % ROWS
    lane = lax.broadcasted_iota(jnp.int32, (count, 128), 1)
    after = pltpu.roll(value[:, low : low + 128], count - 1, 0)
    before = pltpu.roll(value[:, high : high + 128], 1, 0)
    after = jnp.where(row == ROWS - 1, 0.0, after)
    before = jnp.where(row == 0, 0.0, before)
    return jnp.where(lane < 64, after, before)


def spread(planes, beside, core, to_ref, lanes):
    for x, plane in enumerate(planes):
        side = beside[x].astype(F32)
        low = jnp.where(core == 1, side, 0.0)
        high = jnp.where(core == 0, side, 0.0)
        cells = jnp.concatenate([low, plane.astype(F32), high], axis=0)
        rows = cells.reshape(-1, lanes)
        shape = cells.shape[:2]
        to_ref[x, :, :, :lanes] = cells.astype(BF)
        edge = edges(rows, 0, lanes - 128)
        to_ref[x, :, :, lanes:] = edge.astype(BF).reshape(*shape, 128)


def plane_mask(x, rows, space, last, core):
    row = lax.broadcasted_iota(jnp.int32, (rows, 1), 0)
    inside = jnp.float32(1.0)
    if x == 0:
        inside = jnp.where(space > 0, 1.0, 0.0)
    if x == 3:
        inside = jnp.where(space < last, 1.0, 0.0)
    low = jnp.where(core == 1, 1.0, 0.0)
    high = jnp.where(core == 0, 1.0, 0.0)
    mask = jnp.where(row < ROWS, low, jnp.where(row >= rows - ROWS, high, 1.0))
    return mask * inside


def forward_body(x_ref, l_ref, r_ref, y_ref, f1_ref, f2_ref, b1_ref, b2_ref, c_ref, e_ref, a_ref, d_ref, o_ref, g_ref, acc):
    core = lax.axis_index("ysp")
    space = lax.axis_index("space")
    last = lax.axis_size("space") - 1
    planes = [ref[i] for ref in (l_ref, x_ref, r_ref) for i in range(2)]
    spread(planes, y_ref, core, e_ref, IN_L)
    wide = x_ref.shape[1] + 2
    total = None
    for tap in range(9):
        a, b = divmod(tap, 3)
        part = dot(e_ref[a : a + 4, b : b + wide].reshape(-1, 256), f1_ref[tap], NT)
        total = part if total is None else total + part
    acc[...] = total
    rows = wide * ROWS
    for x in range(4):
        y1 = acc[x * rows : (x + 1) * rows, :] + b1_ref[...]
        mask = plane_mask(x, rows, space, last, core)
        sig = jax.nn.sigmoid(y1)
        d_ref[x] = (sig * (1.0 + y1 * (1.0 - sig)) * mask).reshape(wide, ROWS, MID_L)
        act = (y1 * sig * mask).astype(BF)
        a_ref[x, :, :, :MID_L] = act.reshape(wide, ROWS, MID_L)
        edge = edges(act.astype(F32), 0, 128)
        a_ref[x, :, :, MID_L:] = edge.astype(BF).reshape(wide, ROWS, 128)
    narrow = wide - 2
    total = None
    for tap in range(9):
        a, b = divmod(tap, 3)
        part = dot(a_ref[a : a + 2, b : b + narrow].reshape(-1, 384), f2_ref[tap], NT)
        total = part if total is None else total + part
    y2 = total + b2_ref[...]
    sig = jax.nn.sigmoid(y2)
    shape = o_ref.shape
    o_ref[...] = (y2 * sig).astype(BF).reshape(shape)
    cot = c_ref[...].reshape(-1, MID_L).astype(F32)
    g_ref[...] = (cot * (sig * (1.0 + y2 * (1.0 - sig)))).astype(BF).reshape(shape)


def flipped(grads):
    turned = grads.astype(F32).T
    sums = jnp.sum(turned, axis=1, keepdims=True)
    bias = sums[0:64] + sums[64:128] + sums[128:192] + sums[192:256]
    return turned.astype(BF), bias


def tap_sum(product, step):
    frame = product.shape[1]
    total = product[64:128]
    for j in (0, 2, 3):
        total = total + pltpu.roll(product[j * 64 : (j + 1) * 64], (frame - (j - 1) * step) % frame, 1)
    return total


def second_weights_body(a_ref, g_ref, p_ref):
    turned, bias = flipped(g_ref[...].reshape(-1, MID_L))
    narrow = g_ref.shape[1]
    lane = lax.broadcasted_iota(jnp.int32, (64, 384), 1)
    held = None
    for tap in range(9):
        a, b = divmod(tap, 3)
        found = tap_sum(dot(turned, a_ref[a : a + 2, b : b + narrow].reshape(-1, 384), NN), C_MID)
        if tap == 8:
            p_ref[:, 1536:1792] = jnp.where(lane < TAP2, found, bias)[:, :256]
        elif tap % 2 == 0:
            held = found
        else:
            at = (tap - 1) * TAP2
            p_ref[:, at : at + 384] = jnp.where(lane < TAP2, held, pltpu.roll(found, TAP2, 1))


def backward_body(g_ref, l_ref, r_ref, y_ref, r2_ref, d_ref, e_ref, p2_ref, k_ref, s_ref, t_ref, wide_g, acc, pack):
    core = lax.axis_index("ysp")
    planes = [ref[i] for ref in (l_ref, g_ref, r_ref) for i in range(2)]
    spread(planes, y_ref, core, wide_g, MID_L)
    narrow = g_ref.shape[1]
    wide = narrow + 2
    total = None
    for tap in range(9):
        a, b = divmod(tap, 3)
        part = dot(wide_g[2 - a : 6 - a, 2 - b : 2 - b + wide].reshape(-1, 384), r2_ref[tap], NN)
        total = part if total is None else total + part
    acc[...] = total
    rows = wide * ROWS
    for x in range(4):
        slope = d_ref[x].reshape(rows, MID_L)
        g1 = (acc[x * rows : (x + 1) * rows, :] * slope).astype(BF)
        t_ref[x, :, :, :MID_L] = g1.reshape(wide, ROWS, MID_L)
        edge = edges(g1.astype(F32), 0, 128)
        t_ref[x, :, :, MID_L:] = edge.astype(BF).reshape(wide, ROWS, 128)
    turned, bias = flipped(t_ref[1:3, 1 : 1 + narrow, :, :MID_L].reshape(-1, MID_L))
    lane = lax.broadcasted_iota(jnp.int32, (64, 384), 1)
    none = jnp.zeros((64, 128), F32)
    held = None
    pack[:, :PACK2] = p2_ref[...]
    for tap in range(9):
        a, b = divmod(tap, 3)
        cells = e_ref[1 + a : 3 + a, 1 + b : 1 + b + narrow].reshape(-1, 256)
        found = tap_sum(dot(turned, cells, NN), C_IN)
        if tap == 8:
            pack[:, PACK2 + 768 : PACK2 + 896] = jnp.where(lane < TAP1, jnp.concatenate([found, none], axis=1), bias)[:, :128]
            continue
        found = jnp.concatenate([found, none], axis=1)
        slot = tap % 4
        if slot == 0:
            held = found
        else:
            held = jnp.where(lane < slot * TAP1, held, pltpu.roll(found, slot * TAP1, 1))
        if slot == 3:
            at = PACK2 + (tap - 3) * TAP1
            pack[:, at : at + 384] = held
    k_ref[...] = pack[pl.ds(core * 32, 32), :]
    s_ref[...] = pack[pl.ds((1 - core) * 32, 32), :].astype(BF)


def input_grad_body(t_ref, r1_ref, o_ref):
    narrow = o_ref.shape[1]
    total = None
    for tap in range(9):
        a, b = divmod(tap, 3)
        part = dot(t_ref[2 - a : 4 - a, 2 - b : 2 - b + narrow].reshape(-1, 384), r1_ref[tap], NN)
        total = part if total is None else total + part
    o_ref[...] = total.astype(BF).reshape(o_ref.shape)


def finish_body(m_ref, h_ref, w1_ref, b1_ref, w2_ref, b2_ref, pack):
    core = lax.axis_index("ysp")
    pack[pl.ds(core * 32, 32), :] = m_ref[...].astype(F32)
    pack[pl.ds((1 - core) * 32, 32), :] = h_ref[...].astype(F32)
    w2_ref[...] = pack[:, :W2_L]
    w1_ref[...] = pack[:, PACK2 : PACK2 + W1_L]
    row = lax.broadcasted_iota(jnp.int32, (64, 64), 0)
    col = lax.broadcasted_iota(jnp.int32, (64, 64), 1)
    for ref, at in ((b2_ref, W2_L), (b1_ref, PACK2 + W1_L)):
        spot = jnp.broadcast_to(pack[:, at : at + 1], (64, 64))
        ref[...] = jnp.sum(jnp.where(row == col, spot, 0.0), axis=0, keepdims=True)


def beside(cells, axis):
    last = lax.axis_size(axis) - 1
    return (
        lax.ppermute(cells, axis, [(i, i + 1) for i in range(last)]),
        lax.ppermute(cells, axis, [(i + 1, i) for i in range(last)]),
    )


def swap(cells, axis, bit):
    return lax.ppermute(cells, axis, [(i, i ^ bit) for i in range(lax.axis_size(axis))])


def other_core(left, own, right):
    wide = own.shape[1]
    start = (1 - lax.axis_index("ysp")) * (wide - 2)
    cols = [lax.dynamic_slice_in_dim(part, start, 2, axis=1) for part in (left, own, right)]
    return swap(jnp.concatenate(cols, axis=0), "ysp", 1)


def on_device(inputs, w_first, b_first, w_second, b_second, cotangent):
    nx, ny = inputs.shape[1], inputs.shape[2]
    cells = inputs.reshape(nx, ny, ROWS, IN_L)
    left, right = beside(cells, "space")
    f1, f2, r2, r1 = call(
        banded_body,
        [((9, 256, 256), BF), ((9, 256, 384), BF), ((9, 384, 256), BF), ((9, 384, 128), BF)],
        [pltpu.VMEM((64, 1152), F32), pltpu.VMEM((64, 2048), F32)],
    )(w_first.T, w_second.T)
    bias1 = jnp.tile(b_first, GROUP).reshape(1, MID_L)
    bias2 = jnp.tile(b_second, GROUP).reshape(1, MID_L)
    cot = cotangent.reshape(nx, ny, ROWS, MID_L)
    across = other_core(left, cells, right)
    wide_in, act, slope, out, g2 = call(
        forward_body,
        [
            ((nx + 4, ny + 4, ROWS, 256), BF),
            ((nx + 2, ny + 2, ROWS, 384), BF),
            ((nx + 2, ny + 2, ROWS, MID_L), F32),
            ((nx, ny, ROWS, MID_L), BF),
            ((nx, ny, ROWS, MID_L), BF),
        ],
        [pltpu.VMEM(((nx + 2) * (ny + 2) * ROWS, MID_L), F32)],
    )(cells, left, right, across, f1, f2, bias1, bias2, cot)
    g_left, g_right = beside(g2, "space")
    (pack2,) = call(second_weights_body, [((64, PACK2), F32)])(act, g2)
    g_across = other_core(g_left, g2, g_right)
    keep, send, turned = call(
        backward_body,
        [((32, PACK2 + PACK1), F32), ((32, PACK2 + PACK1), BF), ((nx + 2, ny + 2, ROWS, 384), BF)],
        [
            pltpu.VMEM((nx + 4, ny + 4, ROWS, 384), BF),
            pltpu.VMEM(((nx + 2) * (ny + 2) * ROWS, MID_L), F32),
            pltpu.VMEM((64, PACK2 + PACK1), F32),
        ],
    )(g2, g_left, g_right, g_across, r2, slope, wide_in, pack2)
    got = swap(send, "ysp", 1)
    total = lax.optimization_barrier((keep + got.astype(F32)).astype(BF))
    (d_in,) = call(input_grad_body, [((nx, ny, ROWS, IN_L), BF)])(turned, r1)
    for axis in ("dp", "space"):
        bit = 1
        while bit < lax.axis_size(axis):
            total = lax.optimization_barrier(total + swap(total, axis, bit))
            bit *= 2
    other = swap(total, "ysp", 1)
    gw1, gb1, gw2, gb2 = call(
        finish_body,
        [((64, W1_L), F32), ((1, 64), F32), ((64, W2_L), F32), ((1, 64), F32)],
        [pltpu.VMEM((64, PACK2 + PACK1), F32)],
    )(total, other)
    output = out.reshape(1, nx, ny, DEPTH * C_MID)
    input_grad = d_in.reshape(1, nx, ny, DEPTH * C_IN)
    return (output, input_grad, gw1.T, gb1.reshape(64), gw2.T, gb2.reshape(64))


def solution(mesh):
    placed = P(("groups", "dp"), "space", "ysp", None)
    return jax.shard_map(
        on_device,
        mesh=mesh,
        in_specs=(placed, P(), P(), P(), P(), placed),
        out_specs=(placed, placed, P("groups", None), P("groups"), P("groups", None), P("groups")),
        check_vma=False,
    )
```

time: 237 us -> 60.9 us (0.26); the launches traced: 234 us -> 60.5 us
  local copies, waits for them, and re-layouts: 82.5 us -> 6.62 us
  waiting for transfers between devices: 61.4 us -> 22.6 us
  blocking collectives: 31.3 us -> 0 us
  between operations: 14.7 us -> 0.79 us
  starting transfers between devices: 31.7 us -> 20.9 us
  matrix products: 10.6 us -> 0 us
  Pallas kernels: 0 us -> 9.4 us
    concatenate x16 -> x0, local copies, waits for them, and re-layouts: 44.9 us -> none  [the longest x8 44 us: columns(): return jnp.concatenate(pieces, axis=-1).reshape(-1, 27 * chans)]
    psum x1 -> x0, waiting for transfers between devices: 41.4 us -> none  [on_device(): lax.psum((grad_w1, grad_b1, grad_w2, grad_b2), ('space', 'dp', 'ysp'))]
    psum x1 -> x0, blocking collectives: 31.3 us -> none  [on_device(): lax.psum((grad_w1, grad_b1, grad_w2, grad_b2), ('space', 'dp', 'ysp'))]
    slice x20 -> x0, local copies, waits for them, and re-layouts: 18.9 us -> none  [the longest x12 17.1 us: columns(): cells[:, first:first + wide_x, second:second + wide_y, third:third + DEPT...]
    ppermute x16 -> x11, starting transfers between devices: 31.6 us -> 20.9 us  [the longest x2 10.5 us: beside(): lax.ppermute(cells, axis, [(i, i + 1) for i in range(last)])]
    dot_general x6 -> x0, matrix products: 10.6 us -> none  [the longest x2 4.68 us: weight_term(): lax.dot_general(patches, grads, (((0,), (0,)), ((), ())), preferred_eleme...]
    pallas_call x0 -> x6, Pallas kernels: none -> 9.4 us  [the longest x1 3.1 us: on_device(): call(forward_body, [((nx + 4, ny + 4, ROWS, 256), BF), ((nx + 2, ny + 2,...]
    reshape x12 -> x2, local copies, waits for them, and re-layouts: 6.86 us -> 1.38 us  [the longest x1 0.72 us: on_device(): output = out.reshape(1, nx, ny, DEPTH * C_MID)]
  transfers between devices with their start and end apart: 17 -> 11, of which waited for: 8 -> 9; matrix products, arithmetic and copies ran while one was open for 15% -> 6% of each run, Pallas kernels for 0% -> 4%
where the time goes in v1:
time: 60.9 us; the launch traced here: 60.5 us
  waiting for transfers between devices  22.6 us (37%)
  starting transfers between devices  20.9 us (34%)
  Pallas kernels  9.4 us (15%)
  local copies, waits for them, and re-layouts  6.62 us (11%)
  between operations  0.79 us (1%)
    ppermute x7, waiting for transfers between devices, swap(): lax.ppermute(cells, axis, [(i, i ^ bit) for i in range(lax.axis_size(axis...  17.4 us
    ppermute x2, starting transfers between devices, beside(): lax.ppermute(cells, axis, [(i, i + 1) for i in range(last)])  10.5 us
    ppermute x7, starting transfers between devices, swap(): lax.ppermute(cells, axis, [(i, i ^ bit) for i in range(lax.axis_size(axis...  7.85 us
    unnamed x6, local copies, waits for them, and re-layouts  3.73 us
    pallas_call x1, Pallas kernels, on_device(): call(forward_body, [((nx + 4, ny + 4, ROWS, 256), BF), ((nx + 2, ny + 2,...  3.1 us
    pallas_call x1, Pallas kernels, on_device(): call(backward_body, [((32, PACK2 + PACK1), F32), ((32, PACK2 + PACK1), BF...  2.91 us
    ppermute x2, waiting for transfers between devices, beside(): lax.ppermute(cells, axis, [(i, i + 1) for i in range(last)])  2.76 us
    ppermute x2, starting transfers between devices, beside(): lax.ppermute(cells, axis, [(i + 1, i) for i in range(last)])  2.58 us
  transfers between devices with their start and end apart: 11, of which 9 were waited for; matrix products, arithmetic and copies ran while one was open for 6% of the time, Pallas kernels for 4%

profile of v1, /device:TPU:0, one launch (start us, length us, event | category | flops | bytes accessed | tf_op | source)
XLA Modules:
  0.0 60.5 jit_solution(12807258551900074665)
XLA Ops:
  0.6 0.9 %copy.17 = bf16[2,8,16,128]{3,2,1,0:T(8,128)(2,1)S(1)} copy(bf16[2,8,16,128]{3,1,2,0:T(8,128)(2,1)} %bitcast.27) | data formatting | bytes 131072
  1.5 1.3 %collective-permute-start.1 = (bf16[2,8,16,128]{3,2,1,0:T(8,128)(2,1)S(1)}, bf16[2,8,16,128]{3,2,1,0:T(8,128)(2,1)S(1)}, u32[]{:S(2)}, u32[]{:S(2)}) collective-permute-start(bf16[2,8,16,128]{3,2,1,0:T(8,128)(2,1)S(1)} %copy.17), channel_id=1, source_target_pairs={{4,0},{8,4},{12,8},{5,1},{9,5},{13,9},{6,2},{10,6},{14,10},{7,3},{... | collective-permute-start | bytes 196616 | tf_op jit(solution)/shard_map/ppermute | solution.py:249
  2.8 5.6 %collective-permute-start = (bf16[2,8,16,128]{3,2,1,0:T(8,128)(2,1)S(1)}, bf16[2,8,16,128]{3,2,1,0:T(8,128)(2,1)S(1)}, u32[]{:S(2)}, u32[]{:S(2)}) collective-permute-start(bf16[2,8,16,128]{3,2,1,0:T(8,128)(2,1)S(1)} %copy.17), channel_id=1, source_target_pairs={{0,4},{4,8},{8,12},{1,5},{5,9},{9,13},{2,6},{6,10},{10,14},{3,7},{... | collective-permute-start | bytes 196616 | tf_op jit(solution)/shard_map/ppermute | solution.py:248
  8.4 0.3 collective-permute-done.1.r_ref
  8.7 1.6 %collective-permute-done.l_ref = bf16[2,8,16,128]{3,2,1,0:T(8,128)(2,1)S(1)} collective-permute-done((bf16[2,8,16,128]{3,2,1,0:T(8,128)(2,1)S(1)}, bf16[2,8,16,128]{3,2,1,0:T(8,128)(2,1)S(1)}, u32[]{:S(2)}, u32[]{:S(2)}) %collective-permute-start) | collective-permute-done | bytes 65568 | tf_op jit(solution)/shard_map/ppermute | solution.py:248
  10.3 0.1 collective-permute-start.2
  10.3 0.7 %tile.4 = f32[4,64]{1,0:T(4,128)S(1)} broadcast(f32[64]{0:T(128)} %param.8), dimensions={1} | broadcast | bytes 1280 | tf_op jit(solution)/shard_map/tile | solution.py:273
  11.0 0.1 reshape_tile.6.b1_ref
  11.1 0.7 %tile.5 = f32[4,64]{1,0:T(4,128)S(1)} broadcast(f32[64]{0:T(128)} %param.10), dimensions={1} | broadcast | bytes 1280 | tf_op jit(solution)/shard_map/tile | solution.py:274
  11.7 0.1 reshape_tile.7.b2_ref
  11.8 0.9 %copy.16 = bf16[2,8,16,256]{3,2,1,0:T(8,128)(2,1)S(1)} copy(bf16[2,8,16,256]{3,1,2,0:T(8,128)(2,1)} %bitcast.26) | data formatting | bytes 262144
  12.7 0.0 copy-start
  12.8 1.0 %copy-done = f32[1728,64]{0,1:T(8,128)S(1)} copy-done((f32[1728,64]{0,1:T(8,128)S(1)}, f32[1728,64]{0,1:T(8,128)}, u32[]{:S(2)}) %copy-start) | copy-done | bytes 442392
  13.8 0.0 copy-start.1
  13.8 0.9 %copy-done.1 = f32[864,64]{0,1:T(8,128)S(1)} copy-done((f32[864,64]{0,1:T(8,128)S(1)}, f32[864,64]{0,1:T(8,128)}, u32[]{:S(2)}) %copy-start.1) | copy-done | bytes 221208
  14.7 0.9 %shard_map.109 = (bf16[9,256,256]{2,1,0:T(8,128)(2,1)S(1)}, bf16[9,256,384]{2,1,0:T(8,128)(2,1)S(1)}, bf16[9,384,256]{2,1,0:T(8,128)(2,1)S(1)}, bf16[9,384,128]{2,1,0:T(8,128)(2,1)S(1)}) custom-call(f32[64,864]{1,0:T(8,128)S(1)} %bitcast.25, f32[64,1728]{1,0:T(8,128)S(1)} %bitcast.24), custom_call_target="tpu_custom_call" | custom-call | tf_op jit(solution)/shard_map/pallas_call | solution.py:268
  15.6 0.0 collective-permute-done.2.y_ref
  15.6 3.1 %shard_map.110 = (bf16[6,12,16,256]{3,2,1,0:T(8,128)(2,1)S(1)}, bf16[4,10,16,384]{3,2,1,0:T(8,128)(2,1)S(1)}, f32[4,10,16,256]{3,2,1,0:T(8,128)S(1)}, bf16[2,8,1...) custom-call(bf16[2,8,16,128]{3,2,1,0:T(8,128)(2,1)S(1)} %copy.17, ...), custom_call_target="tpu_custom_call" | custom-call | tf_op jit(solution)/shard_map/pallas_call | solution.py:277
  18.7 1.3 %collective-permute-start.4 = (bf16[2,8,16,256]{3,2,1,0:T(8,128)(2,1)S(1)}, bf16[2,8,16,256]{3,2,1,0:T(8,128)(2,1)S(1)}, u32[]{:S(2)}, u32[]{:S(2)}) collective-permute-start(bf16[2,8,16,256]{3,2,1,0:T(8,128)(2,1)S(1)} %get-tuple-element.25.g_ref), channel_id=1, source_target_pairs={{4,0},{8,4},{12,8},{5,1},{9,5},{13,9},{6,2},{10,6},{14,10},{7,3},{... | collective-permute-start | bytes 393224 | tf_op jit(solution)/shard_map/ppermute | solution.py:249
  20.0 4.9 %collective-permute-start.3 = (bf16[2,8,16,256]{3,2,1,0:T(8,128)(2,1)S(1)}, bf16[2,8,16,256]{3,2,1,0:T(8,128)(2,1)S(1)}, u32[]{:S(2)}, u32[]{:S(2)}) collective-permute-start(bf16[2,8,16,256]{3,2,1,0:T(8,128)(2,1)S(1)} %get-tuple-element.25.g_ref), channel_id=1, source_target_pairs={{0,4},{4,8},{8,12},{1,5},{5,9},{9,13},{2,6},{6,10},{10,14},{3,7},{... | collective-permute-start | bytes 393224 | tf_op jit(solution)/shard_map/ppermute | solution.py:248
  25.0 2.2 %collective-permute-done.4.r_ref = bf16[2,8,16,256]{3,2,1,0:T(8,128)(2,1)S(1)} collective-permute-done((bf16[2,8,16,256]{3,2,1,0:T(8,128)(2,1)S(1)}, bf16[2,8,16,256]{3,2,1,0:T(8,128)(2,1)S(1)}, u32[]{:S(2)}, u32[]{:S(2)}) %collective-permute-start.4) | collective-permute-done | bytes 131104 | tf_op jit(solution)/shard_map/ppermute | solution.py:249
  27.2 1.2 %collective-permute-done.3.l_ref = bf16[2,8,16,256]{3,2,1,0:T(8,128)(2,1)S(1)} collective-permute-done((bf16[2,8,16,256]{3,2,1,0:T(8,128)(2,1)S(1)}, bf16[2,8,16,256]{3,2,1,0:T(8,128)(2,1)S(1)}, u32[]{:S(2)}, u32[]{:S(2)}) %collective-permute-start.3) | collective-permute-done | bytes 131104 | tf_op jit(solution)/shard_map/ppermute | solution.py:248
  28.4 0.1 collective-permute-start.5
  28.4 0.9 %shard_map.111.p2_ref = f32[64,1792]{1,0:T(8,128)S(1)} custom-call(bf16[4,10,16,384]{3,2,1,0:T(8,128)(2,1)S(1)} %get-tuple-element.29.a_ref, bf16[2,8,16,256]{3,2,1,0:T(8,128)(2,1)S(1)} %get-tuple-element.25.g_ref), custom_call_target="tpu_custom_call" | custom-call | tf_op jit(solution)/shard_map/pallas_call | solution.py:289
  29.4 0.3 collective-permute-done.5.y_ref
  29.7 2.9 %shard_map.112 = (f32[32,2688]{1,0:T(8,128)S(1)}, bf16[32,2688]{1,0:T(8,128)(2,1)S(1)}, bf16[4,10,16,384]{3,2,1,0:T(8,128)(2,1)S(1)}) custom-call(bf16[2,8,16,256]{3,2,1,0:T(8,128)(2,1)S(1)} %get-tuple-element.25.g_ref, bf16[2,8,16,256]{3,2,1,0:T(8,128)(2,1)S(1)} %collective-permute-done.3.l_ref, bf16[2,8,16,256]{3,2,1,0:T(8,128)(2,1)S(1)} %collective-permute-done.4.r_ref, ...), custom_call_target="tpu_custom_call" | custom-call | tf_op jit(solution)/shard_map/pallas_call | solution.py:291
  32.6 0.2 collective-permute-start.6
  32.9 1.2 %collective-permute-done.6 = bf16[32,2688]{1,0:T(8,128)(2,1)S(1)} collective-permute-done((bf16[32,2688]{1,0:T(8,128)(2,1)S(1)}, bf16[32,2688]{1,0:T(8,128)(2,1)S(1)}, u32[]{:S(2)}, u32[]{:S(2)}) %collective-permute-start.6) | collective-permute-done | bytes 172064 | tf_op jit(solution)/shard_map/ppermute | solution.py:254
  34.1 2.0 %collective-permute-start.7 = (bf16[32,2688]{1,0:T(8,128)(2,1)S(1)}, bf16[32,2688]{1,0:T(8,128)(2,1)S(1)}, u32[]{:S(2)}, u32[]{:S(2)}) collective-permute-start(bf16[32,2688]{1,0:T(8,128)(2,1)S(1)} %add_convert_fusion), channel_id=1, source_target_pairs={{0,2},{2,0},{1,3},{3,1},{4,6},{6,4},{5,7},{7,5},{8,10},{10,8},{9,1... | collective-permute-start | bytes 516104 | tf_op jit(solution)/shard_map/ppermute | solution.py:254
  36.1 4.7 %collective-permute-done.7 = bf16[32,2688]{1,0:T(8,128)(2,1)S(1)} collective-permute-done((bf16[32,2688]{1,0:T(8,128)(2,1)S(1)}, bf16[32,2688]{1,0:T(8,128)(2,1)S(1)}, u32[]{:S(2)}, u32[]{:S(2)}) %collective-permute-start.7) | collective-permute-done | bytes 172064 | tf_op jit(solution)/shard_map/ppermute | solution.py:254
  40.9 2.5 %collective-permute-start.8 = (bf16[32,2688]{1,0:T(8,128)(2,1)S(1)}, bf16[32,2688]{1,0:T(8,128)(2,1)S(1)}, u32[]{:S(2)}, u32[]{:S(2)}) collective-permute-start(bf16[32,2688]{1,0:T(8,128)(2,1)S(1)} %add.22), channel_id=1, source_target_pairs={{0,4},{4,0},{8,12},{12,8},{1,5},{5,1},{9,13},{13,9},{2,6},{6,2},{1... | collective-permute-start | bytes 516104 | tf_op jit(solution)/shard_map/ppermute | solution.py:254
  43.4 4.1 %collective-permute-done.8 = bf16[32,2688]{1,0:T(8,128)(2,1)S(1)} collective-permute-done((bf16[32,2688]{1,0:T(8,128)(2,1)S(1)}, bf16[32,2688]{1,0:T(8,128)(2,1)S(1)}, u32[]{:S(2)}, u32[]{:S(2)}) %collective-permute-start.8) | collective-permute-done | bytes 172064 | tf_op jit(solution)/shard_map/ppermute | solution.py:254
  47.6 2.9 %collective-permute-start.9 = (bf16[32,2688]{1,0:T(8,128)(2,1)S(1)}, bf16[32,2688]{1,0:T(8,128)(2,1)S(1)}, u32[]{:S(2)}, u32[]{:S(2)}) collective-permute-start(bf16[32,2688]{1,0:T(8,128)(2,1)S(1)} %add.23), channel_id=1, source_target_pairs={{0,8},{4,12},{8,0},{12,4},{1,9},{5,13},{9,1},{13,5},{2,10},{6,14},... | collective-permute-start | bytes 516104 | tf_op jit(solution)/shard_map/ppermute | solution.py:254
  50.5 7.0 %collective-permute-done.9 = bf16[32,2688]{1,0:T(8,128)(2,1)S(1)} collective-permute-done((bf16[32,2688]{1,0:T(8,128)(2,1)S(1)}, bf16[32,2688]{1,0:T(8,128)(2,1)S(1)}, u32[]{:S(2)}, u32[]{:S(2)}) %collective-permute-start.9) | collective-permute-done | bytes 172064 | tf_op jit(solution)/shard_map/ppermute | solution.py:254
  57.5 0.1 collective-permute-start.10
  57.6 0.7 %reshape.34 = bf16[1,2,8,4096]{3,2,1,0:T(8,128)(2,1)} reshape(bf16[2,8,16,256]{3,2,1,0:T(8,128)(2,1)S(1)} %get-tuple-element.24) | data formatting | bytes 262144 | tf_op jit(solution)/shard_map/reshape | solution.py:314
  58.3 0.6 %shard_map.113 = bf16[2,8,16,128]{3,2,1,0:T(8,128)(2,1)S(1)} custom-call(bf16[4,10,16,384]{3,2,1,0:T(8,128)(2,1)S(1)} %get-tuple-element.30.t_ref, bf16[9,384,128]{2,1,0:T(8,128)(2,1)S(1)} %get-tuple-element.31.r1_ref), custom_call_target="tpu_custom_call" | custom-call | tf_op jit(solution)/shard_map/pallas_call | solution.py:302
  59.0 0.7 %reshape.35 = bf16[1,2,8,2048]{3,2,1,0:T(8,128)(2,1)} reshape(bf16[2,8,16,128]{3,2,1,0:T(8,128)(2,1)S(1)} %shard_map.113) | data formatting | bytes 131072 | tf_op jit(solution)/shard_map/reshape | solution.py:315
  59.6 0.0 collective-permute-done.10.h_ref
  59.6 0.9 %shard_map.114 = (f32[64,864]{1,0:T(8,128)}, f32[1,64]{1,0:T(1,128)}, f32[64,1728]{1,0:T(8,128)}, f32[1,64]{1,0:T(1,128)}) custom-call(bf16[32,2688]{1,0:T(8,128)(2,1)S(1)} %add.24.m_ref, bf16[32,2688]{1,0:T(8,128)(2,1)S(1)} %collective-permute-done.10.h_ref), custom_call_target="tpu_custom_call" | custom-call | tf_op jit(solution)/shard_map/pallas_call | solution.py:309
  (12 shorter events, 0.2 us)
Async XLA Ops:
  1.5 7.2 %collective-permute-start.1 = (bf16[2,8,16,128]{3,2,1,0:T(8,128)(2,1)S(1)}, bf16[2,8,16,128]{3,2,1,0:T(8,128)(2,1)S(1)}, u32[]{:S(2)}, u32[]{:S(2)}) collective-permute-start(bf16[2,8,16,128]{3,2,1,0:T(8,128)(2,1)S(1)} %copy.17), channel_id=1, source_target_pairs={{4,0},{8,4},{12,8},{5,1},{9,5},{13,9},{6,2},{10,6},{14,10},{7,3},{... | collective-permute-start | bytes 196616 | tf_op jit(solution)/shard_map/ppermute | solution.py:249
  2.8 7.5 %collective-permute-start = (bf16[2,8,16,128]{3,2,1,0:T(8,128)(2,1)S(1)}, bf16[2,8,16,128]{3,2,1,0:T(8,128)(2,1)S(1)}, u32[]{:S(2)}, u32[]{:S(2)}) collective-permute-start(bf16[2,8,16,128]{3,2,1,0:T(8,128)(2,1)S(1)} %copy.17), channel_id=1, source_target_pairs={{0,4},{4,8},{8,12},{1,5},{5,9},{9,13},{2,6},{6,10},{10,14},{3,7},{... | collective-permute-start | bytes 196616 | tf_op jit(solution)/shard_map/ppermute | solution.py:248
  10.3 5.4 %collective-permute-start.2 = (bf16[6,2,16,128]{3,2,1,0:T(8,128)(2,1)S(1)}, bf16[6,2,16,128]{3,2,1,0:T(8,128)(2,1)S(1)}, u32[]{:S(2)}, u32[]{:S(2)}) collective-permute-start(bf16[6,2,16,128]{3,2,1,0:T(8,128)(2,1)S(1)} %pad_maximum_fusion.1), channel_id=1, source_target_pairs={{0,1},{1,0},{2,3},{3,2},{4,5},{5,4},{6,7},{7,6},{8,9},{9,8},{10,11... | collective-permute-start | bytes 147464 | tf_op jit(solution)/shard_map/ppermute | solution.py:254
  12.7 1.0 %copy-start = (f32[1728,64]{0,1:T(8,128)S(1)}, f32[1728,64]{0,1:T(8,128)}, u32[]{:S(2)}) copy-start(f32[1728,64]{0,1:T(8,128)} %param.9) | copy-start | bytes 1327108
  13.8 0.9 %copy-start.1 = (f32[864,64]{0,1:T(8,128)S(1)}, f32[864,64]{0,1:T(8,128)}, u32[]{:S(2)}) copy-start(f32[864,64]{0,1:T(8,128)} %param.7) | copy-start | bytes 663556
  18.7 8.4 %collective-permute-start.4 = (bf16[2,8,16,256]{3,2,1,0:T(8,128)(2,1)S(1)}, bf16[2,8,16,256]{3,2,1,0:T(8,128)(2,1)S(1)}, u32[]{:S(2)}, u32[]{:S(2)}) collective-permute-start(bf16[2,8,16,256]{3,2,1,0:T(8,128)(2,1)S(1)} %get-tuple-element.25.g_ref), channel_id=1, source_target_pairs={{4,0},{8,4},{12,8},{5,1},{9,5},{13,9},{6,2},{10,6},{14,10},{7,3},{... | collective-permute-start | bytes 393224 | tf_op jit(solution)/shard_map/ppermute | solution.py:249
  20.0 8.3 %collective-permute-start.3 = (bf16[2,8,16,256]{3,2,1,0:T(8,128)(2,1)S(1)}, bf16[2,8,16,256]{3,2,1,0:T(8,128)(2,1)S(1)}, u32[]{:S(2)}, u32[]{:S(2)}) collective-permute-start(bf16[2,8,16,256]{3,2,1,0:T(8,128)(2,1)S(1)} %get-tuple-element.25.g_ref), channel_id=1, source_target_pairs={{0,4},{4,8},{8,12},{1,5},{5,9},{9,13},{2,6},{6,10},{10,14},{3,7},{... | collective-permute-start | bytes 393224 | tf_op jit(solution)/shard_map/ppermute | solution.py:248
  28.4 1.4 %collective-permute-start.5 = (bf16[6,2,16,256]{3,2,1,0:T(8,128)(2,1)S(1)}, bf16[6,2,16,256]{3,2,1,0:T(8,128)(2,1)S(1)}, u32[]{:S(2)}, u32[]{:S(2)}) collective-permute-start(bf16[6,2,16,256]{3,2,1,0:T(8,128)(2,1)S(1)} %pad_maximum_fusion), channel_id=1, source_target_pairs={{0,1},{1,0},{2,3},{3,2},{4,5},{5,4},{6,7},{7,6},{8,9},{9,8},{10,11... | collective-permute-start | bytes 294920 | tf_op jit(solution)/shard_map/ppermute | solution.py:254
  32.6 1.5 %collective-permute-start.6 = (bf16[32,2688]{1,0:T(8,128)(2,1)S(1)}, bf16[32,2688]{1,0:T(8,128)(2,1)S(1)}, u32[]{:S(2)}, u32[]{:S(2)}) collective-permute-start(bf16[32,2688]{1,0:T(8,128)(2,1)S(1)} %get-tuple-element.33), channel_id=1, source_target_pairs={{0,1},{1,0},{2,3},{3,2},{4,5},{5,4},{6,7},{7,6},{8,9},{9,8},{10,11... | collective-permute-start | bytes 516104 | tf_op jit(solution)/shard_map/ppermute | solution.py:254
  34.1 6.7 %collective-permute-start.7 = (bf16[32,2688]{1,0:T(8,128)(2,1)S(1)}, bf16[32,2688]{1,0:T(8,128)(2,1)S(1)}, u32[]{:S(2)}, u32[]{:S(2)}) collective-permute-start(bf16[32,2688]{1,0:T(8,128)(2,1)S(1)} %add_convert_fusion), channel_id=1, source_target_pairs={{0,2},{2,0},{1,3},{3,1},{4,6},{6,4},{5,7},{7,5},{8,10},{10,8},{9,1... | collective-permute-start | bytes 516104 | tf_op jit(solution)/shard_map/ppermute | solution.py:254
  40.9 6.6 %collective-permute-start.8 = (bf16[32,2688]{1,0:T(8,128)(2,1)S(1)}, bf16[32,2688]{1,0:T(8,128)(2,1)S(1)}, u32[]{:S(2)}, u32[]{:S(2)}) collective-permute-start(bf16[32,2688]{1,0:T(8,128)(2,1)S(1)} %add.22), channel_id=1, source_target_pairs={{0,4},{4,0},{8,12},{12,8},{1,5},{5,1},{9,13},{13,9},{2,6},{6,2},{1... | collective-permute-start | bytes 516104 | tf_op jit(solution)/shard_map/ppermute | solution.py:254
  47.6 9.9 %collective-permute-start.9 = (bf16[32,2688]{1,0:T(8,128)(2,1)S(1)}, bf16[32,2688]{1,0:T(8,128)(2,1)S(1)}, u32[]{:S(2)}, u32[]{:S(2)}) collective-permute-start(bf16[32,2688]{1,0:T(8,128)(2,1)S(1)} %add.23), channel_id=1, source_target_pairs={{0,8},{4,12},{8,0},{12,4},{1,9},{5,13},{9,1},{13,5},{2,10},{6,14},... | collective-permute-start | bytes 516104 | tf_op jit(solution)/shard_map/ppermute | solution.py:254
  57.5 2.1 %collective-permute-start.10 = (bf16[32,2688]{1,0:T(8,128)(2,1)S(1)}, bf16[32,2688]{1,0:T(8,128)(2,1)S(1)}, u32[]{:S(2)}, u32[]{:S(2)}) collective-permute-start(bf16[32,2688]{1,0:T(8,128)(2,1)S(1)} %add.24.m_ref), channel_id=1, source_target_pairs={{0,1},{1,0},{2,3},{3,2},{4,5},{5,4},{6,7},{7,6},{8,9},{9,8},{10,11... | collective-permute-start | bytes 516104 | tf_op jit(solution)/shard_map/ppermute | solution.py:254

commit v2 on v1

v2 whole, which is shorter than its diff:
```python
import jax
import jax.numpy as jnp
from jax import lax
from jax.experimental import pallas as pl
from jax.experimental.pallas import tpu as pltpu
from jax.sharding import PartitionSpec as P

C_IN = 32
C_MID = 64
DEPTH = 64
BF = jnp.bfloat16
F32 = jnp.float32
GROUP = 4
ROWS = DEPTH // GROUP
IN_L = GROUP * C_IN
MID_L = GROUP * C_MID
TAP1 = 3 * C_IN
TAP2 = 3 * C_MID
W1_L = 9 * TAP1
W2_L = 9 * TAP2
PACK2 = 1792
PACK1 = 896
NT = (((1,), (1,)), ((), ()))
NN = (((1,), (0,)), ((), ()))


def call(body, flops, outs, scratch=(), vmem=16 << 20, **specs):
    return pl.pallas_call(
        body,
        out_shape=[jax.ShapeDtypeStruct(shape, kind) for shape, kind in outs],
        scratch_shapes=list(scratch),
        compiler_params=pltpu.CompilerParams(vmem_limit_bytes=vmem),
        cost_estimate=pl.CostEstimate(flops=flops, bytes_accessed=flops // 256, transcendentals=0),
        **specs,
    )


def dot(a, b, dims):
    return lax.dot_general(a, b, dims, preferred_element_type=F32)


def window(ref, start, width):
    frame = 256 if width <= 128 else 384
    at = start // 128 * 128
    stop = min(at + frame, ref.shape[1])
    value = ref[:, at:stop]
    if stop < at + frame:
        value = jnp.concatenate([value, jnp.zeros((64, at + frame - stop), F32)], axis=1)
    if start != at:
        value = pltpu.roll(value, frame - (start - at), 1)
    lane = lax.broadcasted_iota(jnp.int32, value.shape, 1)
    return jnp.where(lane < width, value, 0.0)


def banded_body(w1_ref, w2_ref, b1_ref, b2_ref, f1_ref, f2_ref, r2_ref, r1_ref, bias_ref, pad1, pad2, lines, sems):
    copies = [
        pltpu.make_async_copy(w1_ref, pad1, sems.at[0]),
        pltpu.make_async_copy(w2_ref, pad2, sems.at[1]),
        pltpu.make_async_copy(b1_ref, lines.at[pl.ds(0, 1)], sems.at[2]),
        pltpu.make_async_copy(b2_ref, lines.at[pl.ds(1, 1)], sems.at[3]),
    ]
    for copy in copies:
        copy.start()
    for copy in copies:
        copy.wait()
    bias_ref[...] = jnp.concatenate([lines[...]] * GROUP, axis=1)
    for tap in range(9):
        one = window(pad1, tap * TAP1, TAP1)
        two = window(pad2, tap * TAP2, TAP2)
        for m in range(-1, 5):
            at = (m % 6) * C_MID
            s1 = pltpu.roll(one, ((m - 1) * C_IN) % 256, 1) if m != 1 else one
            s2 = pltpu.roll(two, ((m - 1) * C_MID) % 384, 1) if m != 1 else two
            s1 = s1.astype(BF)
            s2 = s2.astype(BF)
            if 0 <= m < 4:
                f1_ref[tap, m * C_MID : (m + 1) * C_MID, :] = s1
                f2_ref[tap, m * C_MID : (m + 1) * C_MID, :] = s2
            r1_ref[tap, at : at + C_MID, :] = s1[:, :IN_L]
            r2_ref[tap, at : at + C_MID, :] = s2[:, :MID_L]


def edges(value, low, high):
    count = value.shape[0]
    row = lax.broadcasted_iota(jnp.int32, (count, 128), 0) % ROWS
    lane = lax.broadcasted_iota(jnp.int32, (count, 128), 1)
    after = pltpu.roll(value[:, low : low + 128], count - 1, 0)
    before = pltpu.roll(value[:, high : high + 128], 1, 0)
    after = jnp.where(row == ROWS - 1, 0.0, after)
    before = jnp.where(row == 0, 0.0, before)
    return jnp.where(lane < 64, after, before)


def spread(parts, core, to_ref, lanes):
    for x, (middle, side) in enumerate(parts):
        side = side.astype(F32)
        low = jnp.where(core == 1, side, 0.0)
        high = jnp.where(core == 0, side, 0.0)
        cells = jnp.concatenate([low, middle.astype(F32), high], axis=0)
        rows = cells.reshape(-1, lanes)
        shape = cells.shape[:2]
        to_ref[x, :, :, :lanes] = cells.astype(BF)
        edge = edges(rows, 0, lanes - 128)
        to_ref[x, :, :, lanes:] = edge.astype(BF).reshape(*shape, 128)


def gathered(own, even, odd, beside, core, space, width):
    count, depth = own.shape[0], even.shape[0]
    end = own.shape[1]
    head, tail = pl.ds(0, width), pl.ds(end - width, width)

    def near(i):
        return jnp.where(core == 0, beside[i, head], beside[i, tail])

    flip = space % 2 == 1
    one = [(even[i], near(i)) for i in range(depth)]
    two = [(odd[i], near(depth + count + i)) for i in range(depth)]
    left = [(jnp.where(flip, p[0], q[0]), jnp.where(flip, p[1], q[1])) for p, q in zip(one, two)]
    right = [(jnp.where(flip, q[0], p[0]), jnp.where(flip, q[1], p[1])) for p, q in zip(one, two)]
    return left + [(own[i], near(depth + i)) for i in range(count)] + right


def plane_mask(x, rows, space, last, core):
    row = lax.broadcasted_iota(jnp.int32, (rows, 1), 0)
    inside = jnp.float32(1.0)
    if x == 0:
        inside = jnp.where(space > 0, 1.0, 0.0)
    if x == 3:
        inside = jnp.where(space < last, 1.0, 0.0)
    low = jnp.where(core == 1, 1.0, 0.0)
    high = jnp.where(core == 0, 1.0, 0.0)
    mask = jnp.where(row < ROWS, low, jnp.where(row >= rows - ROWS, high, 1.0))
    return mask * inside


def forward_body(x_ref, ev_ref, od_ref, by_ref, f1_ref, f2_ref, b_ref, c_ref, e_ref, a_ref, d_ref, o_ref, g_ref, acc):
    core = lax.axis_index("ysp")
    space = lax.axis_index("space")
    last = lax.axis_size("space") - 1
    spread(gathered(x_ref, ev_ref, od_ref, by_ref, core, space, 2), core, e_ref, IN_L)
    wide = x_ref.shape[1] + 2
    narrow = wide - 2
    total = None
    for tap in range(9):
        a, b = divmod(tap, 3)
        part = dot(e_ref[a : a + 4, b : b + wide].reshape(-1, 256), f1_ref[tap], NT)
        total = part if total is None else total + part
    acc[...] = total
    rows = wide * ROWS
    bias1, bias2 = b_ref[0:1], b_ref[1:2]
    for x in range(4):
        y1 = acc[x * rows : (x + 1) * rows, :] + bias1
        mask = plane_mask(x, rows, space, last, core)
        sig = jax.nn.sigmoid(y1)
        d_ref[x] = (sig * (1.0 + y1 * (1.0 - sig)) * mask).reshape(wide, ROWS, MID_L)
        act = (y1 * sig * mask).astype(BF)
        a_ref[x, :, :, :MID_L] = act.reshape(wide, ROWS, MID_L)
        edge = edges(act.astype(F32), 0, 128)
        a_ref[x, :, :, MID_L:] = edge.astype(BF).reshape(wide, ROWS, 128)
    total = None
    for tap in range(9):
        a, b = divmod(tap, 3)
        part = dot(a_ref[a : a + 2, b : b + narrow].reshape(-1, 384), f2_ref[tap], NT)
        total = part if total is None else total + part
    y2 = total + bias2
    sig = jax.nn.sigmoid(y2)
    shape = o_ref.shape
    o_ref[...] = (y2 * sig).astype(BF).reshape(shape)
    cot = c_ref[...].reshape(-1, MID_L).astype(F32)
    g_ref[...] = (cot * (sig * (1.0 + y2 * (1.0 - sig)))).astype(BF).reshape(shape)


def flipped(grads):
    turned = grads.astype(F32).T
    sums = jnp.sum(turned, axis=1, keepdims=True)
    bias = sums[0:64] + sums[64:128] + sums[128:192] + sums[192:256]
    return turned.astype(BF), bias


def tap_sum(product, step):
    frame = product.shape[1]
    total = product[64:128]
    for j in (0, 2, 3):
        total = total + pltpu.roll(product[j * 64 : (j + 1) * 64], (frame - (j - 1) * step) % frame, 1)
    return total


def second_weights_body(a_ref, g_ref, k_ref, s_ref, p_ref):
    turned, bias = flipped(g_ref[...].reshape(-1, MID_L))
    narrow = g_ref.shape[1]
    lane = lax.broadcasted_iota(jnp.int32, (64, 384), 1)
    held = None
    for tap in range(9):
        a, b = divmod(tap, 3)
        found = tap_sum(dot(turned, a_ref[a : a + 2, b : b + narrow].reshape(-1, 384), NN), C_MID)
        if tap == 8:
            p_ref[:, 1536:1792] = jnp.where(lane < TAP2, found, bias)[:, :256]
        elif tap % 2 == 0:
            held = found
        else:
            at = (tap - 1) * TAP2
            p_ref[:, at : at + 384] = jnp.where(lane < TAP2, held, pltpu.roll(found, TAP2, 1))
    halves(p_ref, k_ref, s_ref)


def halves(pack, keep_ref, send_ref):
    core = lax.axis_index("ysp")
    keep_ref[...] = pack[pl.ds(core * 32, 32), :]
    send_ref[...] = pack[pl.ds((1 - core) * 32, 32), :].astype(BF)


def adjoint(wide_ref, taps_ref, tall, wide):
    total = None
    for tap in range(9):
        a, b = divmod(tap, 3)
        part = dot(wide_ref[2 - a : 2 - a + tall, 2 - b : 2 - b + wide].reshape(-1, 384), taps_ref[tap], NN)
        total = part if total is None else total + part
    return total


def backward_body(g_ref, ev_ref, od_ref, by_ref, r2_ref, d_ref, e_ref, k_ref, s_ref, t_ref, wide_g, acc, pack):
    core = lax.axis_index("ysp")
    space = lax.axis_index("space")
    spread(gathered(g_ref, ev_ref, od_ref, by_ref, core, space, 2), core, wide_g, MID_L)
    narrow = g_ref.shape[1]
    wide = narrow + 2
    rows = wide * ROWS
    acc[...] = adjoint(wide_g, r2_ref, 4, wide)
    for x in range(4):
        slope = d_ref[x].reshape(rows, MID_L)
        g1 = (acc[x * rows : (x + 1) * rows, :] * slope).astype(BF)
        t_ref[x, :, :, :MID_L] = g1.reshape(wide, ROWS, MID_L)
        edge = edges(g1.astype(F32), 0, 128)
        t_ref[x, :, :, MID_L:] = edge.astype(BF).reshape(wide, ROWS, 128)
    g1 = t_ref[1:3, 1 : 1 + narrow, :, :MID_L].reshape(-1, MID_L)
    turned, bias = flipped(g1)
    lane = lax.broadcasted_iota(jnp.int32, (64, 384), 1)
    none = jnp.zeros((64, 128), F32)
    held = None
    for tap in range(9):
        a, b = divmod(tap, 3)
        cells = e_ref[1 + a : 3 + a, 1 + b : 1 + b + narrow].reshape(-1, 256)
        found = tap_sum(dot(turned, cells, NN), C_IN)
        if tap == 8:
            pack[:, 768:896] = jnp.where(lane < TAP1, jnp.concatenate([found, none], axis=1), bias)[:, :128]
            continue
        found = jnp.concatenate([found, none], axis=1)
        slot = tap % 4
        if slot == 0:
            held = found
        else:
            held = jnp.where(lane < slot * TAP1, held, pltpu.roll(found, slot * TAP1, 1))
        if slot == 3:
            at = (tap - 3) * TAP1
            pack[:, at : at + 384] = held
    halves(pack, k_ref, s_ref)


def input_grad_body(t_ref, r1_ref, o_ref):
    o_ref[...] = adjoint(t_ref, r1_ref, *o_ref.shape[:2]).astype(BF).reshape(o_ref.shape)


def finish_body(m_ref, h_ref, w2_ref, b2_ref, w1_ref, b1_ref, pack):
    core = lax.axis_index("ysp")
    pack[pl.ds(core * 32, 32), :] = m_ref[...].astype(F32)
    pack[pl.ds((1 - core) * 32, 32), :] = h_ref[...].astype(F32)
    row = lax.broadcasted_iota(jnp.int32, (64, 64), 0)
    col = lax.broadcasted_iota(jnp.int32, (64, 64), 1)
    for at, w_ref, b_ref in ((0, w2_ref, b2_ref), (PACK2, w1_ref, b1_ref)):
        width = w_ref.shape[1]
        w_ref[...] = pack[:, at : at + width]
        spot = jnp.broadcast_to(pack[:, at + width : at + width + 1], (64, 64))
        b_ref[...] = jnp.sum(jnp.where(row == col, spot, 0.0), axis=0, keepdims=True)


def swap(cells, axis, bit):
    return lax.ppermute(cells, axis, [(i, i ^ bit) for i in range(lax.axis_size(axis))])


def halo(own, even, odd):
    count = lax.axis_size("space")
    pairs = [(i, i + 1) for i in range(1, count - 1, 2)]
    odd = lax.ppermute(odd, "space", pairs + [(j, i) for i, j in pairs])
    pairs = [(i, i + 1) for i in range(0, count - 1, 2)]
    even = lax.ppermute(even, "space", pairs + [(j, i) for i, j in pairs])
    return even, odd


def other_core(own, even, odd):
    return swap(jnp.concatenate([even, own, odd], axis=0), "ysp", 1)


hold = lax.optimization_barrier


def first_half(keep, send):
    return hold((keep + swap(send, "ysp", 1).astype(F32)).astype(BF))


def masks(axis):
    return [(axis, 2 * m - 1) for m in (1, 2, 4, 8, 16, 32, 64) if m < lax.axis_size(axis)]


def stage(total, axis, mask):
    return hold(total + swap(total, axis, mask))


def on_device(inputs, w_first, b_first, w_second, b_second, cotangent):
    nx, ny = inputs.shape[1], inputs.shape[2]
    own = inputs.reshape(nx, ny, ROWS, IN_L)
    even, odd = halo(own, own, own)
    hbm = pl.BlockSpec(memory_space=pltpu.HBM)
    banded = call(
        banded_body,
        2000000000,
        [
            ((9, 256, 256), BF),
            ((9, 256, 384), BF),
            ((9, 384, 256), BF),
            ((9, 384, 128), BF),
            ((2, MID_L), F32),
        ],
        [
            pltpu.VMEM((64, W1_L), F32),
            pltpu.VMEM((64, W2_L), F32),
            pltpu.VMEM((2, C_MID), F32),
            pltpu.SemaphoreType.DMA((4,)),
        ],
        vmem=16 << 20,
        in_specs=[hbm] * 4,
    )(*[pltpu.with_memory_space_constraint(v, pltpu.HBM) for v in (w_first.T, w_second.T, b_first.reshape(1, C_MID), b_second.reshape(1, C_MID))])
    cot = cotangent.reshape(nx, ny, ROWS, MID_L)
    even, odd, cot, f1, f2, r2, r1, bias = hold((even, odd, cot, *banded))
    wide_in, act, slope, out, g2 = call(
        forward_body,
        4800000000,
        [
            ((nx + 4, ny + 4, ROWS, 256), BF),
            ((nx + 2, ny + 2, ROWS, 384), BF),
            ((nx + 2, ny + 2, ROWS, MID_L), F32),
            ((nx, ny, ROWS, MID_L), BF),
            ((nx, ny, ROWS, MID_L), BF),
        ],
        [pltpu.VMEM(((nx + 2) * (ny + 2) * ROWS, MID_L), F32)],
    )(own, even, odd, other_core(own, even, odd), f1, f2, bias, cot)
    even, odd = halo(g2, g2, g2)
    keep2, send2 = call(
        second_weights_body, 1800000000, [((32, PACK2), F32), ((32, PACK2), BF)], [pltpu.VMEM((64, PACK2), F32)]
    )(act, g2)
    *early, final = masks("dp") + masks("space")
    even, odd, keep2, send2 = hold((even, odd, keep2, send2))
    sum2 = first_half(keep2, send2)
    got2 = swap(sum2, *early[0])
    keep1, send1, wide_g = call(
        backward_body,
        5600000000,
        [((32, PACK1), F32), ((32, PACK1), BF), ((nx + 2, ny + 2, ROWS, 384), BF)],
        [
            pltpu.VMEM((nx + 4, ny + 4, ROWS, 384), BF),
            pltpu.VMEM(((nx + 2) * (ny + 2) * ROWS, MID_L), F32),
            pltpu.VMEM((64, PACK1), F32),
        ],
    )(g2, even, odd, other_core(g2, even, odd), r2, slope, wide_in)
    got2, keep1, send1, wide_g = hold((got2, keep1, send1, wide_g))
    sum2 = hold(sum2 + got2)
    for axis, mask in early[1:]:
        sum2 = stage(sum2, axis, mask)
    sum1 = first_half(keep1, send1)
    (d_in,) = call(input_grad_body, 1200000000, [((nx, ny, ROWS, IN_L), BF)])(wide_g, r1)
    output = out.reshape(1, nx, ny, DEPTH * C_MID)
    input_grad = d_in.reshape(1, nx, ny, DEPTH * C_IN)
    sum2 = stage(sum2, *final)
    for at, (axis, mask) in enumerate([*early, final]):
        got1 = swap(sum1, axis, mask)
        if at == 0:
            got1, output, input_grad = hold((got1, output, input_grad))
        sum1 = hold(sum1 + got1)
    total = jnp.concatenate([sum2, sum1], axis=1)
    gw2, gb2, gw1, gb1 = call(
        finish_body,
        1200000000,
        [((64, W2_L), F32), ((1, 64), F32), ((64, W1_L), F32), ((1, 64), F32)],
        [pltpu.VMEM((64, PACK2 + PACK1), F32)],
    )(total, swap(total, "ysp", 1))
    return (output, input_grad, gw1.T, gb1.reshape(64), gw2.T, gb2.reshape(64))


def solution(mesh):
    placed = P(("groups", "dp"), "space", "ysp", None)
    return jax.shard_map(
        on_device,
        mesh=mesh,
        in_specs=(placed, P(), P(), P(), P(), placed),
        out_specs=(placed, placed, P("groups", None), P("groups"), P("groups", None), P("groups")),
        check_vma=False,
    )
```

time: 60.9 us -> 50.1 us (0.82)
  waiting for transfers between devices: 22.6 us -> 13.1 us
  local copies, waits for them, and re-layouts: 6.62 us -> 2.26 us
  starting transfers between devices: 20.9 us -> 22.8 us
  Pallas kernels: 9.4 us -> 10.7 us
    ppermute x7 -> x11, waiting for transfers between devices: 17.4 us -> 10.5 us  [swap(): lax.ppermute(cells, axis, [(i, i ^ bit) for i in range(lax.axis_size(axis...]
    ppermute x7 -> x11, starting transfers between devices: 7.85 us -> 11.8 us  [swap(): lax.ppermute(cells, axis, [(i, i ^ bit) for i in range(lax.axis_size(axis...]
    unnamed x6 -> x4, local copies, waits for them, and re-layouts: 3.73 us -> 0.88 us
    ppermute x4, waiting for transfers between devices: 5.23 us -> 2.6 us  [the longest x2 2.6 us: halo(): even = lax.ppermute(even, 'space', pairs + [(j, i) for i, j in pairs])]
    ppermute x4, starting transfers between devices: 13 us -> 11 us  [the longest x2 9.68 us: halo(): even = lax.ppermute(even, 'space', pairs + [(j, i) for i, j in pairs])]
    another operation x4 -> x0, local copies, waits for them, and re-layouts: 1.48 us -> none  [the longest x2 0.74 us: on_device(): bias1 = jnp.tile(b_first, GROUP).reshape(1, MID_L)]
    pallas_call x6, Pallas kernels: 9.4 us -> 10.7 us  [the longest x1 3.11 us: on_device(): call(forward_body, 4800000000, [((nx + 4, ny + 4, ROWS, 256), BF), ((nx +...]
  transfers between devices with their start and end apart: 11 -> 15, of which waited for: 9 -> 9; matrix products, arithmetic and copies ran while one was open for 6% -> 3% of each run, Pallas kernels for 4% -> 13%
where the time goes in v2:
time: 50.1 us; the launch traced here: 49.9 us
  starting transfers between devices  22.8 us (46%)
  waiting for transfers between devices  13.1 us (26%)
  Pallas kernels  10.7 us (21%)
  local copies, waits for them, and re-layouts  2.26 us (5%)
  between operations  0.79 us (2%)
    ppermute x11, starting transfers between devices, swap(): lax.ppermute(cells, axis, [(i, i ^ bit) for i in range(lax.axis_size(axis...  11.8 us
    ppermute x11, waiting for transfers between devices, swap(): lax.ppermute(cells, axis, [(i, i ^ bit) for i in range(lax.axis_size(axis...  10.5 us
    ppermute x2, starting transfers between devices, halo(): even = lax.ppermute(even, 'space', pairs + [(j, i) for i, j in pairs])  9.68 us
    pallas_call x1, Pallas kernels, on_device(): call(forward_body, 4800000000, [((nx + 4, ny + 4, ROWS, 256), BF), ((nx +...  3.11 us
    pallas_call x1, Pallas kernels, on_device(): call(backward_body, 5600000000, [((32, PACK1), F32), ((32, PACK1), BF), (...  2.91 us
    ppermute x2, waiting for transfers between devices, halo(): even = lax.ppermute(even, 'space', pairs + [(j, i) for i, j in pairs])  2.6 us
    pallas_call x1, Pallas kernels, on_device(): call(banded_body, 2000000000, [((9, 256, 256), BF), ((9, 256, 384), BF),...  2.08 us
    ppermute x2, starting transfers between devices, halo(): odd = lax.ppermute(odd, 'space', pairs + [(j, i) for i, j in pairs])  1.33 us
  transfers between devices with their start and end apart: 15, of which 9 were waited for; matrix products, arithmetic and copies ran while one was open for 3% of the time, Pallas kernels for 13%

profile of v2, /device:TPU:0, one launch (start us, length us, event | category | flops | bytes accessed | tf_op | source)
XLA Modules:
  0.0 49.9 jit_solution(2036825936694015594)
XLA Ops:
  0.6 0.9 %copy.17 = bf16[2,8,16,128]{3,2,1,0:T(8,128)(2,1)S(1)} copy(bf16[2,8,16,128]{3,1,2,0:T(8,128)(2,1)} %bitcast.27) | data formatting | bytes 131072
  1.5 0.7 %collective-permute-start.1 = (bf16[2,8,16,128]{3,2,1,0:T(8,128)(2,1)S(1)}, bf16[2,8,16,128]{3,2,1,0:T(8,128)(2,1)S(1)}, u32[]{:S(2)}, u32[]{:S(2)}) collective-permute-start(bf16[2,8,16,128]{3,2,1,0:T(8,128)(2,1)S(1)} %copy.17), channel_id=1, source_target_pairs={{4,8},{8,4},{5,9},{9,5},{6,10},{10,6},{7,11},{11,7},{20,24},{24,20... | collective-permute-start | bytes 196616 | tf_op jit(solution)/shard_map/ppermute | solution.py:283
  2.2 5.9 %collective-permute-start = (bf16[2,8,16,128]{3,2,1,0:T(8,128)(2,1)S(1)}, bf16[2,8,16,128]{3,2,1,0:T(8,128)(2,1)S(1)}, u32[]{:S(2)}, u32[]{:S(2)}) collective-permute-start(bf16[2,8,16,128]{3,2,1,0:T(8,128)(2,1)S(1)} %copy.17), channel_id=1, source_target_pairs={{0,4},{8,12},{4,0},{12,8},{1,5},{9,13},{5,1},{13,9},{2,6},{10,14},... | collective-permute-start | bytes 196616 | tf_op jit(solution)/shard_map/ppermute | solution.py:285
  8.1 0.0 copy-start
  8.1 2.1 %shard_map.109 = (bf16[9,256,256]{2,1,0:T(8,128)(2,1)S(1)}, bf16[9,256,384]{2,1,0:T(8,128)(2,1)S(1)}, bf16[9,384,256]{2,1,0:T(8,128)(2,1)S(1)}, bf16[9,384,128]{2,1,0:T(8,128)(2,1)S(1)}, f32[2,256]{1,0:T(2,128)S(1)}) custom-call(f32[64,864]{1,0:T(8,128)} %bitcast.29, f32[64,1728]{1,0:T(8,128)} %bitcast.28, f32[1,64]{1,0:T(1,128)} %bitcast.30, f32[1,64]{1,0:T(1,128)} %bitcast.31), custom_call_target="tpu_custom_call" | custom-call | flops 2000000000 | bytes 7812500 | tf_op jit(solution)/shard_map/pallas_call | solution.py:313
  10.2 0.0 copy-done
  10.2 0.0 collective-permute-done.1.od_ref
  10.2 0.1 collective-permute-done.ev_ref
  10.3 0.1 collective-permute-start.2
  10.4 1.4 %collective-permute-done.2.by_ref = bf16[6,8,16,128]{3,2,1,0:T(8,128)(2,1)S(1)} collective-permute-done((bf16[6,8,16,128]{3,2,1,0:T(8,128)(2,1)S(1)}, bf16[6,8,16,128]{3,2,1,0:T(8,128)(2,1)S(1)}, u32[]{:S(2)}, u32[]{:S(2)}) %collective-permute-start.2) | collective-permute-done | bytes 196640 | tf_op jit(solution)/shard_map/ppermute | solution.py:277
  11.8 3.1 %shard_map.110 = (bf16[6,12,16,256]{3,2,1,0:T(8,128)(2,1)S(1)}, bf16[4,10,16,384]{3,2,1,0:T(8,128)(2,1)S(1)}, f32[4,10,16,256]{3,2,1,0:T(8,128)S(1)}, bf16[2,8,1...) custom-call(bf16[2,8,16,128]{3,2,1,0:T(8,128)(2,1)S(1)} %copy.17, ...), custom_call_target="tpu_custom_call" | custom-call | flops 4800000000 | bytes 18750000 | tf_op jit(solution)/shard_map/pallas_call | solution.py:334
  15.0 0.7 %collective-permute-start.4 = (bf16[2,8,16,256]{3,2,1,0:T(8,128)(2,1)S(1)}, bf16[2,8,16,256]{3,2,1,0:T(8,128)(2,1)S(1)}, u32[]{:S(2)}, u32[]{:S(2)}) collective-permute-start(bf16[2,8,16,256]{3,2,1,0:T(8,128)(2,1)S(1)} %get-tuple-element.55.g_ref), channel_id=1, source_target_pairs={{4,8},{8,4},{5,9},{9,5},{6,10},{10,6},{7,11},{11,7},{20,24},{24,20... | collective-permute-start | bytes 393224 | tf_op jit(solution)/shard_map/ppermute | solution.py:283
  15.6 3.8 %collective-permute-start.3 = (bf16[2,8,16,256]{3,2,1,0:T(8,128)(2,1)S(1)}, bf16[2,8,16,256]{3,2,1,0:T(8,128)(2,1)S(1)}, u32[]{:S(2)}, u32[]{:S(2)}) collective-permute-start(bf16[2,8,16,256]{3,2,1,0:T(8,128)(2,1)S(1)} %get-tuple-element.55.g_ref), channel_id=1, source_target_pairs={{0,4},{8,12},{4,0},{12,8},{1,5},{9,13},{5,1},{13,9},{2,6},{10,14},... | collective-permute-start | bytes 393224 | tf_op jit(solution)/shard_map/ppermute | solution.py:285
  19.4 1.0 %shard_map.111 = (f32[32,1792]{1,0:T(8,128)S(1)}, bf16[32,1792]{1,0:T(8,128)(2,1)S(1)}) custom-call(bf16[4,10,16,384]{3,2,1,0:T(8,128)(2,1)S(1)} %get-tuple-element.56.a_ref, bf16[2,8,16,256]{3,2,1,0:T(8,128)(2,1)S(1)} %get-tuple-element.55.g_ref), custom_call_target="tpu_custom_call" | custom-call | flops 1800000000 | bytes 7031250 | tf_op jit(solution)/shard_map/pallas_call | solution.py:347
  20.4 0.0 collective-permute-done.4.od_ref
  20.4 2.5 %collective-permute-done.3.ev_ref = bf16[2,8,16,256]{3,2,1,0:T(8,128)(2,1)S(1)} collective-permute-done((bf16[2,8,16,256]{3,2,1,0:T(8,128)(2,1)S(1)}, bf16[2,8,16,256]{3,2,1,0:T(8,128)(2,1)S(1)}, u32[]{:S(2)}, u32[]{:S(2)}) %collective-permute-start.3) | collective-permute-done | bytes 131104 | tf_op jit(solution)/shard_map/ppermute | solution.py:285
  22.9 0.0 collective-permute-start.5
  23.0 0.6 %collective-permute-start.7 = (bf16[6,8,16,256]{3,2,1,0:T(8,128)(2,1)S(1)}, bf16[6,8,16,256]{3,2,1,0:T(8,128)(2,1)S(1)}, u32[]{:S(2)}, u32[]{:S(2)}) collective-permute-start(bf16[6,8,16,256]{3,2,1,0:T(8,128)(2,1)S(1)} %pad_maximum_fusion), channel_id=1, source_target_pairs={{0,1},{1,0},{2,3},{3,2},{4,5},{5,4},{6,7},{7,6},{8,9},{9,8},{10,11... | collective-permute-start | bytes 1179656 | tf_op jit(solution)/shard_map/ppermute | solution.py:277
  23.6 0.7 %collective-permute-done.5 = bf16[32,1792]{1,0:T(8,128)(2,1)S(1)} collective-permute-done((bf16[32,1792]{1,0:T(8,128)(2,1)S(1)}, bf16[32,1792]{1,0:T(8,128)(2,1)S(1)}, u32[]{:S(2)}, u32[]{:S(2)}) %collective-permute-start.5) | collective-permute-done | bytes 114720 | tf_op jit(solution)/shard_map/ppermute | solution.py:277
  24.3 1.6 %collective-permute-start.6 = (bf16[32,1792]{1,0:T(8,128)(2,1)S(1)}, bf16[32,1792]{1,0:T(8,128)(2,1)S(1)}, u32[]{:S(2)}, u32[]{:S(2)}) collective-permute-start(bf16[32,1792]{1,0:T(8,128)(2,1)S(1)} %add_convert_fusion), channel_id=1, source_target_pairs={{0,2},{2,0},{1,3},{3,1},{4,6},{6,4},{5,7},{7,5},{8,10},{10,8},{9,1... | collective-permute-start | bytes 344072 | tf_op jit(solution)/shard_map/ppermute | solution.py:277
  25.8 0.0 collective-permute-done.7.by_ref
  25.8 2.9 %shard_map.112 = (f32[32,896]{1,0:T(8,128)S(1)}, bf16[32,896]{1,0:T(8,128)(2,1)S(1)}, bf16[4,10,16,384]{3,2,1,0:T(8,128)(2,1)S(1)}) custom-call(bf16[2,8,16,256]{3,2,1,0:T(8,128)(2,1)S(1)} %get-tuple-element.55.g_ref, bf16[2,8,16,256]{3,2,1,0:T(8,128)(2,1)S(1)} %collective-permute-done.3.ev_ref, bf16[2,8,16,256]{3,2,1,0:T(8,128)(2,1)S(1)} %collective-permute-done.4.od_ref, ...), custom_call_target="tpu_custom_call" | custom-call | flops 5600000000 | bytes 21875000 | tf_op jit(solution)/shard_map/pallas_call | solution.py:354
  28.8 0.8 %collective-permute-done.6 = bf16[32,1792]{1,0:T(8,128)(2,1)S(1)} collective-permute-done((bf16[32,1792]{1,0:T(8,128)(2,1)S(1)}, bf16[32,1792]{1,0:T(8,128)(2,1)S(1)}, u32[]{:S(2)}, u32[]{:S(2)}) %collective-permute-start.6) | collective-permute-done | bytes 114720 | tf_op jit(solution)/shard_map/ppermute | solution.py:277
  29.6 0.0 collective-permute-start.8
  29.6 0.7 %reshape.40 = bf16[1,2,8,4096]{3,2,1,0:T(8,128)(2,1)} reshape(bf16[2,8,16,256]{3,2,1,0:T(8,128)(2,1)S(1)} %get-tuple-element.71) | data formatting | bytes 262144 | tf_op jit(solution)/shard_map/reshape | solution.py:370
  30.3 1.8 %collective-permute-start.10 = (bf16[32,1792]{1,0:T(8,128)(2,1)S(1)}, bf16[32,1792]{1,0:T(8,128)(2,1)S(1)}, u32[]{:S(2)}, u32[]{:S(2)}) collective-permute-start(bf16[32,1792]{1,0:T(8,128)(2,1)S(1)} %add.26), channel_id=1, source_target_pairs={{0,4},{4,0},{8,12},{12,8},{1,5},{5,1},{9,13},{13,9},{2,6},{6,2},{1... | collective-permute-start | bytes 344072 | tf_op jit(solution)/shard_map/ppermute | solution.py:277
  32.1 0.0 collective-permute-done.8
  32.1 1.6 %collective-permute-start.9 = (bf16[32,896]{1,0:T(8,128)(2,1)S(1)}, bf16[32,896]{1,0:T(8,128)(2,1)S(1)}, u32[]{:S(2)}, u32[]{:S(2)}) collective-permute-start(bf16[32,896]{1,0:T(8,128)(2,1)S(1)} %add_convert_fusion.1), channel_id=1, source_target_pairs={{0,2},{2,0},{1,3},{3,1},{4,6},{6,4},{5,7},{7,5},{8,10},{10,8},{9,1... | collective-permute-start | bytes 172040 | tf_op jit(solution)/shard_map/ppermute | solution.py:277
  33.7 0.6 %shard_map.113 = bf16[2,8,16,128]{3,2,1,0:T(8,128)(2,1)S(1)} custom-call(bf16[4,10,16,384]{3,2,1,0:T(8,128)(2,1)S(1)} %get-tuple-element.72.t_ref, bf16[9,384,128]{2,1,0:T(8,128)(2,1)S(1)} %get-tuple-element.73.r1_ref), custom_call_target="tpu_custom_call" | custom-call | flops 1200000000 | bytes 4687500 | tf_op jit(solution)/shard_map/pallas_call | solution.py:369
  34.3 0.7 %reshape.41 = bf16[1,2,8,2048]{3,2,1,0:T(8,128)(2,1)} reshape(bf16[2,8,16,128]{3,2,1,0:T(8,128)(2,1)S(1)} %shard_map.113) | data formatting | bytes 131072 | tf_op jit(solution)/shard_map/reshape | solution.py:371
  35.0 1.4 %collective-permute-done.9 = bf16[32,896]{1,0:T(8,128)(2,1)S(1)} collective-permute-done((bf16[32,896]{1,0:T(8,128)(2,1)S(1)}, bf16[32,896]{1,0:T(8,128)(2,1)S(1)}, u32[]{:S(2)}, u32[]{:S(2)}) %collective-permute-start.9) | collective-permute-done | bytes 57376 | tf_op jit(solution)/shard_map/ppermute | solution.py:277
  36.4 0.5 collective-permute-start.12
  36.9 0.0 collective-permute-done.10
  36.9 2.5 %collective-permute-start.11 = (bf16[32,1792]{1,0:T(8,128)(2,1)S(1)}, bf16[32,1792]{1,0:T(8,128)(2,1)S(1)}, u32[]{:S(2)}, u32[]{:S(2)}) collective-permute-start(bf16[32,1792]{1,0:T(8,128)(2,1)S(1)} %add.27), channel_id=1, source_target_pairs={{0,12},{4,8},{8,4},{12,0},{1,13},{5,9},{9,5},{13,1},{2,14},{6,10},... | collective-permute-start | bytes 344072 | tf_op jit(solution)/shard_map/ppermute | solution.py:277
  39.5 1.8 %collective-permute-done.12 = bf16[32,896]{1,0:T(8,128)(2,1)S(1)} collective-permute-done((bf16[32,896]{1,0:T(8,128)(2,1)S(1)}, bf16[32,896]{1,0:T(8,128)(2,1)S(1)}, u32[]{:S(2)}, u32[]{:S(2)}) %collective-permute-start.12) | collective-permute-done | bytes 57376 | tf_op jit(solution)/shard_map/ppermute | solution.py:277
  41.3 3.1 %collective-permute-start.13 = (bf16[32,896]{1,0:T(8,128)(2,1)S(1)}, bf16[32,896]{1,0:T(8,128)(2,1)S(1)}, u32[]{:S(2)}, u32[]{:S(2)}) collective-permute-start(bf16[32,896]{1,0:T(8,128)(2,1)S(1)} %add.30), channel_id=1, source_target_pairs={{0,12},{4,8},{8,4},{12,0},{1,13},{5,9},{9,5},{13,1},{2,14},{6,10},... | collective-permute-start | bytes 172040 | tf_op jit(solution)/shard_map/ppermute | solution.py:277
  44.4 2.9 %collective-permute-done.13 = bf16[32,896]{1,0:T(8,128)(2,1)S(1)} collective-permute-done((bf16[32,896]{1,0:T(8,128)(2,1)S(1)}, bf16[32,896]{1,0:T(8,128)(2,1)S(1)}, u32[]{:S(2)}, u32[]{:S(2)}) %collective-permute-start.13) | collective-permute-done | bytes 57376 | tf_op jit(solution)/shard_map/ppermute | solution.py:277
  47.4 0.0 collective-permute-done.11
  47.5 0.1 collective-permute-start.14
  47.5 1.4 %collective-permute-done.14.h_ref = bf16[32,2688]{1,0:T(8,128)(2,1)S(1)} collective-permute-done((bf16[32,2688]{1,0:T(8,128)(2,1)S(1)}, bf16[32,2688]{1,0:T(8,128)(2,1)S(1)}, u32[]{:S(2)}, u32[]{:S(2)}) %collective-permute-start.14) | collective-permute-done | bytes 172064 | tf_op jit(solution)/shard_map/ppermute | solution.py:277
  48.9 0.9 %shard_map.114 = (f32[64,1728]{1,0:T(8,128)}, f32[1,64]{1,0:T(1,128)}, f32[64,864]{1,0:T(8,128)}, f32[1,64]{1,0:T(1,128)}) custom-call(bf16[32,2688]{1,0:T(8,128)(2,1)S(1)} %pad_maximum_fusion.2.m_ref, bf16[32,2688]{1,0:T(8,128)(2,1)S(1)} %collective-permute-done.14.h_ref), custom_call_target="tpu_custom_call" | custom-call | flops 1200000000 | bytes 4687500 | tf_op jit(solution)/shard_map/pallas_call | solution.py:379
  (12 shorter events, 0.3 us)
Async XLA Ops:
  1.5 8.7 %collective-permute-start.1 = (bf16[2,8,16,128]{3,2,1,0:T(8,128)(2,1)S(1)}, bf16[2,8,16,128]{3,2,1,0:T(8,128)(2,1)S(1)}, u32[]{:S(2)}, u32[]{:S(2)}) collective-permute-start(bf16[2,8,16,128]{3,2,1,0:T(8,128)(2,1)S(1)} %copy.17), channel_id=1, source_target_pairs={{4,8},{8,4},{5,9},{9,5},{6,10},{10,6},{7,11},{11,7},{20,24},{24,20... | collective-permute-start | bytes 196616 | tf_op jit(solution)/shard_map/ppermute | solution.py:283
  2.2 8.2 %collective-permute-start = (bf16[2,8,16,128]{3,2,1,0:T(8,128)(2,1)S(1)}, bf16[2,8,16,128]{3,2,1,0:T(8,128)(2,1)S(1)}, u32[]{:S(2)}, u32[]{:S(2)}) collective-permute-start(bf16[2,8,16,128]{3,2,1,0:T(8,128)(2,1)S(1)} %copy.17), channel_id=1, source_target_pairs={{0,4},{8,12},{4,0},{12,8},{1,5},{9,13},{5,1},{13,9},{2,6},{10,14},... | collective-permute-start | bytes 196616 | tf_op jit(solution)/shard_map/ppermute | solution.py:285
  8.1 2.1 %copy-start = (bf16[1,2,8,4096]{3,2,1,0:T(8,128)(2,1)S(1)}, bf16[1,2,8,4096]{3,2,1,0:T(8,128)(2,1)}, u32[]{:S(2)}) copy-start(bf16[1,2,8,4096]{3,2,1,0:T(8,128)(2,1)} %param.11) | copy-start | bytes 393220
  10.3 1.5 %collective-permute-start.2 = (bf16[6,8,16,128]{3,2,1,0:T(8,128)(2,1)S(1)}, bf16[6,8,16,128]{3,2,1,0:T(8,128)(2,1)S(1)}, u32[]{:S(2)}, u32[]{:S(2)}) collective-permute-start(bf16[6,8,16,128]{3,2,1,0:T(8,128)(2,1)S(1)} %pad_maximum_fusion.1), channel_id=1, source_target_pairs={{0,1},{1,0},{2,3},{3,2},{4,5},{5,4},{6,7},{7,6},{8,9},{9,8},{10,11... | collective-permute-start | bytes 589832 | tf_op jit(solution)/shard_map/ppermute | solution.py:277
  15.0 5.5 %collective-permute-start.4 = (bf16[2,8,16,256]{3,2,1,0:T(8,128)(2,1)S(1)}, bf16[2,8,16,256]{3,2,1,0:T(8,128)(2,1)S(1)}, u32[]{:S(2)}, u32[]{:S(2)}) collective-permute-start(bf16[2,8,16,256]{3,2,1,0:T(8,128)(2,1)S(1)} %get-tuple-element.55.g_ref), channel_id=1, source_target_pairs={{4,8},{8,4},{5,9},{9,5},{6,10},{10,6},{7,11},{11,7},{20,24},{24,20... | collective-permute-start | bytes 393224 | tf_op jit(solution)/shard_map/ppermute | solution.py:283
  15.6 7.3 %collective-permute-start.3 = (bf16[2,8,16,256]{3,2,1,0:T(8,128)(2,1)S(1)}, bf16[2,8,16,256]{3,2,1,0:T(8,128)(2,1)S(1)}, u32[]{:S(2)}, u32[]{:S(2)}) collective-permute-start(bf16[2,8,16,256]{3,2,1,0:T(8,128)(2,1)S(1)} %get-tuple-element.55.g_ref), channel_id=1, source_target_pairs={{0,4},{8,12},{4,0},{12,8},{1,5},{9,13},{5,1},{13,9},{2,6},{10,14},... | collective-permute-start | bytes 393224 | tf_op jit(solution)/shard_map/ppermute | solution.py:285
  22.9 1.3 %collective-permute-start.5 = (bf16[32,1792]{1,0:T(8,128)(2,1)S(1)}, bf16[32,1792]{1,0:T(8,128)(2,1)S(1)}, u32[]{:S(2)}, u32[]{:S(2)}) collective-permute-start(bf16[32,1792]{1,0:T(8,128)(2,1)S(1)} %get-tuple-element.60), channel_id=1, source_target_pairs={{0,1},{1,0},{2,3},{3,2},{4,5},{5,4},{6,7},{7,6},{8,9},{9,8},{10,11... | collective-permute-start | bytes 344072 | tf_op jit(solution)/shard_map/ppermute | solution.py:277
  23.0 2.9 %collective-permute-start.7 = (bf16[6,8,16,256]{3,2,1,0:T(8,128)(2,1)S(1)}, bf16[6,8,16,256]{3,2,1,0:T(8,128)(2,1)S(1)}, u32[]{:S(2)}, u32[]{:S(2)}) collective-permute-start(bf16[6,8,16,256]{3,2,1,0:T(8,128)(2,1)S(1)} %pad_maximum_fusion), channel_id=1, source_target_pairs={{0,1},{1,0},{2,3},{3,2},{4,5},{5,4},{6,7},{7,6},{8,9},{9,8},{10,11... | collective-permute-start | bytes 1179656 | tf_op jit(solution)/shard_map/ppermute | solution.py:277
  24.3 5.3 %collective-permute-start.6 = (bf16[32,1792]{1,0:T(8,128)(2,1)S(1)}, bf16[32,1792]{1,0:T(8,128)(2,1)S(1)}, u32[]{:S(2)}, u32[]{:S(2)}) collective-permute-start(bf16[32,1792]{1,0:T(8,128)(2,1)S(1)} %add_convert_fusion), channel_id=1, source_target_pairs={{0,2},{2,0},{1,3},{3,1},{4,6},{6,4},{5,7},{7,5},{8,10},{10,8},{9,1... | collective-permute-start | bytes 344072 | tf_op jit(solution)/shard_map/ppermute | solution.py:277
  29.6 2.6 %collective-permute-start.8 = (bf16[32,896]{1,0:T(8,128)(2,1)S(1)}, bf16[32,896]{1,0:T(8,128)(2,1)S(1)}, u32[]{:S(2)}, u32[]{:S(2)}) collective-permute-start(bf16[32,896]{1,0:T(8,128)(2,1)S(1)} %get-tuple-element.70), channel_id=1, source_target_pairs={{0,1},{1,0},{2,3},{3,2},{4,5},{5,4},{6,7},{7,6},{8,9},{9,8},{10,11... | collective-permute-start | bytes 172040 | tf_op jit(solution)/shard_map/ppermute | solution.py:277
  30.3 6.6 %collective-permute-start.10 = (bf16[32,1792]{1,0:T(8,128)(2,1)S(1)}, bf16[32,1792]{1,0:T(8,128)(2,1)S(1)}, u32[]{:S(2)}, u32[]{:S(2)}) collective-permute-start(bf16[32,1792]{1,0:T(8,128)(2,1)S(1)} %add.26), channel_id=1, source_target_pairs={{0,4},{4,0},{8,12},{12,8},{1,5},{5,1},{9,13},{13,9},{2,6},{6,2},{1... | collective-permute-start | bytes 344072 | tf_op jit(solution)/shard_map/ppermute | solution.py:277
  32.1 4.2 %collective-permute-start.9 = (bf16[32,896]{1,0:T(8,128)(2,1)S(1)}, bf16[32,896]{1,0:T(8,128)(2,1)S(1)}, u32[]{:S(2)}, u32[]{:S(2)}) collective-permute-start(bf16[32,896]{1,0:T(8,128)(2,1)S(1)} %add_convert_fusion.1), channel_id=1, source_target_pairs={{0,2},{2,0},{1,3},{3,1},{4,6},{6,4},{5,7},{7,5},{8,10},{10,8},{9,1... | collective-permute-start | bytes 172040 | tf_op jit(solution)/shard_map/ppermute | solution.py:277
  36.4 4.9 %collective-permute-start.12 = (bf16[32,896]{1,0:T(8,128)(2,1)S(1)}, bf16[32,896]{1,0:T(8,128)(2,1)S(1)}, u32[]{:S(2)}, u32[]{:S(2)}) collective-permute-start(bf16[32,896]{1,0:T(8,128)(2,1)S(1)} %add.29), channel_id=1, source_target_pairs={{0,4},{4,0},{8,12},{12,8},{1,5},{5,1},{9,13},{13,9},{2,6},{6,2},{1... | collective-permute-start | bytes 172040 | tf_op jit(solution)/shard_map/ppermute | solution.py:277
  36.9 10.5 %collective-permute-start.11 = (bf16[32,1792]{1,0:T(8,128)(2,1)S(1)}, bf16[32,1792]{1,0:T(8,128)(2,1)S(1)}, u32[]{:S(2)}, u32[]{:S(2)}) collective-permute-start(bf16[32,1792]{1,0:T(8,128)(2,1)S(1)} %add.27), channel_id=1, source_target_pairs={{0,12},{4,8},{8,4},{12,0},{1,13},{5,9},{9,5},{13,1},{2,14},{6,10},... | collective-permute-start | bytes 344072 | tf_op jit(solution)/shard_map/ppermute | solution.py:277
  41.3 6.0 %collective-permute-start.13 = (bf16[32,896]{1,0:T(8,128)(2,1)S(1)}, bf16[32,896]{1,0:T(8,128)(2,1)S(1)}, u32[]{:S(2)}, u32[]{:S(2)}) collective-permute-start(bf16[32,896]{1,0:T(8,128)(2,1)S(1)} %add.30), channel_id=1, source_target_pairs={{0,12},{4,8},{8,4},{12,0},{1,13},{5,9},{9,5},{13,1},{2,14},{6,10},... | collective-permute-start | bytes 172040 | tf_op jit(solution)/shard_map/ppermute | solution.py:277
  47.5 1.5 %collective-permute-start.14 = (bf16[32,2688]{1,0:T(8,128)(2,1)S(1)}, bf16[32,2688]{1,0:T(8,128)(2,1)S(1)}, u32[]{:S(2)}, u32[]{:S(2)}) collective-permute-start(bf16[32,2688]{1,0:T(8,128)(2,1)S(1)} %pad_maximum_fusion.2.m_ref), channel_id=1, source_target_pairs={{0,1},{1,0},{2,3},{3,2},{4,5},{5,4},{6,7},{7,6},{8,9},{9,8},{10,11... | collective-permute-start | bytes 516104 | tf_op jit(solution)/shard_map/ppermute | solution.py:277

commit v3 on v2

--- a/solution.py
+++ b/solution.py
@@ -74,8 +74,8 @@
             s1 = s1.astype(BF)
             s2 = s2.astype(BF)
             if 0 <= m < 4:
-                f1_ref[tap, m * C_MID : (m + 1) * C_MID, :] = s1
-                f2_ref[tap, m * C_MID : (m + 1) * C_MID, :] = s2
+                f1_ref[m * C_MID : (m + 1) * C_MID, tap * 256 : (tap + 1) * 256] = s1
+                f2_ref[m * C_MID : (m + 1) * C_MID, tap * 384 : (tap + 1) * 384] = s2
             r1_ref[tap, at : at + C_MID, :] = s1[:, :IN_L]
             r2_ref[tap, at : at + C_MID, :] = s2[:, :MID_L]
 
@@ -104,20 +104,23 @@
         to_ref[x, :, :, lanes:] = edge.astype(BF).reshape(*shape, 128)
 
 
-def gathered(own, even, odd, beside, core, space, width):
-    count, depth = own.shape[0], even.shape[0]
-    end = own.shape[1]
-    head, tail = pl.ds(0, width), pl.ds(end - width, width)
-
-    def near(i):
-        return jnp.where(core == 0, beside[i, head], beside[i, tail])
-
+def gathered(own, side, even, odd, space):
+    count, narrow = own.shape[:2]
+    both = [(even[i], odd[i]) for i in range(even.shape[0])]
     flip = space % 2 == 1
-    one = [(even[i], near(i)) for i in range(depth)]
-    two = [(odd[i], near(depth + count + i)) for i in range(depth)]
-    left = [(jnp.where(flip, p[0], q[0]), jnp.where(flip, p[1], q[1])) for p, q in zip(one, two)]
-    right = [(jnp.where(flip, q[0], p[0]), jnp.where(flip, q[1], p[1])) for p, q in zip(one, two)]
-    return left + [(own[i], near(depth + i)) for i in range(count)] + right
+    left = [jnp.where(flip, one, two) for one, two in both]
+    right = [jnp.where(flip, two, one) for one, two in both]
+    mid = [(own[i], side[i]) for i in range(count)]
+    return [(p[:narrow], p[narrow:]) for p in left] + mid + [(p[:narrow], p[narrow:]) for p in right]
+
+
+def taps(of):
+    parts = [of(*divmod(tap, 3)) for tap in range(9)]
+    return jnp.concatenate([part.reshape(-1, part.shape[-1]) for part in parts], axis=1)
+
+
+def sigmoid(value):
+    return 0.5 * jnp.tanh(0.5 * value) + 0.5
 
 
 def plane_mask(x, rows, space, last, core):
@@ -133,41 +136,32 @@
     return mask * inside
 
 
-def forward_body(x_ref, ev_ref, od_ref, by_ref, f1_ref, f2_ref, b_ref, c_ref, e_ref, a_ref, d_ref, o_ref, g_ref, acc):
+def forward_body(x_ref, by_ref, ev_ref, od_ref, f1_ref, f2_ref, b_ref, c_ref, e_ref, a_ref, d_ref, o_ref, g_ref, n_ref, acc):
     core = lax.axis_index("ysp")
     space = lax.axis_index("space")
     last = lax.axis_size("space") - 1
-    spread(gathered(x_ref, ev_ref, od_ref, by_ref, core, space, 2), core, e_ref, IN_L)
+    spread(gathered(x_ref, by_ref, ev_ref, od_ref, space), core, e_ref, IN_L)
     wide = x_ref.shape[1] + 2
     narrow = wide - 2
-    total = None
-    for tap in range(9):
-        a, b = divmod(tap, 3)
-        part = dot(e_ref[a : a + 4, b : b + wide].reshape(-1, 256), f1_ref[tap], NT)
-        total = part if total is None else total + part
-    acc[...] = total
+    acc[...] = dot(taps(lambda a, b: e_ref[a : a + 4, b : b + wide]), f1_ref[...], NT)
     rows = wide * ROWS
     bias1, bias2 = b_ref[0:1], b_ref[1:2]
     for x in range(4):
         y1 = acc[x * rows : (x + 1) * rows, :] + bias1
         mask = plane_mask(x, rows, space, last, core)
-        sig = jax.nn.sigmoid(y1)
-        d_ref[x] = (sig * (1.0 + y1 * (1.0 - sig)) * mask).reshape(wide, ROWS, MID_L)
+        sig = sigmoid(y1)
+        d_ref[x] = y1.reshape(wide, ROWS, MID_L)
         act = (y1 * sig * mask).astype(BF)
         a_ref[x, :, :, :MID_L] = act.reshape(wide, ROWS, MID_L)
         edge = edges(act.astype(F32), 0, 128)
         a_ref[x, :, :, MID_L:] = edge.astype(BF).reshape(wide, ROWS, 128)
-    total = None
-    for tap in range(9):
-        a, b = divmod(tap, 3)
-        part = dot(a_ref[a : a + 2, b : b + narrow].reshape(-1, 384), f2_ref[tap], NT)
-        total = part if total is None else total + part
-    y2 = total + bias2
-    sig = jax.nn.sigmoid(y2)
+    y2 = dot(taps(lambda a, b: a_ref[a : a + 2, b : b + narrow]), f2_ref[...], NT) + bias2
+    sig = sigmoid(y2)
     shape = o_ref.shape
     o_ref[...] = (y2 * sig).astype(BF).reshape(shape)
     cot = c_ref[...].reshape(-1, MID_L).astype(F32)
     g_ref[...] = (cot * (sig * (1.0 + y2 * (1.0 - sig)))).astype(BF).reshape(shape)
+    n_ref[...] = g_ref[:, pl.ds((1 - core) * (narrow - 2), 2)]
 
 
 def flipped(grads):
@@ -185,7 +179,7 @@
     return total
 
 
-def second_weights_body(a_ref, g_ref, k_ref, s_ref, p_ref):
+def second_weights_body(a_ref, g_ref, y_ref, k_ref, s_ref, d_ref, p_ref):
     turned, bias = flipped(g_ref[...].reshape(-1, MID_L))
     narrow = g_ref.shape[1]
     lane = lax.broadcasted_iota(jnp.int32, (64, 384), 1)
@@ -200,28 +194,32 @@
         else:
             at = (tap - 1) * TAP2
             p_ref[:, at : at + 384] = jnp.where(lane < TAP2, held, pltpu.roll(found, TAP2, 1))
-    halves(p_ref, k_ref, s_ref)
-
-
-def halves(pack, keep_ref, send_ref):
-    core = lax.axis_index("ysp")
-    keep_ref[...] = pack[pl.ds(core * 32, 32), :]
-    send_ref[...] = pack[pl.ds((1 - core) * 32, 32), :].astype(BF)
-
-
-def adjoint(wide_ref, taps_ref, tall, wide):
-    total = None
-    for tap in range(9):
-        a, b = divmod(tap, 3)
-        part = dot(wide_ref[2 - a : 2 - a + tall, 2 - b : 2 - b + wide].reshape(-1, 384), taps_ref[tap], NN)
-        total = part if total is None else total + part
-    return total
-
-
-def backward_body(g_ref, ev_ref, od_ref, by_ref, r2_ref, d_ref, e_ref, k_ref, s_ref, t_ref, wide_g, acc, pack):
+    k_ref[...], s_ref[...] = halves(p_ref, lax.axis_index("dp") % 2)
     core = lax.axis_index("ysp")
     space = lax.axis_index("space")
-    spread(gathered(g_ref, ev_ref, od_ref, by_ref, core, space, 2), core, wide_g, MID_L)
+    last = lax.axis_size("space") - 1
+    rows = y_ref.shape[1] * ROWS
+    for x in range(4):
+        y1 = y_ref[x].reshape(rows, MID_L)
+        sig = sigmoid(y1)
+        slope = sig * (1.0 + y1 * (1.0 - sig)) * plane_mask(x, rows, space, last, core)
+        d_ref[x] = slope.reshape(y_ref.shape[1:])
+
+
+def halves(pack, which):
+    count = pack.shape[0] // 2
+    return pack[pl.ds(which * count, count), :], pack[pl.ds((1 - which) * count, count), :].astype(BF)
+
+
+def adjoint(wide_ref, taps_ref, tall, wide):
+    cells = taps(lambda a, b: wide_ref[2 - a : 2 - a + tall, 2 - b : 2 - b + wide])
+    return dot(cells, taps_ref[...].reshape(9 * 384, -1), NN)
+
+
+def backward_body(g_ref, by_ref, ev_ref, od_ref, r2_ref, d_ref, e_ref, k2_ref, h2_ref, k_ref, s_ref, t_ref, wide_g, acc, pack, pack2):
+    core = lax.axis_index("ysp")
+    space = lax.axis_index("space")
+    spread(gathered(g_ref, by_ref, ev_ref, od_ref, space), core, wide_g, MID_L)
     narrow = g_ref.shape[1]
     wide = narrow + 2
     rows = wide * ROWS
@@ -229,10 +227,8 @@
     for x in range(4):
         slope = d_ref[x].reshape(rows, MID_L)
         g1 = (acc[x * rows : (x + 1) * rows, :] * slope).astype(BF)
-        t_ref[x, :, :, :MID_L] = g1.reshape(wide, ROWS, MID_L)
-        edge = edges(g1.astype(F32), 0, 128)
-        t_ref[x, :, :, MID_L:] = edge.astype(BF).reshape(wide, ROWS, 128)
-    g1 = t_ref[1:3, 1 : 1 + narrow, :, :MID_L].reshape(-1, MID_L)
+        t_ref[x] = g1.reshape(wide, ROWS, MID_L)
+    g1 = t_ref[1:3, 1 : 1 + narrow].reshape(-1, MID_L)
     turned, bias = flipped(g1)
     lane = lax.broadcasted_iota(jnp.int32, (64, 384), 1)
     none = jnp.zeros((64, 128), F32)
@@ -253,23 +249,36 @@
         if slot == 3:
             at = (tap - 3) * TAP1
             pack[:, at : at + 384] = held
-    halves(pack, k_ref, s_ref)
-
-
-def input_grad_body(t_ref, r1_ref, o_ref):
-    o_ref[...] = adjoint(t_ref, r1_ref, *o_ref.shape[:2]).astype(BF).reshape(o_ref.shape)
-
-
-def finish_body(m_ref, h_ref, w2_ref, b2_ref, w1_ref, b1_ref, pack):
+    k_ref[:32], s_ref[:32] = halves(pack, core)
+    pack2[...] = k2_ref[...] + h2_ref[...].astype(F32)
+    keep, send = halves(pack2, core)
+    k_ref[32:48], k_ref[48:] = keep[:, :PACK1], keep[:, PACK1:]
+    s_ref[32:48], s_ref[48:] = send[:, :PACK1], send[:, PACK1:]
+
+
+def input_grad_body(t_ref, r1_ref, o_ref, wide_g):
+    for x in range(t_ref.shape[0]):
+        wide_g[x, :, :, :MID_L] = t_ref[x]
+        edge = edges(t_ref[x].reshape(-1, MID_L).astype(F32), 0, 128)
+        wide_g[x, :, :, MID_L:] = edge.astype(BF).reshape(-1, ROWS, 128)
+    o_ref[...] = adjoint(wide_g, r1_ref, *o_ref.shape[:2]).astype(BF).reshape(o_ref.shape)
+
+
+def finish_body(m_ref, h_ref, w2_ref, b2_ref, w1_ref, b1_ref, pack2, pack1):
     core = lax.axis_index("ysp")
-    pack[pl.ds(core * 32, 32), :] = m_ref[...].astype(F32)
-    pack[pl.ds((1 - core) * 32, 32), :] = h_ref[...].astype(F32)
+    first = lax.axis_index("dp") % 2
+    for ref, of in ((m_ref, core), (h_ref, 1 - core)):
+        for at, half in ((0, first), (32, 1 - first)):
+            rows = pl.ds(half * 32 + of * 16, 16)
+            pack2[rows, :PACK1] = ref[at : at + 16].astype(F32)
+            pack2[rows, PACK1:] = ref[at + 16 : at + 32].astype(F32)
+        pack1[pl.ds(of * 32, 32), :] = ref[64:].astype(F32)
     row = lax.broadcasted_iota(jnp.int32, (64, 64), 0)
     col = lax.broadcasted_iota(jnp.int32, (64, 64), 1)
-    for at, w_ref, b_ref in ((0, w2_ref, b2_ref), (PACK2, w1_ref, b1_ref)):
+    for pack, w_ref, b_ref in ((pack2, w2_ref, b2_ref), (pack1, w1_ref, b1_ref)):
         width = w_ref.shape[1]
-        w_ref[...] = pack[:, at : at + width]
-        spot = jnp.broadcast_to(pack[:, at + width : at + width + 1], (64, 64))
+        w_ref[...] = pack[:, :width]
+        spot = jnp.broadcast_to(pack[:, width : width + 1], (64, 64))
         b_ref[...] = jnp.sum(jnp.where(row == col, spot, 0.0), axis=0, keepdims=True)
 
 
@@ -277,28 +286,22 @@
     return lax.ppermute(cells, axis, [(i, i ^ bit) for i in range(lax.axis_size(axis))])
 
 
-def halo(own, even, odd):
+def halo(own, edge):
+    side = swap(edge, "ysp", 1)
+    cells = jnp.concatenate([own, side], axis=1)
     count = lax.axis_size("space")
     pairs = [(i, i + 1) for i in range(1, count - 1, 2)]
-    odd = lax.ppermute(odd, "space", pairs + [(j, i) for i, j in pairs])
+    odd = lax.ppermute(cells, "space", pairs + [(j, i) for i, j in pairs])
     pairs = [(i, i + 1) for i in range(0, count - 1, 2)]
-    even = lax.ppermute(even, "space", pairs + [(j, i) for i, j in pairs])
-    return even, odd
-
-
-def other_core(own, even, odd):
-    return swap(jnp.concatenate([even, own, odd], axis=0), "ysp", 1)
+    even = lax.ppermute(cells, "space", pairs + [(j, i) for i, j in pairs])
+    return side, even, odd
 
 
 hold = lax.optimization_barrier
 
 
-def first_half(keep, send):
-    return hold((keep + swap(send, "ysp", 1).astype(F32)).astype(BF))
-
-
-def masks(axis):
-    return [(axis, 2 * m - 1) for m in (1, 2, 4, 8, 16, 32, 64) if m < lax.axis_size(axis)]
+def powers(axis, first):
+    return [m for m in (1, 2, 4, 8, 16, 32, 64) if first <= m < lax.axis_size(axis)]
 
 
 def stage(total, axis, mask):
@@ -308,14 +311,15 @@
 def on_device(inputs, w_first, b_first, w_second, b_second, cotangent):
     nx, ny = inputs.shape[1], inputs.shape[2]
     own = inputs.reshape(nx, ny, ROWS, IN_L)
-    even, odd = halo(own, own, own)
+    edge = lax.dynamic_slice_in_dim(own, (1 - lax.axis_index("ysp")) * (ny - 2), 2, axis=1)
+    side, even, odd = halo(own, edge)
     hbm = pl.BlockSpec(memory_space=pltpu.HBM)
     banded = call(
         banded_body,
         2000000000,
         [
-            ((9, 256, 256), BF),
-            ((9, 256, 384), BF),
+            ((256, 9 * 256), BF),
+            ((256, 9 * 384), BF),
             ((9, 384, 256), BF),
             ((9, 384, 128), BF),
             ((2, MID_L), F32),
@@ -331,7 +335,7 @@
     )(*[pltpu.with_memory_space_constraint(v, pltpu.HBM) for v in (w_first.T, w_second.T, b_first.reshape(1, C_MID), b_second.reshape(1, C_MID))])
     cot = cotangent.reshape(nx, ny, ROWS, MID_L)
     even, odd, cot, f1, f2, r2, r1, bias = hold((even, odd, cot, *banded))
-    wide_in, act, slope, out, g2 = call(
+    wide_in, act, y1, out, g2, edge = call(
         forward_body,
         4800000000,
         [
@@ -340,47 +344,59 @@
             ((nx + 2, ny + 2, ROWS, MID_L), F32),
             ((nx, ny, ROWS, MID_L), BF),
             ((nx, ny, ROWS, MID_L), BF),
+            ((nx, 2, ROWS, MID_L), BF),
         ],
         [pltpu.VMEM(((nx + 2) * (ny + 2) * ROWS, MID_L), F32)],
-    )(own, even, odd, other_core(own, even, odd), f1, f2, bias, cot)
-    even, odd = halo(g2, g2, g2)
-    keep2, send2 = call(
-        second_weights_body, 1800000000, [((32, PACK2), F32), ((32, PACK2), BF)], [pltpu.VMEM((64, PACK2), F32)]
-    )(act, g2)
-    *early, final = masks("dp") + masks("space")
-    even, odd, keep2, send2 = hold((even, odd, keep2, send2))
-    sum2 = first_half(keep2, send2)
-    got2 = swap(sum2, *early[0])
-    keep1, send1, wide_g = call(
+    )(own, side, even, odd, f1, f2, bias, cot)
+    side, even, odd = halo(g2, edge)
+    keep2, send2, slope = call(
+        second_weights_body,
+        1800000000,
+        [((32, PACK2), F32), ((32, PACK2), BF), ((nx + 2, ny + 2, ROWS, MID_L), F32)],
+        [pltpu.VMEM((64, PACK2), F32)],
+    )(act, g2, y1)
+    got2 = swap(send2, "dp", 1)
+    even, odd, keep2, got2 = hold((even, odd, keep2, got2))
+    keep, send, g1 = call(
         backward_body,
         5600000000,
-        [((32, PACK1), F32), ((32, PACK1), BF), ((nx + 2, ny + 2, ROWS, 384), BF)],
+        [((64, PACK1), F32), ((64, PACK1), BF), ((nx + 2, ny + 2, ROWS, MID_L), BF)],
         [
             pltpu.VMEM((nx + 4, ny + 4, ROWS, 384), BF),
             pltpu.VMEM(((nx + 2) * (ny + 2) * ROWS, MID_L), F32),
             pltpu.VMEM((64, PACK1), F32),
+            pltpu.VMEM((32, PACK2), F32),
         ],
-    )(g2, even, odd, other_core(g2, even, odd), r2, slope, wide_in)
-    got2, keep1, send1, wide_g = hold((got2, keep1, send1, wide_g))
-    sum2 = hold(sum2 + got2)
-    for axis, mask in early[1:]:
-        sum2 = stage(sum2, axis, mask)
-    sum1 = first_half(keep1, send1)
-    (d_in,) = call(input_grad_body, 1200000000, [((nx, ny, ROWS, IN_L), BF)])(wide_g, r1)
+    )(g2, side, even, odd, r2, slope, wide_in, keep2, got2)
+    total = hold((keep + swap(send, "ysp", 1).astype(F32)).astype(BF))
+    sum1, sum2 = hold((total[:32], total[32:]))
+    (d_in,) = call(
+        input_grad_body,
+        1200000000,
+        [((nx, ny, ROWS, IN_L), BF)],
+        [pltpu.VMEM((nx + 2, ny + 2, ROWS, 384), BF)],
+    )(g1, r1)
     output = out.reshape(1, nx, ny, DEPTH * C_MID)
     input_grad = d_in.reshape(1, nx, ny, DEPTH * C_IN)
-    sum2 = stage(sum2, *final)
-    for at, (axis, mask) in enumerate([*early, final]):
-        got1 = swap(sum1, axis, mask)
-        if at == 0:
-            got1, output, input_grad = hold((got1, output, input_grad))
+    along = [("space", 2 * m - 1) for m in powers("space", 1)]
+    stages1 = [("dp", m) for m in powers("dp", 1)] + along
+    stages2 = [("dp", m) for m in powers("dp", 2)] + along
+    for at, (one, two) in enumerate(zip(stages1, [*stages2, None])):
+        got1 = swap(sum1, *one)
+        got2 = swap(sum2, *two) if two else swap(sum2, "dp", 1)
+        if at == 1:
+            got1, output = hold((got1, output))
+        if at == 1:
+            got1, input_grad = hold((got1, input_grad))
         sum1 = hold(sum1 + got1)
-    total = jnp.concatenate([sum2, sum1], axis=1)
+        if two:
+            sum2 = hold(sum2 + got2)
+    total = jnp.concatenate([sum2, got2, sum1], axis=0)
     gw2, gb2, gw1, gb1 = call(
         finish_body,
         1200000000,
         [((64, W2_L), F32), ((1, 64), F32), ((64, W1_L), F32), ((1, 64), F32)],
-        [pltpu.VMEM((64, PACK2 + PACK1), F32)],
+        [pltpu.VMEM((64, PACK2), F32), pltpu.VMEM((64, PACK1), F32)],
     )(total, swap(total, "ysp", 1))
     return (output, input_grad, gw1.T, gb1.reshape(64), gw2.T, gb2.reshape(64))
 

time: 50.1 us -> 48.9 us (0.976)
  starting transfers between devices: 22.8 us -> 20.5 us
  waiting for transfers between devices: 13.1 us -> 14.9 us
  Pallas kernels: 10.7 us -> 10 us
    ppermute x11, waiting for transfers between devices: 10.5 us -> 14.6 us  [swap(): lax.ppermute(cells, axis, [(i, i ^ bit) for i in range(lax.axis_size(axis...]
    ppermute x4, waiting for transfers between devices: 2.6 us -> 0.36 us  [the longest x2 0.36 us: halo(): even = lax.ppermute(cells, 'space', pairs + [(j, i) for i, j in pairs])]
    ppermute x11, starting transfers between devices: 11.8 us -> 9.67 us  [swap(): lax.ppermute(cells, axis, [(i, i ^ bit) for i in range(lax.axis_size(axis...]
  transfers between devices with their start and end apart: 15 -> 15, of which waited for: 9 -> 11; matrix products, arithmetic and copies ran while one was open for 3% -> 3% of each run, Pallas kernels for 13% -> 8%
where the time goes in v3:
time: 48.9 us; the launch traced here: 48.7 us
  starting transfers between devices  20.5 us (42%)
  waiting for transfers between devices  14.9 us (30%)
  Pallas kernels  10 us (20%)
  local copies, waits for them, and re-layouts  2.31 us (5%)
  between operations  0.79 us (2%)
    ppermute x11, waiting for transfers between devices, swap(): lax.ppermute(cells, axis, [(i, i ^ bit) for i in range(lax.axis_size(axis...  14.6 us
    ppermute x11, starting transfers between devices, swap(): lax.ppermute(cells, axis, [(i, i ^ bit) for i in range(lax.axis_size(axis...  9.67 us
    ppermute x2, starting transfers between devices, halo(): even = lax.ppermute(cells, 'space', pairs + [(j, i) for i, j in pairs])  9.5 us
    pallas_call x1, Pallas kernels, on_device(): call(forward_body, 4800000000, [((nx + 4, ny + 4, ROWS, 256), BF), ((nx +...  2.65 us
    pallas_call x1, Pallas kernels, on_device(): call(backward_body, 5600000000, [((64, PACK1), F32), ((64, PACK1), BF), (...  2.54 us
    pallas_call x1, Pallas kernels, on_device(): call(banded_body, 2000000000, [((256, 9 * 256), BF), ((256, 9 * 384), BF)...  2.08 us
    ppermute x2, starting transfers between devices, halo(): odd = lax.ppermute(cells, 'space', pairs + [(j, i) for i, j in pairs])  1.31 us
    pallas_call x1, Pallas kernels, on_device(): call(second_weights_body, 1800000000, [((32, PACK2), F32), ((32, PACK2),...  1.17 us
  transfers between devices with their start and end apart: 15, of which 11 were waited for; matrix products, arithmetic and copies ran while one was open for 3% of the time, Pallas kernels for 8%

profile of v3, /device:TPU:0, one launch (start us, length us, event | category | flops | bytes accessed | tf_op | source)
XLA Modules:
  0.0 48.7 jit_solution(15791486581629044325)
XLA Ops:
  0.6 0.9 %constant_dynamic-update-slice_fusion.1 = (bf16[2,10,16,128]{3,2,1,0:T(8,128)(2,1)S(1)}, bf16[2,8,16,128]{3,2,1,0:T(8,128)(2,1)S(1)}) fusion(bf16[2,8,16,128]{3,1,2,0:T(8,128)(2,1)} %bitcast.28), kind=kLoop, calls=%fused_computation.5 | loop fusion | bytes 196608
  1.5 0.5 %collective-permute-start = (bf16[2,2,16,128]{3,2,1,0:T(8,128)(2,1)S(1)}, bf16[2,2,16,128]{3,2,1,0:T(8,128)(2,1)S(1)}, u32[]{:S(2)}, u32[]{:S(2)}) collective-permute-start(bf16[2,2,16,128]{3,2,1,0:T(8,128)(2,1)S(1)} %constant_dynamic-slice_fusion), channel_id=1, source_target_pairs={{0,1},{1,0},{2,3},{3,2},{4,5},{5,4},{6,7},{7,6},{8,9},{9,8},{10,11... | collective-permute-start | bytes 49160 | tf_op jit(solution)/shard_map/ppermute | solution.py:286
  2.0 0.8 %collective-permute-done.by_ref = bf16[2,2,16,128]{3,2,1,0:T(8,128)(2,1)S(1)} collective-permute-done((bf16[2,2,16,128]{3,2,1,0:T(8,128)(2,1)S(1)}, bf16[2,2,16,128]{3,2,1,0:T(8,128)(2,1)S(1)}, u32[]{:S(2)}, u32[]{:S(2)}) %collective-permute-start) | collective-permute-done | bytes 16416 | tf_op jit(solution)/shard_map/ppermute | solution.py:286
  2.9 0.7 %collective-permute-start.2 = (bf16[2,10,16,128]{3,2,1,0:T(8,128)(2,1)S(1)}, bf16[2,10,16,128]{3,2,1,0:T(8,128)(2,1)S(1)}, u32[]{:S(2)}, u32[]{:S(2)}) collective-permute-start(bf16[2,10,16,128]{3,2,1,0:T(8,128)(2,1)S(1)} %constant_dynamic-update-slice_fusion), channel_id=1, source_target_pairs={{4,8},{8,4},{5,9},{9,5},{6,10},{10,6},{7,11},{11,7},{20,24},{24,20... | collective-permute-start | bytes 245768 | tf_op jit(solution)/shard_map/ppermute | solution.py:294
  3.5 5.8 %collective-permute-start.1 = (bf16[2,10,16,128]{3,2,1,0:T(8,128)(2,1)S(1)}, bf16[2,10,16,128]{3,2,1,0:T(8,128)(2,1)S(1)}, u32[]{:S(2)}, u32[]{:S(2)}) collective-permute-start(bf16[2,10,16,128]{3,2,1,0:T(8,128)(2,1)S(1)} %constant_dynamic-update-slice_fusion), channel_id=1, source_target_pairs={{0,4},{8,12},{4,0},{12,8},{1,5},{9,13},{5,1},{13,9},{2,6},{10,14},... | collective-permute-start | bytes 245768 | tf_op jit(solution)/shard_map/ppermute | solution.py:296
  9.3 0.0 copy-start
  9.3 2.1 %shard_map.109 = (bf16[256,2304]{1,0:T(8,128)(2,1)S(1)}, bf16[256,3456]{1,0:T(8,128)(2,1)S(1)}, bf16[9,384,256]{2,1,0:T(8,128)(2,1)S(1)}, bf16[9,384,128]{2,1,0:T(8,128)(2,1)S(1)}, f32[2,256]{1,0:T(2,128)S(1)}) custom-call(f32[64,864]{1,0:T(8,128)} %bitcast.30, f32[64,1728]{1,0:T(8,128)} %bitcast.29, f32[1,64]{1,0:T(1,128)} %bitcast.31, f32[1,64]{1,0:T(1,128)} %bitcast.32), custom_call_target="tpu_custom_call" | custom-call | flops 2000000000 | bytes 7812500 | tf_op jit(solution)/shard_map/pallas_call | solution.py:317
  11.4 0.0 copy-done
  11.5 0.0 collective-permute-done.2.od_ref
  11.5 0.4 collective-permute-done.1.ev_ref
  11.8 2.7 %shard_map.110 = (bf16[6,12,16,256]{3,2,1,0:T(8,128)(2,1)S(1)}, bf16[4,10,16,384]{3,2,1,0:T(8,128)(2,1)S(1)}, f32[4,10,16,256]{3,2,1,0:T(8,128)S(1)}, bf16[2,8,1...) custom-call(bf16[2,8,16,128]{3,2,1,0:T(8,128)(2,1)S(1)} %get-tuple-element.87.x_r, ...), custom_call_target="tpu_custom_call" | custom-call | flops 4800000000 | bytes 18750000 | tf_op jit(solution)/shard_map/pallas_call | solution.py:338
  14.5 0.1 collective-permute-start.3
  14.6 1.2 %collective-permute-done.3.by_ref = bf16[2,2,16,256]{3,2,1,0:T(8,128)(2,1)S(1)} collective-permute-done((bf16[2,2,16,256]{3,2,1,0:T(8,128)(2,1)S(1)}, bf16[2,2,16,256]{3,2,1,0:T(8,128)(2,1)S(1)}, u32[]{:S(2)}, u32[]{:S(2)}) %collective-permute-start.3) | collective-permute-done | bytes 32800 | tf_op jit(solution)/shard_map/ppermute | solution.py:286
  15.8 0.7 %collective-permute-start.5 = (bf16[2,10,16,256]{3,2,1,0:T(8,128)(2,1)S(1)}, bf16[2,10,16,256]{3,2,1,0:T(8,128)(2,1)S(1)}, u32[]{:S(2)}, u32[]{:S(2)}) collective-permute-start(bf16[2,10,16,256]{3,2,1,0:T(8,128)(2,1)S(1)} %constant_dynamic-update-slice_fusion.2), channel_id=1, source_target_pairs={{4,8},{8,4},{5,9},{9,5},{6,10},{10,6},{7,11},{11,7},{20,24},{24,20... | collective-permute-start | bytes 491528 | tf_op jit(solution)/shard_map/ppermute | solution.py:294
  16.4 3.7 %collective-permute-start.4 = (bf16[2,10,16,256]{3,2,1,0:T(8,128)(2,1)S(1)}, bf16[2,10,16,256]{3,2,1,0:T(8,128)(2,1)S(1)}, u32[]{:S(2)}, u32[]{:S(2)}) collective-permute-start(bf16[2,10,16,256]{3,2,1,0:T(8,128)(2,1)S(1)} %constant_dynamic-update-slice_fusion.2), channel_id=1, source_target_pairs={{0,4},{8,12},{4,0},{12,8},{1,5},{9,13},{5,1},{13,9},{2,6},{10,14},... | collective-permute-start | bytes 491528 | tf_op jit(solution)/shard_map/ppermute | solution.py:296
  20.1 1.2 %shard_map.111 = (f32[32,1792]{1,0:T(8,128)S(1)}, bf16[32,1792]{1,0:T(8,128)(2,1)S(1)}, f32[4,10,16,256]{3,2,1,0:T(8,128)S(1)}) custom-call(bf16[4,10,16,384]{3,2,1,0:T(8,128)(2,1)S(1)} %get-tuple-element.58.a_ref, bf16[2,8,16,256]{3,2,1,0:T(8,128)(2,1)S(1)} %get-tuple-element.56.g_ref, f32[4,10,16,256]{3,2,1,0:T(8,128)S(1)} %get-tuple-element.59.y_ref), custom_call_target="tpu_custom_call" | custom-call | flops 1800000000 | bytes 7031250 | tf_op jit(solution)/shard_map/pallas_call | solution.py:352
  21.3 1.6 %collective-permute-start.6 = (bf16[32,1792]{1,0:T(8,128)(2,1)S(1)}, bf16[32,1792]{1,0:T(8,128)(2,1)S(1)}, u32[]{:S(2)}, u32[]{:S(2)}) collective-permute-start(bf16[32,1792]{1,0:T(8,128)(2,1)S(1)} %get-tuple-element.61), channel_id=1, source_target_pairs={{0,2},{2,0},{1,3},{3,1},{4,6},{6,4},{5,7},{7,5},{8,10},{10,8},{9,1... | collective-permute-start | bytes 344072 | tf_op jit(solution)/shard_map/ppermute | solution.py:286
  22.9 3.3 %collective-permute-done.6.h2_ref = bf16[32,1792]{1,0:T(8,128)(2,1)S(1)} collective-permute-done((bf16[32,1792]{1,0:T(8,128)(2,1)S(1)}, bf16[32,1792]{1,0:T(8,128)(2,1)S(1)}, u32[]{:S(2)}, u32[]{:S(2)}) %collective-permute-start.6) | collective-permute-done | bytes 114720 | tf_op jit(solution)/shard_map/ppermute | solution.py:286
  26.2 0.0 collective-permute-done.5.od_ref
  26.2 0.0 collective-permute-done.4.ev_ref
  26.2 2.5 %shard_map.112 = (f32[64,896]{1,0:T(8,128)S(1)}, bf16[64,896]{1,0:T(8,128)(2,1)S(1)}, bf16[4,10,16,256]{3,2,1,0:T(8,128)(2,1)S(1)}) custom-call(bf16[2,8,16,256]{3,2,1,0:T(8,128)(2,1)S(1)} %get-tuple-element.56.g_ref, bf16[2,2,16,256]{3,2,1,0:T(8,128)(2,1)S(1)} %collective-permute-done.3.by_ref, bf16[2,10,16,256]{3,2,1,0:T(8,128)(2,1)S(1)} %collective-permute-done.4.ev_ref, ...), custom_call_target="tpu_custom_call" | custom-call | flops 5600000000 | bytes 21875000 | tf_op jit(solution)/shard_map/pallas_call | solution.py:360
  28.7 0.1 collective-permute-start.7
  28.8 1.3 %collective-permute-done.7 = bf16[64,896]{1,0:T(8,128)(2,1)S(1)} collective-permute-done((bf16[64,896]{1,0:T(8,128)(2,1)S(1)}, bf16[64,896]{1,0:T(8,128)(2,1)S(1)}, u32[]{:S(2)}, u32[]{:S(2)}) %collective-permute-start.7) | collective-permute-done | bytes 114720 | tf_op jit(solution)/shard_map/ppermute | solution.py:286
  30.2 1.6 %collective-permute-start.8 = (bf16[32,896]{1,0:T(8,128)(2,1)S(1)}, bf16[32,896]{1,0:T(8,128)(2,1)S(1)}, u32[]{:S(2)}, u32[]{:S(2)}) collective-permute-start(bf16[32,896]{1,0:T(8,128)(2,1)S(1)} %get-tuple-element.71), channel_id=1, source_target_pairs={{0,2},{2,0},{1,3},{3,1},{4,6},{6,4},{5,7},{7,5},{8,10},{10,8},{9,1... | collective-permute-start | bytes 172040 | tf_op jit(solution)/shard_map/ppermute | solution.py:286
  31.7 0.2 collective-permute-start.10
  31.9 0.7 %reshape.40 = bf16[1,2,8,4096]{3,2,1,0:T(8,128)(2,1)} reshape(bf16[2,8,16,256]{3,2,1,0:T(8,128)(2,1)S(1)} %get-tuple-element.72) | data formatting | bytes 262144 | tf_op jit(solution)/shard_map/reshape | solution.py:379
  32.6 1.8 %collective-permute-done.8 = bf16[32,896]{1,0:T(8,128)(2,1)S(1)} collective-permute-done((bf16[32,896]{1,0:T(8,128)(2,1)S(1)}, bf16[32,896]{1,0:T(8,128)(2,1)S(1)}, u32[]{:S(2)}, u32[]{:S(2)}) %collective-permute-start.8) | collective-permute-done | bytes 57376 | tf_op jit(solution)/shard_map/ppermute | solution.py:286
  34.4 0.2 collective-permute-start.9
  34.7 1.3 %collective-permute-done.10 = bf16[32,896]{1,0:T(8,128)(2,1)S(1)} collective-permute-done((bf16[32,896]{1,0:T(8,128)(2,1)S(1)}, bf16[32,896]{1,0:T(8,128)(2,1)S(1)}, u32[]{:S(2)}, u32[]{:S(2)}) %collective-permute-start.10) | collective-permute-done | bytes 57376 | tf_op jit(solution)/shard_map/ppermute | solution.py:286
  35.9 2.5 %collective-permute-start.11 = (bf16[32,896]{1,0:T(8,128)(2,1)S(1)}, bf16[32,896]{1,0:T(8,128)(2,1)S(1)}, u32[]{:S(2)}, u32[]{:S(2)}) collective-permute-start(bf16[32,896]{1,0:T(8,128)(2,1)S(1)} %add.24), channel_id=1, source_target_pairs={{0,12},{4,8},{8,4},{12,0},{1,13},{5,9},{9,5},{13,1},{2,14},{6,10},... | collective-permute-start | bytes 172040 | tf_op jit(solution)/shard_map/ppermute | solution.py:286
  38.5 0.6 %shard_map.113 = bf16[2,8,16,128]{3,2,1,0:T(8,128)(2,1)S(1)} custom-call(bf16[4,10,16,256]{3,2,1,0:T(8,128)(2,1)S(1)} %get-tuple-element.75.t_ref, bf16[9,384,128]{2,1,0:T(8,128)(2,1)S(1)} %get-tuple-element.76.r1_ref), custom_call_target="tpu_custom_call" | custom-call | flops 1200000000 | bytes 4687500 | tf_op jit(solution)/shard_map/pallas_call | solution.py:373
  39.1 0.7 %reshape.41 = bf16[1,2,8,2048]{3,2,1,0:T(8,128)(2,1)} reshape(bf16[2,8,16,128]{3,2,1,0:T(8,128)(2,1)S(1)} %shard_map.113) | data formatting | bytes 131072 | tf_op jit(solution)/shard_map/reshape | solution.py:380
  39.8 0.0 collective-permute-done.9
  39.8 1.4 %collective-permute-start.13 = (bf16[32,896]{1,0:T(8,128)(2,1)S(1)}, bf16[32,896]{1,0:T(8,128)(2,1)S(1)}, u32[]{:S(2)}, u32[]{:S(2)}) collective-permute-start(bf16[32,896]{1,0:T(8,128)(2,1)S(1)} %add.26), channel_id=1, source_target_pairs={{0,12},{4,8},{8,4},{12,0},{1,13},{5,9},{9,5},{13,1},{2,14},{6,10},... | collective-permute-start | bytes 172040 | tf_op jit(solution)/shard_map/ppermute | solution.py:286
  41.2 0.7 %collective-permute-done.11 = bf16[32,896]{1,0:T(8,128)(2,1)S(1)} collective-permute-done((bf16[32,896]{1,0:T(8,128)(2,1)S(1)}, bf16[32,896]{1,0:T(8,128)(2,1)S(1)}, u32[]{:S(2)}, u32[]{:S(2)}) %collective-permute-start.11) | collective-permute-done | bytes 57376 | tf_op jit(solution)/shard_map/ppermute | solution.py:286
  42.0 1.5 %collective-permute-start.12 = (bf16[32,896]{1,0:T(8,128)(2,1)S(1)}, bf16[32,896]{1,0:T(8,128)(2,1)S(1)}, u32[]{:S(2)}, u32[]{:S(2)}) collective-permute-start(bf16[32,896]{1,0:T(8,128)(2,1)S(1)} %add.25), channel_id=1, source_target_pairs={{0,2},{2,0},{1,3},{3,1},{4,6},{6,4},{5,7},{7,5},{8,10},{10,8},{9,1... | collective-permute-start | bytes 172040 | tf_op jit(solution)/shard_map/ppermute | solution.py:286
  43.4 2.4 %collective-permute-done.13 = bf16[32,896]{1,0:T(8,128)(2,1)S(1)} collective-permute-done((bf16[32,896]{1,0:T(8,128)(2,1)S(1)}, bf16[32,896]{1,0:T(8,128)(2,1)S(1)}, u32[]{:S(2)}, u32[]{:S(2)}) %collective-permute-start.13) | collective-permute-done | bytes 57376 | tf_op jit(solution)/shard_map/ppermute | solution.py:286
  45.9 0.4 collective-permute-done.12
  46.3 0.1 collective-permute-start.14
  46.3 1.4 %collective-permute-done.14.h_ref = bf16[96,896]{1,0:T(8,128)(2,1)S(1)} collective-permute-done((bf16[96,896]{1,0:T(8,128)(2,1)S(1)}, bf16[96,896]{1,0:T(8,128)(2,1)S(1)}, u32[]{:S(2)}, u32[]{:S(2)}) %collective-permute-start.14) | collective-permute-done | bytes 172064 | tf_op jit(solution)/shard_map/ppermute | solution.py:286
  47.7 0.9 %shard_map.114 = (f32[64,1728]{1,0:T(8,128)}, f32[1,64]{1,0:T(1,128)}, f32[64,864]{1,0:T(8,128)}, f32[1,64]{1,0:T(1,128)}) custom-call(bf16[96,896]{1,0:T(8,128)(2,1)S(1)} %pad_maximum_fusion.m_ref, bf16[96,896]{1,0:T(8,128)(2,1)S(1)} %collective-permute-done.14.h_ref), custom_call_target="tpu_custom_call" | custom-call | flops 1200000000 | bytes 4687500 | tf_op jit(solution)/shard_map/pallas_call | solution.py:395
  (13 shorter events, 0.2 us)
Async XLA Ops:
  1.5 1.4 %collective-permute-start = (bf16[2,2,16,128]{3,2,1,0:T(8,128)(2,1)S(1)}, bf16[2,2,16,128]{3,2,1,0:T(8,128)(2,1)S(1)}, u32[]{:S(2)}, u32[]{:S(2)}) collective-permute-start(bf16[2,2,16,128]{3,2,1,0:T(8,128)(2,1)S(1)} %constant_dynamic-slice_fusion), channel_id=1, source_target_pairs={{0,1},{1,0},{2,3},{3,2},{4,5},{5,4},{6,7},{7,6},{8,9},{9,8},{10,11... | collective-permute-start | bytes 49160 | tf_op jit(solution)/shard_map/ppermute | solution.py:286
  2.9 8.6 %collective-permute-start.2 = (bf16[2,10,16,128]{3,2,1,0:T(8,128)(2,1)S(1)}, bf16[2,10,16,128]{3,2,1,0:T(8,128)(2,1)S(1)}, u32[]{:S(2)}, u32[]{:S(2)}) collective-permute-start(bf16[2,10,16,128]{3,2,1,0:T(8,128)(2,1)S(1)} %constant_dynamic-update-slice_fusion), channel_id=1, source_target_pairs={{4,8},{8,4},{5,9},{9,5},{6,10},{10,6},{7,11},{11,7},{20,24},{24,20... | collective-permute-start | bytes 245768 | tf_op jit(solution)/shard_map/ppermute | solution.py:294
  3.5 8.3 %collective-permute-start.1 = (bf16[2,10,16,128]{3,2,1,0:T(8,128)(2,1)S(1)}, bf16[2,10,16,128]{3,2,1,0:T(8,128)(2,1)S(1)}, u32[]{:S(2)}, u32[]{:S(2)}) collective-permute-start(bf16[2,10,16,128]{3,2,1,0:T(8,128)(2,1)S(1)} %constant_dynamic-update-slice_fusion), channel_id=1, source_target_pairs={{0,4},{8,12},{4,0},{12,8},{1,5},{9,13},{5,1},{13,9},{2,6},{10,14},... | collective-permute-start | bytes 245768 | tf_op jit(solution)/shard_map/ppermute | solution.py:296
  9.3 2.1 %copy-start = (bf16[1,2,8,4096]{3,2,1,0:T(8,128)(2,1)S(1)}, bf16[1,2,8,4096]{3,2,1,0:T(8,128)(2,1)}, u32[]{:S(2)}) copy-start(bf16[1,2,8,4096]{3,2,1,0:T(8,128)(2,1)} %param.11) | copy-start | bytes 393220
  14.5 1.3 %collective-permute-start.3 = (bf16[2,2,16,256]{3,2,1,0:T(8,128)(2,1)S(1)}, bf16[2,2,16,256]{3,2,1,0:T(8,128)(2,1)S(1)}, u32[]{:S(2)}, u32[]{:S(2)}) collective-permute-start(bf16[2,2,16,256]{3,2,1,0:T(8,128)(2,1)S(1)} %get-tuple-element.57), channel_id=1, source_target_pairs={{0,1},{1,0},{2,3},{3,2},{4,5},{5,4},{6,7},{7,6},{8,9},{9,8},{10,11... | collective-permute-start | bytes 98312 | tf_op jit(solution)/shard_map/ppermute | solution.py:286
  15.8 10.4 %collective-permute-start.5 = (bf16[2,10,16,256]{3,2,1,0:T(8,128)(2,1)S(1)}, bf16[2,10,16,256]{3,2,1,0:T(8,128)(2,1)S(1)}, u32[]{:S(2)}, u32[]{:S(2)}) collective-permute-start(bf16[2,10,16,256]{3,2,1,0:T(8,128)(2,1)S(1)} %constant_dynamic-update-slice_fusion.2), channel_id=1, source_target_pairs={{4,8},{8,4},{5,9},{9,5},{6,10},{10,6},{7,11},{11,7},{20,24},{24,20... | collective-permute-start | bytes 491528 | tf_op jit(solution)/shard_map/ppermute | solution.py:294
  16.4 9.7 %collective-permute-start.4 = (bf16[2,10,16,256]{3,2,1,0:T(8,128)(2,1)S(1)}, bf16[2,10,16,256]{3,2,1,0:T(8,128)(2,1)S(1)}, u32[]{:S(2)}, u32[]{:S(2)}) collective-permute-start(bf16[2,10,16,256]{3,2,1,0:T(8,128)(2,1)S(1)} %constant_dynamic-update-slice_fusion.2), channel_id=1, source_target_pairs={{0,4},{8,12},{4,0},{12,8},{1,5},{9,13},{5,1},{13,9},{2,6},{10,14},... | collective-permute-start | bytes 491528 | tf_op jit(solution)/shard_map/ppermute | solution.py:296
  21.3 4.9 %collective-permute-start.6 = (bf16[32,1792]{1,0:T(8,128)(2,1)S(1)}, bf16[32,1792]{1,0:T(8,128)(2,1)S(1)}, u32[]{:S(2)}, u32[]{:S(2)}) collective-permute-start(bf16[32,1792]{1,0:T(8,128)(2,1)S(1)} %get-tuple-element.61), channel_id=1, source_target_pairs={{0,2},{2,0},{1,3},{3,1},{4,6},{6,4},{5,7},{7,5},{8,10},{10,8},{9,1... | collective-permute-start | bytes 344072 | tf_op jit(solution)/shard_map/ppermute | solution.py:286
  28.7 1.4 %collective-permute-start.7 = (bf16[64,896]{1,0:T(8,128)(2,1)S(1)}, bf16[64,896]{1,0:T(8,128)(2,1)S(1)}, u32[]{:S(2)}, u32[]{:S(2)}) collective-permute-start(bf16[64,896]{1,0:T(8,128)(2,1)S(1)} %get-tuple-element.70), channel_id=1, source_target_pairs={{0,1},{1,0},{2,3},{3,2},{4,5},{5,4},{6,7},{7,6},{8,9},{9,8},{10,11... | collective-permute-start | bytes 344072 | tf_op jit(solution)/shard_map/ppermute | solution.py:286
  30.2 4.2 %collective-permute-start.8 = (bf16[32,896]{1,0:T(8,128)(2,1)S(1)}, bf16[32,896]{1,0:T(8,128)(2,1)S(1)}, u32[]{:S(2)}, u32[]{:S(2)}) collective-permute-start(bf16[32,896]{1,0:T(8,128)(2,1)S(1)} %get-tuple-element.71), channel_id=1, source_target_pairs={{0,2},{2,0},{1,3},{3,1},{4,6},{6,4},{5,7},{7,5},{8,10},{10,8},{9,1... | collective-permute-start | bytes 172040 | tf_op jit(solution)/shard_map/ppermute | solution.py:286
  31.7 4.2 %collective-permute-start.10 = (bf16[32,896]{1,0:T(8,128)(2,1)S(1)}, bf16[32,896]{1,0:T(8,128)(2,1)S(1)}, u32[]{:S(2)}, u32[]{:S(2)}) collective-permute-start(bf16[32,896]{1,0:T(8,128)(2,1)S(1)} %get-tuple-element.78), channel_id=1, source_target_pairs={{0,4},{4,0},{8,12},{12,8},{1,5},{5,1},{9,13},{13,9},{2,6},{6,2},{1... | collective-permute-start | bytes 172040 | tf_op jit(solution)/shard_map/ppermute | solution.py:286
  34.4 5.3 %collective-permute-start.9 = (bf16[32,896]{1,0:T(8,128)(2,1)S(1)}, bf16[32,896]{1,0:T(8,128)(2,1)S(1)}, u32[]{:S(2)}, u32[]{:S(2)}) collective-permute-start(bf16[32,896]{1,0:T(8,128)(2,1)S(1)} %add.23), channel_id=1, source_target_pairs={{0,4},{4,0},{8,12},{12,8},{1,5},{5,1},{9,13},{13,9},{2,6},{6,2},{1... | collective-permute-start | bytes 172040 | tf_op jit(solution)/shard_map/ppermute | solution.py:286
  35.9 6.0 %collective-permute-start.11 = (bf16[32,896]{1,0:T(8,128)(2,1)S(1)}, bf16[32,896]{1,0:T(8,128)(2,1)S(1)}, u32[]{:S(2)}, u32[]{:S(2)}) collective-permute-start(bf16[32,896]{1,0:T(8,128)(2,1)S(1)} %add.24), channel_id=1, source_target_pairs={{0,12},{4,8},{8,4},{12,0},{1,13},{5,9},{9,5},{13,1},{2,14},{6,10},... | collective-permute-start | bytes 172040 | tf_op jit(solution)/shard_map/ppermute | solution.py:286
  39.8 6.0 %collective-permute-start.13 = (bf16[32,896]{1,0:T(8,128)(2,1)S(1)}, bf16[32,896]{1,0:T(8,128)(2,1)S(1)}, u32[]{:S(2)}, u32[]{:S(2)}) collective-permute-start(bf16[32,896]{1,0:T(8,128)(2,1)S(1)} %add.26), channel_id=1, source_target_pairs={{0,12},{4,8},{8,4},{12,0},{1,13},{5,9},{9,5},{13,1},{2,14},{6,10},... | collective-permute-start | bytes 172040 | tf_op jit(solution)/shard_map/ppermute | solution.py:286
  42.0 4.2 %collective-permute-start.12 = (bf16[32,896]{1,0:T(8,128)(2,1)S(1)}, bf16[32,896]{1,0:T(8,128)(2,1)S(1)}, u32[]{:S(2)}, u32[]{:S(2)}) collective-permute-start(bf16[32,896]{1,0:T(8,128)(2,1)S(1)} %add.25), channel_id=1, source_target_pairs={{0,2},{2,0},{1,3},{3,1},{4,6},{6,4},{5,7},{7,5},{8,10},{10,8},{9,1... | collective-permute-start | bytes 172040 | tf_op jit(solution)/shard_map/ppermute | solution.py:286
  46.3 1.5 %collective-permute-start.14 = (bf16[96,896]{1,0:T(8,128)(2,1)S(1)}, bf16[96,896]{1,0:T(8,128)(2,1)S(1)}, u32[]{:S(2)}, u32[]{:S(2)}) collective-permute-start(bf16[96,896]{1,0:T(8,128)(2,1)S(1)} %pad_maximum_fusion.m_ref), channel_id=1, source_target_pairs={{0,1},{1,0},{2,3},{3,2},{4,5},{5,4},{6,7},{7,6},{8,9},{9,8},{10,11... | collective-permute-start | bytes 516104 | tf_op jit(solution)/shard_map/ppermute | solution.py:286

commit v4 on v3

--- a/solution.py
+++ b/solution.py
@@ -10,6 +10,7 @@
 DEPTH = 64
 BF = jnp.bfloat16
 F32 = jnp.float32
+hold = lax.optimization_barrier
 GROUP = 4
 ROWS = DEPTH // GROUP
 IN_L = GROUP * C_IN
@@ -204,6 +205,15 @@
         sig = sigmoid(y1)
         slope = sig * (1.0 + y1 * (1.0 - sig)) * plane_mask(x, rows, space, last, core)
         d_ref[x] = slope.reshape(y_ref.shape[1:])
+
+
+def parity():
+    bits = lax.axis_index("ysp")
+    for axis in ("dp", "space"):
+        at, count = lax.axis_index(axis), lax.axis_size(axis)
+        while count > 1:
+            bits, at, count = bits + at % 2, at // 2, (count + 1) // 2
+    return bits % 2
 
 
 def halves(pack, which):
@@ -249,9 +259,10 @@
         if slot == 3:
             at = (tap - 3) * TAP1
             pack[:, at : at + 384] = held
-    k_ref[:32], s_ref[:32] = halves(pack, core)
+    which = parity()
+    k_ref[:32], s_ref[:32] = halves(pack, which)
     pack2[...] = k2_ref[...] + h2_ref[...].astype(F32)
-    keep, send = halves(pack2, core)
+    keep, send = halves(pack2, which)
     k_ref[32:48], k_ref[48:] = keep[:, :PACK1], keep[:, PACK1:]
     s_ref[32:48], s_ref[48:] = send[:, :PACK1], send[:, PACK1:]
 
@@ -265,9 +276,9 @@
 
 
 def finish_body(m_ref, h_ref, w2_ref, b2_ref, w1_ref, b1_ref, pack2, pack1):
-    core = lax.axis_index("ysp")
+    which = parity()
     first = lax.axis_index("dp") % 2
-    for ref, of in ((m_ref, core), (h_ref, 1 - core)):
+    for ref, of in ((m_ref, which), (h_ref, 1 - which)):
         for at, half in ((0, first), (32, 1 - first)):
             rows = pl.ds(half * 32 + of * 16, 16)
             pack2[rows, :PACK1] = ref[at : at + 16].astype(F32)
@@ -286,26 +297,24 @@
     return lax.ppermute(cells, axis, [(i, i ^ bit) for i in range(lax.axis_size(axis))])
 
 
-def halo(own, edge):
-    side = swap(edge, "ysp", 1)
+def halo(own, edge, *ready):
+    side, *ready = hold((swap(edge, "ysp", 1), *ready))
     cells = jnp.concatenate([own, side], axis=1)
     count = lax.axis_size("space")
     pairs = [(i, i + 1) for i in range(1, count - 1, 2)]
     odd = lax.ppermute(cells, "space", pairs + [(j, i) for i, j in pairs])
     pairs = [(i, i + 1) for i in range(0, count - 1, 2)]
     even = lax.ppermute(cells, "space", pairs + [(j, i) for i, j in pairs])
-    return side, even, odd
-
-
-hold = lax.optimization_barrier
+    return side, even, odd, *ready
 
 
 def powers(axis, first):
     return [m for m in (1, 2, 4, 8, 16, 32, 64) if first <= m < lax.axis_size(axis)]
 
 
-def stage(total, axis, mask):
-    return hold(total + swap(total, axis, mask))
+def cross(cells, axis, bit):
+    pairs = [(2 * i + c, 2 * (i ^ bit) + 1 - c) for i in range(lax.axis_size(axis)) for c in range(2)]
+    return lax.ppermute(cells, (axis, "ysp"), pairs)
 
 
 def on_device(inputs, w_first, b_first, w_second, b_second, cotangent):
@@ -348,14 +357,14 @@
         ],
         [pltpu.VMEM(((nx + 2) * (ny + 2) * ROWS, MID_L), F32)],
     )(own, side, even, odd, f1, f2, bias, cot)
-    side, even, odd = halo(g2, edge)
     keep2, send2, slope = call(
         second_weights_body,
         1800000000,
         [((32, PACK2), F32), ((32, PACK2), BF), ((nx + 2, ny + 2, ROWS, MID_L), F32)],
         [pltpu.VMEM((64, PACK2), F32)],
     )(act, g2, y1)
-    got2 = swap(send2, "dp", 1)
+    side, even, odd, keep2, send2, slope = halo(g2, edge, keep2, send2, slope)
+    got2 = cross(send2, "dp", 1)
     even, odd, keep2, got2 = hold((even, odd, keep2, got2))
     keep, send, g1 = call(
         backward_body,
@@ -378,15 +387,15 @@
     )(g1, r1)
     output = out.reshape(1, nx, ny, DEPTH * C_MID)
     input_grad = d_in.reshape(1, nx, ny, DEPTH * C_IN)
-    along = [("space", 2 * m - 1) for m in powers("space", 1)]
+    along = [("space", m) for m in powers("space", 1)]
     stages1 = [("dp", m) for m in powers("dp", 1)] + along
     stages2 = [("dp", m) for m in powers("dp", 2)] + along
     for at, (one, two) in enumerate(zip(stages1, [*stages2, None])):
-        got1 = swap(sum1, *one)
-        got2 = swap(sum2, *two) if two else swap(sum2, "dp", 1)
-        if at == 1:
+        got1 = cross(sum1, *one)
+        got2 = cross(sum2, *(two or ("dp", 1)))
+        if at == 2:
             got1, output = hold((got1, output))
-        if at == 1:
+        if at == 2:
             got1, input_grad = hold((got1, input_grad))
         sum1 = hold(sum1 + got1)
         if two:

time: 48.9 us -> 47.4 us (0.969)
  waiting for transfers between devices: 14.9 us -> 12.7 us
  starting transfers between devices: 20.5 us -> 21.2 us
    ppermute x11 -> x4, waiting for transfers between devices: 14.6 us -> 3.34 us  [swap(): lax.ppermute(cells, axis, [(i, i ^ bit) for i in range(lax.axis_size(axis...]
    ppermute x0 -> x7, starting transfers between devices: none -> 9.37 us  [cross(): return lax.ppermute(cells, (axis, 'ysp'), pairs)]
    ppermute x0 -> x7, waiting for transfers between devices: none -> 9.05 us  [cross(): return lax.ppermute(cells, (axis, 'ysp'), pairs)]
    ppermute x11 -> x4, starting transfers between devices: 9.67 us -> 0.96 us  [swap(): lax.ppermute(cells, axis, [(i, i ^ bit) for i in range(lax.axis_size(axis...]
where the time goes in v4:
time: 47.4 us; the launch traced here: 47.2 us
  starting transfers between devices  21.2 us (45%)
  waiting for transfers between devices  12.7 us (27%)
  Pallas kernels  10 us (21%)
  local copies, waits for them, and re-layouts  2.3 us (5%)
  between operations  0.79 us (2%)
    ppermute x2, starting transfers between devices, halo(): even = lax.ppermute(cells, 'space', pairs + [(j, i) for i, j in pairs])  9.5 us
    ppermute x7, starting transfers between devices, cross(): return lax.ppermute(cells, (axis, 'ysp'), pairs)  9.37 us
    ppermute x7, waiting for transfers between devices, cross(): return lax.ppermute(cells, (axis, 'ysp'), pairs)  9.05 us
    ppermute x4, waiting for transfers between devices, swap(): lax.ppermute(cells, axis, [(i, i ^ bit) for i in range(lax.axis_size(axis...  3.34 us
    pallas_call x1, Pallas kernels, on_device(): call(forward_body, 4800000000, [((nx + 4, ny + 4, ROWS, 256), BF), ((nx +...  2.65 us
    pallas_call x1, Pallas kernels, on_device(): call(backward_body, 5600000000, [((64, PACK1), F32), ((64, PACK1), BF), (...  2.55 us
    pallas_call x1, Pallas kernels, on_device(): call(banded_body, 2000000000, [((256, 9 * 256), BF), ((256, 9 * 384), BF)...  2.08 us
    ppermute x2, starting transfers between devices, halo(): odd = lax.ppermute(cells, 'space', pairs + [(j, i) for i, j in pairs])  1.34 us
  transfers between devices with their start and end apart: 15, of which 11 were waited for; matrix products, arithmetic and copies ran while one was open for 3% of the time, Pallas kernels for 8%

profile of v4, /device:TPU:0, one launch (start us, length us, event | category | flops | bytes accessed | tf_op | source)
XLA Modules:
  0.0 47.2 jit_solution(17757167708491930165)
XLA Ops:
  0.6 0.9 %copy.17 = bf16[2,8,16,128]{3,2,1,0:T(8,128)(2,1)S(1)} copy(bf16[2,8,16,128]{3,1,2,0:T(8,128)(2,1)} %bitcast.27) | data formatting | bytes 131072
  1.5 0.5 %collective-permute-start = (bf16[2,2,16,128]{3,2,1,0:T(8,128)(2,1)S(1)}, bf16[2,2,16,128]{3,2,1,0:T(8,128)(2,1)S(1)}, u32[]{:S(2)}, u32[]{:S(2)}) collective-permute-start(bf16[2,2,16,128]{3,2,1,0:T(8,128)(2,1)S(1)} %constant_dynamic-slice_fusion), channel_id=1, source_target_pairs={{0,1},{1,0},{2,3},{3,2},{4,5},{5,4},{6,7},{7,6},{8,9},{9,8},{10,11... | collective-permute-start | bytes 49160 | tf_op jit(solution)/shard_map/ppermute | solution.py:297
  2.0 0.8 %collective-permute-done.by_ref = bf16[2,2,16,128]{3,2,1,0:T(8,128)(2,1)S(1)} collective-permute-done((bf16[2,2,16,128]{3,2,1,0:T(8,128)(2,1)S(1)}, bf16[2,2,16,128]{3,2,1,0:T(8,128)(2,1)S(1)}, u32[]{:S(2)}, u32[]{:S(2)}) %collective-permute-start) | collective-permute-done | bytes 16416 | tf_op jit(solution)/shard_map/ppermute | solution.py:297
  2.9 0.7 %collective-permute-start.2 = (bf16[2,10,16,128]{3,2,1,0:T(8,128)(2,1)S(1)}, bf16[2,10,16,128]{3,2,1,0:T(8,128)(2,1)S(1)}, u32[]{:S(2)}, u32[]{:S(2)}) collective-permute-start(bf16[2,10,16,128]{3,2,1,0:T(8,128)(2,1)S(1)} %pad_maximum_fusion.1), channel_id=1, source_target_pairs={{4,8},{8,4},{5,9},{9,5},{6,10},{10,6},{7,11},{11,7},{20,24},{24,20... | collective-permute-start | bytes 245768 | tf_op jit(solution)/shard_map/ppermute | solution.py:305
  3.6 5.8 %collective-permute-start.1 = (bf16[2,10,16,128]{3,2,1,0:T(8,128)(2,1)S(1)}, bf16[2,10,16,128]{3,2,1,0:T(8,128)(2,1)S(1)}, u32[]{:S(2)}, u32[]{:S(2)}) collective-permute-start(bf16[2,10,16,128]{3,2,1,0:T(8,128)(2,1)S(1)} %pad_maximum_fusion.1), channel_id=1, source_target_pairs={{0,4},{8,12},{4,0},{12,8},{1,5},{9,13},{5,1},{13,9},{2,6},{10,14},... | collective-permute-start | bytes 245768 | tf_op jit(solution)/shard_map/ppermute | solution.py:307
  9.4 0.0 copy-start
  9.4 2.1 %shard_map.109 = (bf16[256,2304]{1,0:T(8,128)(2,1)S(1)}, bf16[256,3456]{1,0:T(8,128)(2,1)S(1)}, bf16[9,384,256]{2,1,0:T(8,128)(2,1)S(1)}, bf16[9,384,128]{2,1,0:T(8,128)(2,1)S(1)}, f32[2,256]{1,0:T(2,128)S(1)}) custom-call(f32[64,864]{1,0:T(8,128)} %bitcast.29, f32[64,1728]{1,0:T(8,128)} %bitcast.28, f32[1,64]{1,0:T(1,128)} %bitcast.30, f32[1,64]{1,0:T(1,128)} %bitcast.31), custom_call_target="tpu_custom_call" | custom-call | flops 2000000000 | bytes 7812500 | tf_op jit(solution)/shard_map/pallas_call | solution.py:326
  11.4 0.0 copy-done
  11.5 0.0 collective-permute-done.2.od_ref
  11.5 0.4 collective-permute-done.1.ev_ref
  11.8 2.7 %shard_map.110 = (bf16[6,12,16,256]{3,2,1,0:T(8,128)(2,1)S(1)}, bf16[4,10,16,384]{3,2,1,0:T(8,128)(2,1)S(1)}, f32[4,10,16,256]{3,2,1,0:T(8,128)S(1)}, bf16[2,8,1...) custom-call(bf16[2,8,16,128]{3,2,1,0:T(8,128)(2,1)S(1)} %copy.17, ...), custom_call_target="tpu_custom_call" | custom-call | flops 4800000000 | bytes 18750000 | tf_op jit(solution)/shard_map/pallas_call | solution.py:347
  14.5 0.1 collective-permute-start.3
  14.6 1.2 %shard_map.111 = (f32[32,1792]{1,0:T(8,128)S(1)}, bf16[32,1792]{1,0:T(8,128)(2,1)S(1)}, f32[4,10,16,256]{3,2,1,0:T(8,128)S(1)}) custom-call(bf16[4,10,16,384]{3,2,1,0:T(8,128)(2,1)S(1)} %get-tuple-element.62.a_ref, bf16[2,8,16,256]{3,2,1,0:T(8,128)(2,1)S(1)} %get-tuple-element.60.g_ref, f32[4,10,16,256]{3,2,1,0:T(8,128)S(1)} %get-tuple-element.63.y_ref), custom_call_target="tpu_custom_call" | custom-call | flops 1800000000 | bytes 7031250 | tf_op jit(solution)/shard_map/pallas_call | solution.py:360
  15.8 0.0 collective-permute-done.3.by_ref
  15.8 0.7 %collective-permute-start.5 = (bf16[2,10,16,256]{3,2,1,0:T(8,128)(2,1)S(1)}, bf16[2,10,16,256]{3,2,1,0:T(8,128)(2,1)S(1)}, u32[]{:S(2)}, u32[]{:S(2)}) collective-permute-start(bf16[2,10,16,256]{3,2,1,0:T(8,128)(2,1)S(1)} %constant_dynamic-update-slice_fusion), channel_id=1, source_target_pairs={{4,8},{8,4},{5,9},{9,5},{6,10},{10,6},{7,11},{11,7},{20,24},{24,20... | collective-permute-start | bytes 491528 | tf_op jit(solution)/shard_map/ppermute | solution.py:305
  16.5 3.7 %collective-permute-start.4 = (bf16[2,10,16,256]{3,2,1,0:T(8,128)(2,1)S(1)}, bf16[2,10,16,256]{3,2,1,0:T(8,128)(2,1)S(1)}, u32[]{:S(2)}, u32[]{:S(2)}) collective-permute-start(bf16[2,10,16,256]{3,2,1,0:T(8,128)(2,1)S(1)} %constant_dynamic-update-slice_fusion), channel_id=1, source_target_pairs={{0,4},{8,12},{4,0},{12,8},{1,5},{9,13},{5,1},{13,9},{2,6},{10,14},... | collective-permute-start | bytes 491528 | tf_op jit(solution)/shard_map/ppermute | solution.py:307
  20.2 1.0 %collective-permute-start.6 = (bf16[32,1792]{1,0:T(8,128)(2,1)S(1)}, bf16[32,1792]{1,0:T(8,128)(2,1)S(1)}, u32[]{:S(2)}, u32[]{:S(2)}) collective-permute-start(bf16[32,1792]{1,0:T(8,128)(2,1)S(1)} %get-tuple-element.69), channel_id=1, source_target_pairs={{0,3},{1,2},{2,1},{3,0},{4,7},{5,6},{6,5},{7,4},{8,11},{9,10},{10,... | collective-permute-start | bytes 344072 | tf_op jit(solution)/shard_map/ppermute | solution.py:317
  21.2 4.3 %collective-permute-done.6.h2_ref = bf16[32,1792]{1,0:T(8,128)(2,1)S(1)} collective-permute-done((bf16[32,1792]{1,0:T(8,128)(2,1)S(1)}, bf16[32,1792]{1,0:T(8,128)(2,1)S(1)}, u32[]{:S(2)}, u32[]{:S(2)}) %collective-permute-start.6) | collective-permute-done | bytes 114720 | tf_op jit(solution)/shard_map/ppermute | solution.py:317
  25.5 0.0 collective-permute-done.5.od_ref
  25.5 0.0 collective-permute-done.4.ev_ref
  25.5 2.5 %shard_map.112 = (f32[64,896]{1,0:T(8,128)S(1)}, bf16[64,896]{1,0:T(8,128)(2,1)S(1)}, bf16[4,10,16,256]{3,2,1,0:T(8,128)(2,1)S(1)}) custom-call(bf16[2,8,16,256]{3,2,1,0:T(8,128)(2,1)S(1)} %get-tuple-element.60.g_ref, bf16[2,2,16,256]{3,2,1,0:T(8,128)(2,1)S(1)} %collective-permute-done.3.by_ref, bf16[2,10,16,256]{3,2,1,0:T(8,128)(2,1)S(1)} %collective-permute-done.4.ev_ref, ...), custom_call_target="tpu_custom_call" | custom-call | flops 5600000000 | bytes 21875000 | tf_op jit(solution)/shard_map/pallas_call | solution.py:369
  28.0 0.2 collective-permute-start.7
  28.2 1.2 %collective-permute-done.7 = bf16[64,896]{1,0:T(8,128)(2,1)S(1)} collective-permute-done((bf16[64,896]{1,0:T(8,128)(2,1)S(1)}, bf16[64,896]{1,0:T(8,128)(2,1)S(1)}, u32[]{:S(2)}, u32[]{:S(2)}) %collective-permute-start.7) | collective-permute-done | bytes 114720 | tf_op jit(solution)/shard_map/ppermute | solution.py:297
  29.5 1.3 %collective-permute-start.8 = (bf16[32,896]{1,0:T(8,128)(2,1)S(1)}, bf16[32,896]{1,0:T(8,128)(2,1)S(1)}, u32[]{:S(2)}, u32[]{:S(2)}) collective-permute-start(bf16[32,896]{1,0:T(8,128)(2,1)S(1)} %get-tuple-element.79), channel_id=1, source_target_pairs={{0,3},{1,2},{2,1},{3,0},{4,7},{5,6},{6,5},{7,4},{8,11},{9,10},{10,... | collective-permute-start | bytes 172040 | tf_op jit(solution)/shard_map/ppermute | solution.py:317
  30.8 0.9 %collective-permute-start.11 = (bf16[32,896]{1,0:T(8,128)(2,1)S(1)}, bf16[32,896]{1,0:T(8,128)(2,1)S(1)}, u32[]{:S(2)}, u32[]{:S(2)}) collective-permute-start(bf16[32,896]{1,0:T(8,128)(2,1)S(1)} %get-tuple-element.86), channel_id=1, source_target_pairs={{0,5},{1,4},{4,1},{5,0},{8,13},{9,12},{12,9},{13,8},{2,7},{3,6},{6... | collective-permute-start | bytes 172040 | tf_op jit(solution)/shard_map/ppermute | solution.py:317
  31.8 1.7 %collective-permute-done.8 = bf16[32,896]{1,0:T(8,128)(2,1)S(1)} collective-permute-done((bf16[32,896]{1,0:T(8,128)(2,1)S(1)}, bf16[32,896]{1,0:T(8,128)(2,1)S(1)}, u32[]{:S(2)}, u32[]{:S(2)}) %collective-permute-start.8) | collective-permute-done | bytes 57376 | tf_op jit(solution)/shard_map/ppermute | solution.py:317
  33.5 0.8 %collective-permute-start.9 = (bf16[32,896]{1,0:T(8,128)(2,1)S(1)}, bf16[32,896]{1,0:T(8,128)(2,1)S(1)}, u32[]{:S(2)}, u32[]{:S(2)}) collective-permute-start(bf16[32,896]{1,0:T(8,128)(2,1)S(1)} %add.23), channel_id=1, source_target_pairs={{0,5},{1,4},{4,1},{5,0},{8,13},{9,12},{12,9},{13,8},{2,7},{3,6},{6... | collective-permute-start | bytes 172040 | tf_op jit(solution)/shard_map/ppermute | solution.py:317
  34.3 0.3 collective-permute-done.11
  34.6 1.9 %collective-permute-start.12 = (bf16[32,896]{1,0:T(8,128)(2,1)S(1)}, bf16[32,896]{1,0:T(8,128)(2,1)S(1)}, u32[]{:S(2)}, u32[]{:S(2)}) collective-permute-start(bf16[32,896]{1,0:T(8,128)(2,1)S(1)} %add.25), channel_id=1, source_target_pairs={{0,9},{1,8},{4,13},{5,12},{8,1},{9,0},{12,5},{13,4},{2,11},{3,10},... | collective-permute-start | bytes 172040 | tf_op jit(solution)/shard_map/ppermute | solution.py:317
  36.6 0.7 %reshape.40 = bf16[1,2,8,4096]{3,2,1,0:T(8,128)(2,1)} reshape(bf16[2,8,16,256]{3,2,1,0:T(8,128)(2,1)S(1)} %get-tuple-element.80) | data formatting | bytes 262144 | tf_op jit(solution)/shard_map/reshape | solution.py:388
  37.3 0.1 collective-permute-done.9
  37.4 2.1 %collective-permute-start.10 = (bf16[32,896]{1,0:T(8,128)(2,1)S(1)}, bf16[32,896]{1,0:T(8,128)(2,1)S(1)}, u32[]{:S(2)}, u32[]{:S(2)}) collective-permute-start(bf16[32,896]{1,0:T(8,128)(2,1)S(1)} %add.24), channel_id=1, source_target_pairs={{0,9},{1,8},{4,13},{5,12},{8,1},{9,0},{12,5},{13,4},{2,11},{3,10},... | collective-permute-start | bytes 172040 | tf_op jit(solution)/shard_map/ppermute | solution.py:317
  39.5 1.1 %collective-permute-done.12 = bf16[32,896]{1,0:T(8,128)(2,1)S(1)} collective-permute-done((bf16[32,896]{1,0:T(8,128)(2,1)S(1)}, bf16[32,896]{1,0:T(8,128)(2,1)S(1)}, u32[]{:S(2)}, u32[]{:S(2)}) %collective-permute-start.12) | collective-permute-done | bytes 57376 | tf_op jit(solution)/shard_map/ppermute | solution.py:317
  40.7 1.2 %collective-permute-start.13 = (bf16[32,896]{1,0:T(8,128)(2,1)S(1)}, bf16[32,896]{1,0:T(8,128)(2,1)S(1)}, u32[]{:S(2)}, u32[]{:S(2)}) collective-permute-start(bf16[32,896]{1,0:T(8,128)(2,1)S(1)} %add.26), channel_id=1, source_target_pairs={{0,3},{1,2},{2,1},{3,0},{4,7},{5,6},{6,5},{7,4},{8,11},{9,10},{10,... | collective-permute-start | bytes 172040 | tf_op jit(solution)/shard_map/ppermute | solution.py:317
  41.9 0.6 %shard_map.113 = bf16[2,8,16,128]{3,2,1,0:T(8,128)(2,1)S(1)} custom-call(bf16[4,10,16,256]{3,2,1,0:T(8,128)(2,1)S(1)} %get-tuple-element.83.t_ref, bf16[9,384,128]{2,1,0:T(8,128)(2,1)S(1)} %get-tuple-element.84.r1_ref), custom_call_target="tpu_custom_call" | custom-call | flops 1200000000 | bytes 4687500 | tf_op jit(solution)/shard_map/pallas_call | solution.py:382
  42.5 0.7 %reshape.41 = bf16[1,2,8,2048]{3,2,1,0:T(8,128)(2,1)} reshape(bf16[2,8,16,128]{3,2,1,0:T(8,128)(2,1)S(1)} %shard_map.113) | data formatting | bytes 131072 | tf_op jit(solution)/shard_map/reshape | solution.py:389
  43.2 0.3 collective-permute-done.10
  43.5 1.2 %collective-permute-done.13 = bf16[32,896]{1,0:T(8,128)(2,1)S(1)} collective-permute-done((bf16[32,896]{1,0:T(8,128)(2,1)S(1)}, bf16[32,896]{1,0:T(8,128)(2,1)S(1)}, u32[]{:S(2)}, u32[]{:S(2)}) %collective-permute-start.13) | collective-permute-done | bytes 57376 | tf_op jit(solution)/shard_map/ppermute | solution.py:317
  44.7 0.2 collective-permute-start.14
  44.9 1.3 %collective-permute-done.14.h_ref = bf16[96,896]{1,0:T(8,128)(2,1)S(1)} collective-permute-done((bf16[96,896]{1,0:T(8,128)(2,1)S(1)}, bf16[96,896]{1,0:T(8,128)(2,1)S(1)}, u32[]{:S(2)}, u32[]{:S(2)}) %collective-permute-start.14) | collective-permute-done | bytes 172064 | tf_op jit(solution)/shard_map/ppermute | solution.py:297
  46.2 1.0 %shard_map.114 = (f32[64,1728]{1,0:T(8,128)}, f32[1,64]{1,0:T(1,128)}, f32[64,864]{1,0:T(8,128)}, f32[1,64]{1,0:T(1,128)}) custom-call(bf16[96,896]{1,0:T(8,128)(2,1)S(1)} %pad_maximum_fusion.m_ref, bf16[96,896]{1,0:T(8,128)(2,1)S(1)} %collective-permute-done.14.h_ref), custom_call_target="tpu_custom_call" | custom-call | flops 1200000000 | bytes 4687500 | tf_op jit(solution)/shard_map/pallas_call | solution.py:404
  (13 shorter events, 0.2 us)
Async XLA Ops:
  1.5 1.4 %collective-permute-start = (bf16[2,2,16,128]{3,2,1,0:T(8,128)(2,1)S(1)}, bf16[2,2,16,128]{3,2,1,0:T(8,128)(2,1)S(1)}, u32[]{:S(2)}, u32[]{:S(2)}) collective-permute-start(bf16[2,2,16,128]{3,2,1,0:T(8,128)(2,1)S(1)} %constant_dynamic-slice_fusion), channel_id=1, source_target_pairs={{0,1},{1,0},{2,3},{3,2},{4,5},{5,4},{6,7},{7,6},{8,9},{9,8},{10,11... | collective-permute-start | bytes 49160 | tf_op jit(solution)/shard_map/ppermute | solution.py:297
  2.9 8.6 %collective-permute-start.2 = (bf16[2,10,16,128]{3,2,1,0:T(8,128)(2,1)S(1)}, bf16[2,10,16,128]{3,2,1,0:T(8,128)(2,1)S(1)}, u32[]{:S(2)}, u32[]{:S(2)}) collective-permute-start(bf16[2,10,16,128]{3,2,1,0:T(8,128)(2,1)S(1)} %pad_maximum_fusion.1), channel_id=1, source_target_pairs={{4,8},{8,4},{5,9},{9,5},{6,10},{10,6},{7,11},{11,7},{20,24},{24,20... | collective-permute-start | bytes 245768 | tf_op jit(solution)/shard_map/ppermute | solution.py:305
  3.6 8.3 %collective-permute-start.1 = (bf16[2,10,16,128]{3,2,1,0:T(8,128)(2,1)S(1)}, bf16[2,10,16,128]{3,2,1,0:T(8,128)(2,1)S(1)}, u32[]{:S(2)}, u32[]{:S(2)}) collective-permute-start(bf16[2,10,16,128]{3,2,1,0:T(8,128)(2,1)S(1)} %pad_maximum_fusion.1), channel_id=1, source_target_pairs={{0,4},{8,12},{4,0},{12,8},{1,5},{9,13},{5,1},{13,9},{2,6},{10,14},... | collective-permute-start | bytes 245768 | tf_op jit(solution)/shard_map/ppermute | solution.py:307
  9.4 2.1 %copy-start = (bf16[1,2,8,4096]{3,2,1,0:T(8,128)(2,1)S(1)}, bf16[1,2,8,4096]{3,2,1,0:T(8,128)(2,1)}, u32[]{:S(2)}) copy-start(bf16[1,2,8,4096]{3,2,1,0:T(8,128)(2,1)} %param.11) | copy-start | bytes 393220
  14.5 1.3 %collective-permute-start.3 = (bf16[2,2,16,256]{3,2,1,0:T(8,128)(2,1)S(1)}, bf16[2,2,16,256]{3,2,1,0:T(8,128)(2,1)S(1)}, u32[]{:S(2)}, u32[]{:S(2)}) collective-permute-start(bf16[2,2,16,256]{3,2,1,0:T(8,128)(2,1)S(1)} %get-tuple-element.61), channel_id=1, source_target_pairs={{0,1},{1,0},{2,3},{3,2},{4,5},{5,4},{6,7},{7,6},{8,9},{9,8},{10,11... | collective-permute-start | bytes 98312 | tf_op jit(solution)/shard_map/ppermute | solution.py:297
  15.8 9.7 %collective-permute-start.5 = (bf16[2,10,16,256]{3,2,1,0:T(8,128)(2,1)S(1)}, bf16[2,10,16,256]{3,2,1,0:T(8,128)(2,1)S(1)}, u32[]{:S(2)}, u32[]{:S(2)}) collective-permute-start(bf16[2,10,16,256]{3,2,1,0:T(8,128)(2,1)S(1)} %constant_dynamic-update-slice_fusion), channel_id=1, source_target_pairs={{4,8},{8,4},{5,9},{9,5},{6,10},{10,6},{7,11},{11,7},{20,24},{24,20... | collective-permute-start | bytes 491528 | tf_op jit(solution)/shard_map/ppermute | solution.py:305
  16.5 9.0 %collective-permute-start.4 = (bf16[2,10,16,256]{3,2,1,0:T(8,128)(2,1)S(1)}, bf16[2,10,16,256]{3,2,1,0:T(8,128)(2,1)S(1)}, u32[]{:S(2)}, u32[]{:S(2)}) collective-permute-start(bf16[2,10,16,256]{3,2,1,0:T(8,128)(2,1)S(1)} %constant_dynamic-update-slice_fusion), channel_id=1, source_target_pairs={{0,4},{8,12},{4,0},{12,8},{1,5},{9,13},{5,1},{13,9},{2,6},{10,14},... | collective-permute-start | bytes 491528 | tf_op jit(solution)/shard_map/ppermute | solution.py:307
  20.2 5.3 %collective-permute-start.6 = (bf16[32,1792]{1,0:T(8,128)(2,1)S(1)}, bf16[32,1792]{1,0:T(8,128)(2,1)S(1)}, u32[]{:S(2)}, u32[]{:S(2)}) collective-permute-start(bf16[32,1792]{1,0:T(8,128)(2,1)S(1)} %get-tuple-element.69), channel_id=1, source_target_pairs={{0,3},{1,2},{2,1},{3,0},{4,7},{5,6},{6,5},{7,4},{8,11},{9,10},{10,... | collective-permute-start | bytes 344072 | tf_op jit(solution)/shard_map/ppermute | solution.py:317
  28.0 1.4 %collective-permute-start.7 = (bf16[64,896]{1,0:T(8,128)(2,1)S(1)}, bf16[64,896]{1,0:T(8,128)(2,1)S(1)}, u32[]{:S(2)}, u32[]{:S(2)}) collective-permute-start(bf16[64,896]{1,0:T(8,128)(2,1)S(1)} %get-tuple-element.78), channel_id=1, source_target_pairs={{0,1},{1,0},{2,3},{3,2},{4,5},{5,4},{6,7},{7,6},{8,9},{9,8},{10,11... | collective-permute-start | bytes 344072 | tf_op jit(solution)/shard_map/ppermute | solution.py:297
  29.5 3.9 %collective-permute-start.8 = (bf16[32,896]{1,0:T(8,128)(2,1)S(1)}, bf16[32,896]{1,0:T(8,128)(2,1)S(1)}, u32[]{:S(2)}, u32[]{:S(2)}) collective-permute-start(bf16[32,896]{1,0:T(8,128)(2,1)S(1)} %get-tuple-element.79), channel_id=1, source_target_pairs={{0,3},{1,2},{2,1},{3,0},{4,7},{5,6},{6,5},{7,4},{8,11},{9,10},{10,... | collective-permute-start | bytes 172040 | tf_op jit(solution)/shard_map/ppermute | solution.py:317
  30.8 3.8 %collective-permute-start.11 = (bf16[32,896]{1,0:T(8,128)(2,1)S(1)}, bf16[32,896]{1,0:T(8,128)(2,1)S(1)}, u32[]{:S(2)}, u32[]{:S(2)}) collective-permute-start(bf16[32,896]{1,0:T(8,128)(2,1)S(1)} %get-tuple-element.86), channel_id=1, source_target_pairs={{0,5},{1,4},{4,1},{5,0},{8,13},{9,12},{12,9},{13,8},{2,7},{3,6},{6... | collective-permute-start | bytes 172040 | tf_op jit(solution)/shard_map/ppermute | solution.py:317
  33.5 3.9 %collective-permute-start.9 = (bf16[32,896]{1,0:T(8,128)(2,1)S(1)}, bf16[32,896]{1,0:T(8,128)(2,1)S(1)}, u32[]{:S(2)}, u32[]{:S(2)}) collective-permute-start(bf16[32,896]{1,0:T(8,128)(2,1)S(1)} %add.23), channel_id=1, source_target_pairs={{0,5},{1,4},{4,1},{5,0},{8,13},{9,12},{12,9},{13,8},{2,7},{3,6},{6... | collective-permute-start | bytes 172040 | tf_op jit(solution)/shard_map/ppermute | solution.py:317
  34.6 6.0 %collective-permute-start.12 = (bf16[32,896]{1,0:T(8,128)(2,1)S(1)}, bf16[32,896]{1,0:T(8,128)(2,1)S(1)}, u32[]{:S(2)}, u32[]{:S(2)}) collective-permute-start(bf16[32,896]{1,0:T(8,128)(2,1)S(1)} %add.25), channel_id=1, source_target_pairs={{0,9},{1,8},{4,13},{5,12},{8,1},{9,0},{12,5},{13,4},{2,11},{3,10},... | collective-permute-start | bytes 172040 | tf_op jit(solution)/shard_map/ppermute | solution.py:317
  37.4 6.1 %collective-permute-start.10 = (bf16[32,896]{1,0:T(8,128)(2,1)S(1)}, bf16[32,896]{1,0:T(8,128)(2,1)S(1)}, u32[]{:S(2)}, u32[]{:S(2)}) collective-permute-start(bf16[32,896]{1,0:T(8,128)(2,1)S(1)} %add.24), channel_id=1, source_target_pairs={{0,9},{1,8},{4,13},{5,12},{8,1},{9,0},{12,5},{13,4},{2,11},{3,10},... | collective-permute-start | bytes 172040 | tf_op jit(solution)/shard_map/ppermute | solution.py:317
  40.7 4.0 %collective-permute-start.13 = (bf16[32,896]{1,0:T(8,128)(2,1)S(1)}, bf16[32,896]{1,0:T(8,128)(2,1)S(1)}, u32[]{:S(2)}, u32[]{:S(2)}) collective-permute-start(bf16[32,896]{1,0:T(8,128)(2,1)S(1)} %add.26), channel_id=1, source_target_pairs={{0,3},{1,2},{2,1},{3,0},{4,7},{5,6},{6,5},{7,4},{8,11},{9,10},{10,... | collective-permute-start | bytes 172040 | tf_op jit(solution)/shard_map/ppermute | solution.py:317
  44.7 1.5 %collective-permute-start.14 = (bf16[96,896]{1,0:T(8,128)(2,1)S(1)}, bf16[96,896]{1,0:T(8,128)(2,1)S(1)}, u32[]{:S(2)}, u32[]{:S(2)}) collective-permute-start(bf16[96,896]{1,0:T(8,128)(2,1)S(1)} %pad_maximum_fusion.m_ref), channel_id=1, source_target_pairs={{0,1},{1,0},{2,3},{3,2},{4,5},{5,4},{6,7},{7,6},{8,9},{9,8},{10,11... | collective-permute-start | bytes 516104 | tf_op jit(solution)/shard_map/ppermute | solution.py:297

commit v5 on v4

--- a/solution.py
+++ b/solution.py
@@ -226,19 +226,15 @@
     return dot(cells, taps_ref[...].reshape(9 * 384, -1), NN)
 
 
-def backward_body(g_ref, by_ref, ev_ref, od_ref, r2_ref, d_ref, e_ref, k2_ref, h2_ref, k_ref, s_ref, t_ref, wide_g, acc, pack, pack2):
+def backward_body(g_ref, by_ref, ev_ref, od_ref, r2_ref, d_ref, e_ref, k2_ref, h2_ref, k_ref, s_ref, t_ref, wide_g, pack, pack2):
     core = lax.axis_index("ysp")
     space = lax.axis_index("space")
-    spread(gathered(g_ref, by_ref, ev_ref, od_ref, space), core, wide_g, MID_L)
+    near = gathered(g_ref, by_ref, ev_ref, od_ref, space)[1:5]
+    spread([(middle, jnp.where(core == 0, side[:1], side[1:])) for middle, side in near], core, wide_g, MID_L)
     narrow = g_ref.shape[1]
-    wide = narrow + 2
-    rows = wide * ROWS
-    acc[...] = adjoint(wide_g, r2_ref, 4, wide)
-    for x in range(4):
-        slope = d_ref[x].reshape(rows, MID_L)
-        g1 = (acc[x * rows : (x + 1) * rows, :] * slope).astype(BF)
-        t_ref[x] = g1.reshape(wide, ROWS, MID_L)
-    g1 = t_ref[1:3, 1 : 1 + narrow].reshape(-1, MID_L)
+    slope = d_ref[1:3, 1 : 1 + narrow].reshape(-1, MID_L)
+    g1 = (adjoint(wide_g, r2_ref, 2, narrow) * slope).astype(BF)
+    t_ref[...] = g1.reshape(t_ref.shape)
     turned, bias = flipped(g1)
     lane = lax.broadcasted_iota(jnp.int32, (64, 384), 1)
     none = jnp.zeros((64, 128), F32)
@@ -267,12 +263,37 @@
     s_ref[32:48], s_ref[48:] = send[:, :PACK1], send[:, PACK1:]
 
 
-def input_grad_body(t_ref, r1_ref, o_ref, wide_g):
-    for x in range(t_ref.shape[0]):
-        wide_g[x, :, :, :MID_L] = t_ref[x]
-        edge = edges(t_ref[x].reshape(-1, MID_L).astype(F32), 0, 128)
-        wide_g[x, :, :, MID_L:] = edge.astype(BF).reshape(-1, ROWS, 128)
-    o_ref[...] = adjoint(wide_g, r1_ref, *o_ref.shape[:2]).astype(BF).reshape(o_ref.shape)
+def outer_body(g_ref, by_ref, ev_ref, od_ref, r2_ref, d_ref, t_ref, o_ref, wide_g):
+    core = lax.axis_index("ysp")
+    space = lax.axis_index("space")
+    spread(gathered(g_ref, by_ref, ev_ref, od_ref, space), core, wide_g, MID_L)
+    narrow = g_ref.shape[1]
+    wide = narrow + 2
+    at = (1 - core) * (wide - 1)
+
+    def around(a, b):
+        cols = pl.ds(2 - b, wide)
+        beside = wide_g[3 - a : 5 - a, pl.ds(2 - b + at, 1)]
+        return jnp.concatenate([wide_g[2 - a, cols], wide_g[5 - a, cols], beside[:, 0]], axis=0)
+
+    slope = jnp.concatenate([d_ref[0], d_ref[3], d_ref[1:3, pl.ds(at, 1)][:, 0]], axis=0)
+    g1 = dot(taps(around), r2_ref[...].reshape(9 * 384, -1), NN) * slope.reshape(-1, MID_L)
+    g1 = g1.astype(BF).reshape(-1, ROWS, MID_L)
+    none = jnp.zeros((1, ROWS, MID_L), BF)
+    planes = [g1[:wide], None, None, g1[wide : 2 * wide]]
+    for x in (1, 2):
+        other = g1[2 * wide + x - 1 : 2 * wide + x]
+        low = jnp.where(core == 1, other, none)
+        high = jnp.where(core == 0, other, none)
+        planes[x] = jnp.concatenate([low, t_ref[x - 1], high], axis=0)
+    for x in range(4):
+        o_ref[x, :, :, :MID_L] = planes[x]
+        edge = edges(planes[x].reshape(-1, MID_L).astype(F32), 0, 128)
+        o_ref[x, :, :, MID_L:] = edge.astype(BF).reshape(wide, ROWS, 128)
+
+
+def input_grad_body(t_ref, r1_ref, o_ref):
+    o_ref[...] = adjoint(t_ref, r1_ref, *o_ref.shape[:2]).astype(BF).reshape(o_ref.shape)
 
 
 def finish_body(m_ref, h_ref, w2_ref, b2_ref, w1_ref, b1_ref, pack2, pack1):
@@ -369,30 +390,32 @@
     keep, send, g1 = call(
         backward_body,
         5600000000,
-        [((64, PACK1), F32), ((64, PACK1), BF), ((nx + 2, ny + 2, ROWS, MID_L), BF)],
+        [((64, PACK1), F32), ((64, PACK1), BF), ((nx, ny, ROWS, MID_L), BF)],
         [
-            pltpu.VMEM((nx + 4, ny + 4, ROWS, 384), BF),
-            pltpu.VMEM(((nx + 2) * (ny + 2) * ROWS, MID_L), F32),
+            pltpu.VMEM((nx + 2, ny + 2, ROWS, 384), BF),
             pltpu.VMEM((64, PACK1), F32),
             pltpu.VMEM((32, PACK2), F32),
         ],
     )(g2, side, even, odd, r2, slope, wide_in, keep2, got2)
     total = hold((keep + swap(send, "ysp", 1).astype(F32)).astype(BF))
     sum1, sum2 = hold((total[:32], total[32:]))
-    (d_in,) = call(
-        input_grad_body,
-        1200000000,
-        [((nx, ny, ROWS, IN_L), BF)],
-        [pltpu.VMEM((nx + 2, ny + 2, ROWS, 384), BF)],
-    )(g1, r1)
+    (wide_g,) = call(
+        outer_body,
+        1400000000,
+        [((nx + 2, ny + 2, ROWS, 384), BF)],
+        [pltpu.VMEM((nx + 4, ny + 4, ROWS, 384), BF)],
+    )(g2, side, even, odd, r2, slope, g1)
     output = out.reshape(1, nx, ny, DEPTH * C_MID)
-    input_grad = d_in.reshape(1, nx, ny, DEPTH * C_IN)
     along = [("space", m) for m in powers("space", 1)]
     stages1 = [("dp", m) for m in powers("dp", 1)] + along
     stages2 = [("dp", m) for m in powers("dp", 2)] + along
     for at, (one, two) in enumerate(zip(stages1, [*stages2, None])):
         got1 = cross(sum1, *one)
         got2 = cross(sum2, *(two or ("dp", 1)))
+        if at == 0:
+            got1, wide_g = hold((got1, wide_g))
+            (d_in,) = call(input_grad_body, 1200000000, [((nx, ny, ROWS, IN_L), BF)])(wide_g, r1)
+            input_grad = d_in.reshape(1, nx, ny, DEPTH * C_IN)
         if at == 2:
             got1, output = hold((got1, output))
         if at == 2:

time: 47.4 us -> 46.6 us (0.983)
  waiting for transfers between devices: 12.7 us -> 11.8 us
    pallas_call x1 -> x2, Pallas kernels: 0.62 us -> 1.61 us  [the longest x1 0.99 us: on_device(): call(outer_body, 1400000000, [((nx + 2, ny + 2, ROWS, 384), BF)], [pltpu....]
    ppermute x7, waiting for transfers between devices: 9.05 us -> 8.07 us  [cross(): return lax.ppermute(cells, (axis, 'ysp'), pairs)]
    pallas_call x1, Pallas kernels: 2.55 us -> 1.86 us  [on_device(): call(backward_body, 5600000000, [((64, PACK1), F32), ((64, PACK1), BF), (...]
  transfers between devices with their start and end apart: 15 -> 15, of which waited for: 11 -> 11; matrix products, arithmetic and copies ran while one was open for 3% -> 3% of each run, Pallas kernels for 8% -> 10%
where the time goes in v5:
time: 46.6 us; the launch traced here: 46.4 us
  starting transfers between devices  21.1 us (45%)
  waiting for transfers between devices  11.8 us (25%)
  Pallas kernels  10.3 us (22%)
  local copies, waits for them, and re-layouts  2.3 us (5%)
  between operations  0.8 us (2%)
    ppermute x2, starting transfers between devices, halo(): even = lax.ppermute(cells, 'space', pairs + [(j, i) for i, j in pairs])  9.5 us
    ppermute x7, starting transfers between devices, cross(): return lax.ppermute(cells, (axis, 'ysp'), pairs)  9.33 us
    ppermute x7, waiting for transfers between devices, cross(): return lax.ppermute(cells, (axis, 'ysp'), pairs)  8.07 us
    ppermute x4, waiting for transfers between devices, swap(): lax.ppermute(cells, axis, [(i, i ^ bit) for i in range(lax.axis_size(axis...  3.34 us
    pallas_call x1, Pallas kernels, on_device(): call(forward_body, 4800000000, [((nx + 4, ny + 4, ROWS, 256), BF), ((nx +...  2.65 us
    pallas_call x1, Pallas kernels, on_device(): call(banded_body, 2000000000, [((256, 9 * 256), BF), ((256, 9 * 384), BF)...  2.08 us
    pallas_call x1, Pallas kernels, on_device(): call(backward_body, 5600000000, [((64, PACK1), F32), ((64, PACK1), BF), (...  1.86 us
    ppermute x2, starting transfers between devices, halo(): odd = lax.ppermute(cells, 'space', pairs + [(j, i) for i, j in pairs])  1.34 us
  transfers between devices with their start and end apart: 15, of which 11 were waited for; matrix products, arithmetic and copies ran while one was open for 3% of the time, Pallas kernels for 10%

profile of v5, /device:TPU:0, one launch (start us, length us, event | category | flops | bytes accessed | tf_op | source)
XLA Modules:
  0.0 46.4 jit_solution(17012359803728053662)
XLA Ops:
  0.6 0.9 %copy.17 = bf16[2,8,16,128]{3,2,1,0:T(8,128)(2,1)S(1)} copy(bf16[2,8,16,128]{3,1,2,0:T(8,128)(2,1)} %bitcast.27) | data formatting | bytes 131072
  1.5 0.5 %collective-permute-start = (bf16[2,2,16,128]{3,2,1,0:T(8,128)(2,1)S(1)}, bf16[2,2,16,128]{3,2,1,0:T(8,128)(2,1)S(1)}, u32[]{:S(2)}, u32[]{:S(2)}) collective-permute-start(bf16[2,2,16,128]{3,2,1,0:T(8,128)(2,1)S(1)} %constant_dynamic-slice_fusion), channel_id=1, source_target_pairs={{0,1},{1,0},{2,3},{3,2},{4,5},{5,4},{6,7},{7,6},{8,9},{9,8},{10,11... | collective-permute-start | bytes 49160 | tf_op jit(solution)/shard_map/ppermute | solution.py:318
  2.0 0.8 %collective-permute-done.by_ref = bf16[2,2,16,128]{3,2,1,0:T(8,128)(2,1)S(1)} collective-permute-done((bf16[2,2,16,128]{3,2,1,0:T(8,128)(2,1)S(1)}, bf16[2,2,16,128]{3,2,1,0:T(8,128)(2,1)S(1)}, u32[]{:S(2)}, u32[]{:S(2)}) %collective-permute-start) | collective-permute-done | bytes 16416 | tf_op jit(solution)/shard_map/ppermute | solution.py:318
  2.9 0.7 %collective-permute-start.2 = (bf16[2,10,16,128]{3,2,1,0:T(8,128)(2,1)S(1)}, bf16[2,10,16,128]{3,2,1,0:T(8,128)(2,1)S(1)}, u32[]{:S(2)}, u32[]{:S(2)}) collective-permute-start(bf16[2,10,16,128]{3,2,1,0:T(8,128)(2,1)S(1)} %pad_maximum_fusion.1), channel_id=1, source_target_pairs={{4,8},{8,4},{5,9},{9,5},{6,10},{10,6},{7,11},{11,7},{20,24},{24,20... | collective-permute-start | bytes 245768 | tf_op jit(solution)/shard_map/ppermute | solution.py:326
  3.6 5.8 %collective-permute-start.1 = (bf16[2,10,16,128]{3,2,1,0:T(8,128)(2,1)S(1)}, bf16[2,10,16,128]{3,2,1,0:T(8,128)(2,1)S(1)}, u32[]{:S(2)}, u32[]{:S(2)}) collective-permute-start(bf16[2,10,16,128]{3,2,1,0:T(8,128)(2,1)S(1)} %pad_maximum_fusion.1), channel_id=1, source_target_pairs={{0,4},{8,12},{4,0},{12,8},{1,5},{9,13},{5,1},{13,9},{2,6},{10,14},... | collective-permute-start | bytes 245768 | tf_op jit(solution)/shard_map/ppermute | solution.py:328
  9.4 0.0 copy-start
  9.4 2.1 %shard_map.109 = (bf16[256,2304]{1,0:T(8,128)(2,1)S(1)}, bf16[256,3456]{1,0:T(8,128)(2,1)S(1)}, bf16[9,384,256]{2,1,0:T(8,128)(2,1)S(1)}, bf16[9,384,128]{2,1,0:T(8,128)(2,1)S(1)}, f32[2,256]{1,0:T(2,128)S(1)}) custom-call(f32[64,864]{1,0:T(8,128)} %bitcast.29, f32[64,1728]{1,0:T(8,128)} %bitcast.28, f32[1,64]{1,0:T(1,128)} %bitcast.30, f32[1,64]{1,0:T(1,128)} %bitcast.31), custom_call_target="tpu_custom_call" | custom-call | flops 2000000000 | bytes 7812500 | tf_op jit(solution)/shard_map/pallas_call | solution.py:347
  11.4 0.0 copy-done
  11.5 0.0 collective-permute-done.2.od_ref
  11.5 0.4 collective-permute-done.1.ev_ref
  11.8 2.7 %shard_map.110 = (bf16[6,12,16,256]{3,2,1,0:T(8,128)(2,1)S(1)}, bf16[4,10,16,384]{3,2,1,0:T(8,128)(2,1)S(1)}, f32[4,10,16,256]{3,2,1,0:T(8,128)S(1)}, bf16[2,8,1...) custom-call(bf16[2,8,16,128]{3,2,1,0:T(8,128)(2,1)S(1)} %copy.17, ...), custom_call_target="tpu_custom_call" | custom-call | flops 4800000000 | bytes 18750000 | tf_op jit(solution)/shard_map/pallas_call | solution.py:368
  14.5 0.1 collective-permute-start.3
  14.6 1.2 %shard_map.111 = (f32[32,1792]{1,0:T(8,128)S(1)}, bf16[32,1792]{1,0:T(8,128)(2,1)S(1)}, f32[4,10,16,256]{3,2,1,0:T(8,128)S(1)}) custom-call(bf16[4,10,16,384]{3,2,1,0:T(8,128)(2,1)S(1)} %get-tuple-element.64.a_ref, bf16[2,8,16,256]{3,2,1,0:T(8,128)(2,1)S(1)} %get-tuple-element.62.g_ref, f32[4,10,16,256]{3,2,1,0:T(8,128)S(1)} %get-tuple-element.65.y_ref), custom_call_target="tpu_custom_call" | custom-call | flops 1800000000 | bytes 7031250 | tf_op jit(solution)/shard_map/pallas_call | solution.py:381
  15.8 0.0 collective-permute-done.3.by_ref
  15.8 0.7 %collective-permute-start.5 = (bf16[2,10,16,256]{3,2,1,0:T(8,128)(2,1)S(1)}, bf16[2,10,16,256]{3,2,1,0:T(8,128)(2,1)S(1)}, u32[]{:S(2)}, u32[]{:S(2)}) collective-permute-start(bf16[2,10,16,256]{3,2,1,0:T(8,128)(2,1)S(1)} %constant_dynamic-update-slice_fusion), channel_id=1, source_target_pairs={{4,8},{8,4},{5,9},{9,5},{6,10},{10,6},{7,11},{11,7},{20,24},{24,20... | collective-permute-start | bytes 491528 | tf_op jit(solution)/shard_map/ppermute | solution.py:326
  16.5 3.7 %collective-permute-start.4 = (bf16[2,10,16,256]{3,2,1,0:T(8,128)(2,1)S(1)}, bf16[2,10,16,256]{3,2,1,0:T(8,128)(2,1)S(1)}, u32[]{:S(2)}, u32[]{:S(2)}) collective-permute-start(bf16[2,10,16,256]{3,2,1,0:T(8,128)(2,1)S(1)} %constant_dynamic-update-slice_fusion), channel_id=1, source_target_pairs={{0,4},{8,12},{4,0},{12,8},{1,5},{9,13},{5,1},{13,9},{2,6},{10,14},... | collective-permute-start | bytes 491528 | tf_op jit(solution)/shard_map/ppermute | solution.py:328
  20.2 1.0 %collective-permute-start.6 = (bf16[32,1792]{1,0:T(8,128)(2,1)S(1)}, bf16[32,1792]{1,0:T(8,128)(2,1)S(1)}, u32[]{:S(2)}, u32[]{:S(2)}) collective-permute-start(bf16[32,1792]{1,0:T(8,128)(2,1)S(1)} %get-tuple-element.71), channel_id=1, source_target_pairs={{0,3},{1,2},{2,1},{3,0},{4,7},{5,6},{6,5},{7,4},{8,11},{9,10},{10,... | collective-permute-start | bytes 344072 | tf_op jit(solution)/shard_map/ppermute | solution.py:338
  21.2 4.3 %collective-permute-done.6.h2_ref = bf16[32,1792]{1,0:T(8,128)(2,1)S(1)} collective-permute-done((bf16[32,1792]{1,0:T(8,128)(2,1)S(1)}, bf16[32,1792]{1,0:T(8,128)(2,1)S(1)}, u32[]{:S(2)}, u32[]{:S(2)}) %collective-permute-start.6) | collective-permute-done | bytes 114720 | tf_op jit(solution)/shard_map/ppermute | solution.py:338
  25.5 0.0 collective-permute-done.5.od_ref
  25.5 0.0 collective-permute-done.4.ev_ref
  25.5 1.9 %shard_map.112 = (f32[64,896]{1,0:T(8,128)S(1)}, bf16[64,896]{1,0:T(8,128)(2,1)S(1)}, bf16[2,8,16,256]{3,2,1,0:T(8,128)(2,1)S(1)}) custom-call(bf16[2,8,16,256]{3,2,1,0:T(8,128)(2,1)S(1)} %get-tuple-element.62.g_ref, bf16[2,2,16,256]{3,2,1,0:T(8,128)(2,1)S(1)} %collective-permute-done.3.by_ref, bf16[2,10,16,256]{3,2,1,0:T(8,128)(2,1)S(1)} %collective-permute-done.4.ev_ref, ...), custom_call_target="tpu_custom_call" | custom-call | flops 5600000000 | bytes 21875000 | tf_op jit(solution)/shard_map/pallas_call | solution.py:390
  27.4 0.2 collective-permute-start.7
  27.6 1.2 %collective-permute-done.7 = bf16[64,896]{1,0:T(8,128)(2,1)S(1)} collective-permute-done((bf16[64,896]{1,0:T(8,128)(2,1)S(1)}, bf16[64,896]{1,0:T(8,128)(2,1)S(1)}, u32[]{:S(2)}, u32[]{:S(2)}) %collective-permute-start.7) | collective-permute-done | bytes 114720 | tf_op jit(solution)/shard_map/ppermute | solution.py:318
  28.8 1.3 %collective-permute-start.8 = (bf16[32,896]{1,0:T(8,128)(2,1)S(1)}, bf16[32,896]{1,0:T(8,128)(2,1)S(1)}, u32[]{:S(2)}, u32[]{:S(2)}) collective-permute-start(bf16[32,896]{1,0:T(8,128)(2,1)S(1)} %get-tuple-element.81), channel_id=1, source_target_pairs={{0,3},{1,2},{2,1},{3,0},{4,7},{5,6},{6,5},{7,4},{8,11},{9,10},{10,... | collective-permute-start | bytes 172040 | tf_op jit(solution)/shard_map/ppermute | solution.py:338
  30.1 0.9 %collective-permute-start.11 = (bf16[32,896]{1,0:T(8,128)(2,1)S(1)}, bf16[32,896]{1,0:T(8,128)(2,1)S(1)}, u32[]{:S(2)}, u32[]{:S(2)}) collective-permute-start(bf16[32,896]{1,0:T(8,128)(2,1)S(1)} %get-tuple-element.90), channel_id=1, source_target_pairs={{0,5},{1,4},{4,1},{5,0},{8,13},{9,12},{12,9},{13,8},{2,7},{3,6},{6... | collective-permute-start | bytes 172040 | tf_op jit(solution)/shard_map/ppermute | solution.py:338
  31.1 1.0 %shard_map.113.t_ref = bf16[4,10,16,384]{3,2,1,0:T(8,128)(2,1)S(1)} custom-call(bf16[2,8,16,256]{3,2,1,0:T(8,128)(2,1)S(1)} %get-tuple-element.62.g_ref, bf16[2,2,16,256]{3,2,1,0:T(8,128)(2,1)S(1)} %collective-permute-done.3.by_ref, bf16[2,10,16,256]{3,2,1,0:T(8,128)(2,1)S(1)} %collective-permute-done.4.ev_ref, ...), custom_call_target="tpu_custom_call" | custom-call | flops 1400000000 | bytes 5468750 | tf_op jit(solution)/shard_map/pallas_call | solution.py:402
  32.1 0.7 %collective-permute-done.8 = bf16[32,896]{1,0:T(8,128)(2,1)S(1)} collective-permute-done((bf16[32,896]{1,0:T(8,128)(2,1)S(1)}, bf16[32,896]{1,0:T(8,128)(2,1)S(1)}, u32[]{:S(2)}, u32[]{:S(2)}) %collective-permute-start.8) | collective-permute-done | bytes 57376 | tf_op jit(solution)/shard_map/ppermute | solution.py:338
  32.8 0.8 %collective-permute-start.9 = (bf16[32,896]{1,0:T(8,128)(2,1)S(1)}, bf16[32,896]{1,0:T(8,128)(2,1)S(1)}, u32[]{:S(2)}, u32[]{:S(2)}) collective-permute-start(bf16[32,896]{1,0:T(8,128)(2,1)S(1)} %add.23), channel_id=1, source_target_pairs={{0,5},{1,4},{4,1},{5,0},{8,13},{9,12},{12,9},{13,8},{2,7},{3,6},{6... | collective-permute-start | bytes 172040 | tf_op jit(solution)/shard_map/ppermute | solution.py:338
  33.6 0.3 collective-permute-done.11
  33.9 1.9 %collective-permute-start.12 = (bf16[32,896]{1,0:T(8,128)(2,1)S(1)}, bf16[32,896]{1,0:T(8,128)(2,1)S(1)}, u32[]{:S(2)}, u32[]{:S(2)}) collective-permute-start(bf16[32,896]{1,0:T(8,128)(2,1)S(1)} %add.25), channel_id=1, source_target_pairs={{0,9},{1,8},{4,13},{5,12},{8,1},{9,0},{12,5},{13,4},{2,11},{3,10},... | collective-permute-start | bytes 172040 | tf_op jit(solution)/shard_map/ppermute | solution.py:338
  35.9 0.7 %reshape.40 = bf16[1,2,8,4096]{3,2,1,0:T(8,128)(2,1)} reshape(bf16[2,8,16,256]{3,2,1,0:T(8,128)(2,1)S(1)} %get-tuple-element.84) | data formatting | bytes 262144 | tf_op jit(solution)/shard_map/reshape | solution.py:408
  36.6 0.1 collective-permute-done.9
  36.7 2.1 %collective-permute-start.10 = (bf16[32,896]{1,0:T(8,128)(2,1)S(1)}, bf16[32,896]{1,0:T(8,128)(2,1)S(1)}, u32[]{:S(2)}, u32[]{:S(2)}) collective-permute-start(bf16[32,896]{1,0:T(8,128)(2,1)S(1)} %add.24), channel_id=1, source_target_pairs={{0,9},{1,8},{4,13},{5,12},{8,1},{9,0},{12,5},{13,4},{2,11},{3,10},... | collective-permute-start | bytes 172040 | tf_op jit(solution)/shard_map/ppermute | solution.py:338
  38.9 1.1 %collective-permute-done.12 = bf16[32,896]{1,0:T(8,128)(2,1)S(1)} collective-permute-done((bf16[32,896]{1,0:T(8,128)(2,1)S(1)}, bf16[32,896]{1,0:T(8,128)(2,1)S(1)}, u32[]{:S(2)}, u32[]{:S(2)}) %collective-permute-start.12) | collective-permute-done | bytes 57376 | tf_op jit(solution)/shard_map/ppermute | solution.py:338
  40.0 1.2 %collective-permute-start.13 = (bf16[32,896]{1,0:T(8,128)(2,1)S(1)}, bf16[32,896]{1,0:T(8,128)(2,1)S(1)}, u32[]{:S(2)}, u32[]{:S(2)}) collective-permute-start(bf16[32,896]{1,0:T(8,128)(2,1)S(1)} %add.26), channel_id=1, source_target_pairs={{0,3},{1,2},{2,1},{3,0},{4,7},{5,6},{6,5},{7,4},{8,11},{9,10},{10,... | collective-permute-start | bytes 172040 | tf_op jit(solution)/shard_map/ppermute | solution.py:338
  41.2 0.6 %shard_map.114 = bf16[2,8,16,128]{3,2,1,0:T(8,128)(2,1)S(1)} custom-call(bf16[4,10,16,384]{3,2,1,0:T(8,128)(2,1)S(1)} %shard_map.113.t_ref, bf16[9,384,128]{2,1,0:T(8,128)(2,1)S(1)} %get-tuple-element.88.r1_ref), custom_call_target="tpu_custom_call" | custom-call | flops 1200000000 | bytes 4687500 | tf_op jit(solution)/shard_map/pallas_call | solution.py:417
  41.8 0.7 %reshape.41 = bf16[1,2,8,2048]{3,2,1,0:T(8,128)(2,1)} reshape(bf16[2,8,16,128]{3,2,1,0:T(8,128)(2,1)S(1)} %shard_map.114) | data formatting | bytes 131072 | tf_op jit(solution)/shard_map/reshape | solution.py:418
  42.4 0.4 collective-permute-done.10
  42.8 1.2 %collective-permute-done.13 = bf16[32,896]{1,0:T(8,128)(2,1)S(1)} collective-permute-done((bf16[32,896]{1,0:T(8,128)(2,1)S(1)}, bf16[32,896]{1,0:T(8,128)(2,1)S(1)}, u32[]{:S(2)}, u32[]{:S(2)}) %collective-permute-start.13) | collective-permute-done | bytes 57376 | tf_op jit(solution)/shard_map/ppermute | solution.py:338
  44.0 0.2 collective-permute-start.14
  44.2 1.3 %collective-permute-done.14.h_ref = bf16[96,896]{1,0:T(8,128)(2,1)S(1)} collective-permute-done((bf16[96,896]{1,0:T(8,128)(2,1)S(1)}, bf16[96,896]{1,0:T(8,128)(2,1)S(1)}, u32[]{:S(2)}, u32[]{:S(2)}) %collective-permute-start.14) | collective-permute-done | bytes 172064 | tf_op jit(solution)/shard_map/ppermute | solution.py:318
  45.5 1.0 %shard_map.115 = (f32[64,1728]{1,0:T(8,128)}, f32[1,64]{1,0:T(1,128)}, f32[64,864]{1,0:T(8,128)}, f32[1,64]{1,0:T(1,128)}) custom-call(bf16[96,896]{1,0:T(8,128)(2,1)S(1)} %pad_maximum_fusion.m_ref, bf16[96,896]{1,0:T(8,128)(2,1)S(1)} %collective-permute-done.14.h_ref), custom_call_target="tpu_custom_call" | custom-call | flops 1200000000 | bytes 4687500 | tf_op jit(solution)/shard_map/pallas_call | solution.py:427
  (13 shorter events, 0.2 us)
Async XLA Ops:
  1.5 1.4 %collective-permute-start = (bf16[2,2,16,128]{3,2,1,0:T(8,128)(2,1)S(1)}, bf16[2,2,16,128]{3,2,1,0:T(8,128)(2,1)S(1)}, u32[]{:S(2)}, u32[]{:S(2)}) collective-permute-start(bf16[2,2,16,128]{3,2,1,0:T(8,128)(2,1)S(1)} %constant_dynamic-slice_fusion), channel_id=1, source_target_pairs={{0,1},{1,0},{2,3},{3,2},{4,5},{5,4},{6,7},{7,6},{8,9},{9,8},{10,11... | collective-permute-start | bytes 49160 | tf_op jit(solution)/shard_map/ppermute | solution.py:318
  2.9 8.6 %collective-permute-start.2 = (bf16[2,10,16,128]{3,2,1,0:T(8,128)(2,1)S(1)}, bf16[2,10,16,128]{3,2,1,0:T(8,128)(2,1)S(1)}, u32[]{:S(2)}, u32[]{:S(2)}) collective-permute-start(bf16[2,10,16,128]{3,2,1,0:T(8,128)(2,1)S(1)} %pad_maximum_fusion.1), channel_id=1, source_target_pairs={{4,8},{8,4},{5,9},{9,5},{6,10},{10,6},{7,11},{11,7},{20,24},{24,20... | collective-permute-start | bytes 245768 | tf_op jit(solution)/shard_map/ppermute | solution.py:326
  3.6 8.3 %collective-permute-start.1 = (bf16[2,10,16,128]{3,2,1,0:T(8,128)(2,1)S(1)}, bf16[2,10,16,128]{3,2,1,0:T(8,128)(2,1)S(1)}, u32[]{:S(2)}, u32[]{:S(2)}) collective-permute-start(bf16[2,10,16,128]{3,2,1,0:T(8,128)(2,1)S(1)} %pad_maximum_fusion.1), channel_id=1, source_target_pairs={{0,4},{8,12},{4,0},{12,8},{1,5},{9,13},{5,1},{13,9},{2,6},{10,14},... | collective-permute-start | bytes 245768 | tf_op jit(solution)/shard_map/ppermute | solution.py:328
  9.4 2.1 %copy-start = (bf16[1,2,8,4096]{3,2,1,0:T(8,128)(2,1)S(1)}, bf16[1,2,8,4096]{3,2,1,0:T(8,128)(2,1)}, u32[]{:S(2)}) copy-start(bf16[1,2,8,4096]{3,2,1,0:T(8,128)(2,1)} %param.11) | copy-start | bytes 393220
  14.5 1.3 %collective-permute-start.3 = (bf16[2,2,16,256]{3,2,1,0:T(8,128)(2,1)S(1)}, bf16[2,2,16,256]{3,2,1,0:T(8,128)(2,1)S(1)}, u32[]{:S(2)}, u32[]{:S(2)}) collective-permute-start(bf16[2,2,16,256]{3,2,1,0:T(8,128)(2,1)S(1)} %get-tuple-element.63), channel_id=1, source_target_pairs={{0,1},{1,0},{2,3},{3,2},{4,5},{5,4},{6,7},{7,6},{8,9},{9,8},{10,11... | collective-permute-start | bytes 98312 | tf_op jit(solution)/shard_map/ppermute | solution.py:318
  15.8 9.7 %collective-permute-start.5 = (bf16[2,10,16,256]{3,2,1,0:T(8,128)(2,1)S(1)}, bf16[2,10,16,256]{3,2,1,0:T(8,128)(2,1)S(1)}, u32[]{:S(2)}, u32[]{:S(2)}) collective-permute-start(bf16[2,10,16,256]{3,2,1,0:T(8,128)(2,1)S(1)} %constant_dynamic-update-slice_fusion), channel_id=1, source_target_pairs={{4,8},{8,4},{5,9},{9,5},{6,10},{10,6},{7,11},{11,7},{20,24},{24,20... | collective-permute-start | bytes 491528 | tf_op jit(solution)/shard_map/ppermute | solution.py:326
  16.5 9.0 %collective-permute-start.4 = (bf16[2,10,16,256]{3,2,1,0:T(8,128)(2,1)S(1)}, bf16[2,10,16,256]{3,2,1,0:T(8,128)(2,1)S(1)}, u32[]{:S(2)}, u32[]{:S(2)}) collective-permute-start(bf16[2,10,16,256]{3,2,1,0:T(8,128)(2,1)S(1)} %constant_dynamic-update-slice_fusion), channel_id=1, source_target_pairs={{0,4},{8,12},{4,0},{12,8},{1,5},{9,13},{5,1},{13,9},{2,6},{10,14},... | collective-permute-start | bytes 491528 | tf_op jit(solution)/shard_map/ppermute | solution.py:328
  20.2 5.3 %collective-permute-start.6 = (bf16[32,1792]{1,0:T(8,128)(2,1)S(1)}, bf16[32,1792]{1,0:T(8,128)(2,1)S(1)}, u32[]{:S(2)}, u32[]{:S(2)}) collective-permute-start(bf16[32,1792]{1,0:T(8,128)(2,1)S(1)} %get-tuple-element.71), channel_id=1, source_target_pairs={{0,3},{1,2},{2,1},{3,0},{4,7},{5,6},{6,5},{7,4},{8,11},{9,10},{10,... | collective-permute-start | bytes 344072 | tf_op jit(solution)/shard_map/ppermute | solution.py:338
  27.4 1.4 %collective-permute-start.7 = (bf16[64,896]{1,0:T(8,128)(2,1)S(1)}, bf16[64,896]{1,0:T(8,128)(2,1)S(1)}, u32[]{:S(2)}, u32[]{:S(2)}) collective-permute-start(bf16[64,896]{1,0:T(8,128)(2,1)S(1)} %get-tuple-element.80), channel_id=1, source_target_pairs={{0,1},{1,0},{2,3},{3,2},{4,5},{5,4},{6,7},{7,6},{8,9},{9,8},{10,11... | collective-permute-start | bytes 344072 | tf_op jit(solution)/shard_map/ppermute | solution.py:318
  28.8 3.9 %collective-permute-start.8 = (bf16[32,896]{1,0:T(8,128)(2,1)S(1)}, bf16[32,896]{1,0:T(8,128)(2,1)S(1)}, u32[]{:S(2)}, u32[]{:S(2)}) collective-permute-start(bf16[32,896]{1,0:T(8,128)(2,1)S(1)} %get-tuple-element.81), channel_id=1, source_target_pairs={{0,3},{1,2},{2,1},{3,0},{4,7},{5,6},{6,5},{7,4},{8,11},{9,10},{10,... | collective-permute-start | bytes 172040 | tf_op jit(solution)/shard_map/ppermute | solution.py:338
  30.1 3.8 %collective-permute-start.11 = (bf16[32,896]{1,0:T(8,128)(2,1)S(1)}, bf16[32,896]{1,0:T(8,128)(2,1)S(1)}, u32[]{:S(2)}, u32[]{:S(2)}) collective-permute-start(bf16[32,896]{1,0:T(8,128)(2,1)S(1)} %get-tuple-element.90), channel_id=1, source_target_pairs={{0,5},{1,4},{4,1},{5,0},{8,13},{9,12},{12,9},{13,8},{2,7},{3,6},{6... | collective-permute-start | bytes 172040 | tf_op jit(solution)/shard_map/ppermute | solution.py:338
  32.8 3.9 %collective-permute-start.9 = (bf16[32,896]{1,0:T(8,128)(2,1)S(1)}, bf16[32,896]{1,0:T(8,128)(2,1)S(1)}, u32[]{:S(2)}, u32[]{:S(2)}) collective-permute-start(bf16[32,896]{1,0:T(8,128)(2,1)S(1)} %add.23), channel_id=1, source_target_pairs={{0,5},{1,4},{4,1},{5,0},{8,13},{9,12},{12,9},{13,8},{2,7},{3,6},{6... | collective-permute-start | bytes 172040 | tf_op jit(solution)/shard_map/ppermute | solution.py:338
  33.9 6.0 %collective-permute-start.12 = (bf16[32,896]{1,0:T(8,128)(2,1)S(1)}, bf16[32,896]{1,0:T(8,128)(2,1)S(1)}, u32[]{:S(2)}, u32[]{:S(2)}) collective-permute-start(bf16[32,896]{1,0:T(8,128)(2,1)S(1)} %add.25), channel_id=1, source_target_pairs={{0,9},{1,8},{4,13},{5,12},{8,1},{9,0},{12,5},{13,4},{2,11},{3,10},... | collective-permute-start | bytes 172040 | tf_op jit(solution)/shard_map/ppermute | solution.py:338
  36.7 6.1 %collective-permute-start.10 = (bf16[32,896]{1,0:T(8,128)(2,1)S(1)}, bf16[32,896]{1,0:T(8,128)(2,1)S(1)}, u32[]{:S(2)}, u32[]{:S(2)}) collective-permute-start(bf16[32,896]{1,0:T(8,128)(2,1)S(1)} %add.24), channel_id=1, source_target_pairs={{0,9},{1,8},{4,13},{5,12},{8,1},{9,0},{12,5},{13,4},{2,11},{3,10},... | collective-permute-start | bytes 172040 | tf_op jit(solution)/shard_map/ppermute | solution.py:338
  40.0 4.0 %collective-permute-start.13 = (bf16[32,896]{1,0:T(8,128)(2,1)S(1)}, bf16[32,896]{1,0:T(8,128)(2,1)S(1)}, u32[]{:S(2)}, u32[]{:S(2)}) collective-permute-start(bf16[32,896]{1,0:T(8,128)(2,1)S(1)} %add.26), channel_id=1, source_target_pairs={{0,3},{1,2},{2,1},{3,0},{4,7},{5,6},{6,5},{7,4},{8,11},{9,10},{10,... | collective-permute-start | bytes 172040 | tf_op jit(solution)/shard_map/ppermute | solution.py:338
  44.0 1.5 %collective-permute-start.14 = (bf16[96,896]{1,0:T(8,128)(2,1)S(1)}, bf16[96,896]{1,0:T(8,128)(2,1)S(1)}, u32[]{:S(2)}, u32[]{:S(2)}) collective-permute-start(bf16[96,896]{1,0:T(8,128)(2,1)S(1)} %pad_maximum_fusion.m_ref), channel_id=1, source_target_pairs={{0,1},{1,0},{2,3},{3,2},{4,5},{5,4},{6,7},{7,6},{8,9},{9,8},{10,11... | collective-permute-start | bytes 516104 | tf_op jit(solution)/shard_map/ppermute | solution.py:318

commit v6 on v5

--- a/solution.py
+++ b/solution.py
@@ -318,14 +318,17 @@
     return lax.ppermute(cells, axis, [(i, i ^ bit) for i in range(lax.axis_size(axis))])
 
 
+def pair_swap(cells, first):
+    count = lax.axis_size("space")
+    pairs = [(i, i + 1) for i in range(first, count - 1, 2)]
+    return lax.ppermute(cells, "space", pairs + [(j, i) for i, j in pairs])
+
+
 def halo(own, edge, *ready):
     side, *ready = hold((swap(edge, "ysp", 1), *ready))
     cells = jnp.concatenate([own, side], axis=1)
-    count = lax.axis_size("space")
-    pairs = [(i, i + 1) for i in range(1, count - 1, 2)]
-    odd = lax.ppermute(cells, "space", pairs + [(j, i) for i, j in pairs])
-    pairs = [(i, i + 1) for i in range(0, count - 1, 2)]
-    even = lax.ppermute(cells, "space", pairs + [(j, i) for i, j in pairs])
+    even = pair_swap(cells, 0)
+    odd = pair_swap(cells, 1)
     return side, even, odd, *ready
 
 
@@ -364,7 +367,7 @@
         in_specs=[hbm] * 4,
     )(*[pltpu.with_memory_space_constraint(v, pltpu.HBM) for v in (w_first.T, w_second.T, b_first.reshape(1, C_MID), b_second.reshape(1, C_MID))])
     cot = cotangent.reshape(nx, ny, ROWS, MID_L)
-    even, odd, cot, f1, f2, r2, r1, bias = hold((even, odd, cot, *banded))
+    odd, even, cot, f1, f2, r2, r1, bias = hold((odd, even, cot, *banded))
     wide_in, act, y1, out, g2, edge = call(
         forward_body,
         4800000000,
@@ -386,7 +389,7 @@
     )(act, g2, y1)
     side, even, odd, keep2, send2, slope = halo(g2, edge, keep2, send2, slope)
     got2 = cross(send2, "dp", 1)
-    even, odd, keep2, got2 = hold((even, odd, keep2, got2))
+    odd, even, keep2, got2 = hold((odd, even, keep2, got2))
     keep, send, g1 = call(
         backward_body,
         5600000000,

time: 46.6 us -> 45.8 us (0.983)
  waiting for transfers between devices: 11.8 us -> 7.64 us
  starting transfers between devices: 21.1 us -> 24.4 us
    ppermute x7, starting transfers between devices: 9.33 us -> 14.2 us  [cross(): return lax.ppermute(cells, (axis, 'ysp'), pairs)]
    ppermute x7, waiting for transfers between devices: 8.07 us -> 4.52 us  [cross(): return lax.ppermute(cells, (axis, 'ysp'), pairs)]
    ppermute x4, starting transfers between devices: 10.8 us -> 9.06 us  [pair_swap(): return lax.ppermute(cells, 'space', pairs + [(j, i) for i, j in pairs])]
  transfers between devices with their start and end apart: 15 -> 15, of which waited for: 11 -> 5; matrix products, arithmetic and copies ran while one was open for 3% -> 3% of each run, Pallas kernels for 10% -> 11%
where the time goes in v6:
time: 45.8 us; the launch traced here: 45.6 us
  starting transfers between devices  24.4 us (53%)
  Pallas kernels  10.3 us (22%)
  waiting for transfers between devices  7.64 us (17%)
  local copies, waits for them, and re-layouts  2.3 us (5%)
  between operations  0.82 us (2%)
    ppermute x7, starting transfers between devices, cross(): return lax.ppermute(cells, (axis, 'ysp'), pairs)  14.2 us
    ppermute x4, starting transfers between devices, pair_swap(): return lax.ppermute(cells, 'space', pairs + [(j, i) for i, j in pairs])  9.06 us
    ppermute x7, waiting for transfers between devices, cross(): return lax.ppermute(cells, (axis, 'ysp'), pairs)  4.52 us
    ppermute x4, waiting for transfers between devices, swap(): lax.ppermute(cells, axis, [(i, i ^ bit) for i in range(lax.axis_size(axis...  3.11 us
    pallas_call x1, Pallas kernels, on_device(): call(forward_body, 4800000000, [((nx + 4, ny + 4, ROWS, 256), BF), ((nx +...  2.66 us
    pallas_call x1, Pallas kernels, on_device(): call(banded_body, 2000000000, [((256, 9 * 256), BF), ((256, 9 * 384), BF)...  2.08 us
    pallas_call x1, Pallas kernels, on_device(): call(backward_body, 5600000000, [((64, PACK1), F32), ((64, PACK1), BF), (...  1.86 us
    ppermute x4, starting transfers between devices, swap(): lax.ppermute(cells, axis, [(i, i ^ bit) for i in range(lax.axis_size(axis...  1.2 us
  transfers between devices with their start and end apart: 15, of which 5 were waited for; matrix products, arithmetic and copies ran while one was open for 3% of the time, Pallas kernels for 11%

profile of v6, /device:TPU:0, one launch (start us, length us, event | category | flops | bytes accessed | tf_op | source)
XLA Modules:
  0.0 45.6 jit_solution(5640348749750797258)
XLA Ops:
  0.6 0.9 %copy.17 = bf16[2,8,16,128]{3,2,1,0:T(8,128)(2,1)S(1)} copy(bf16[2,8,16,128]{3,1,2,0:T(8,128)(2,1)} %bitcast.27) | data formatting | bytes 131072
  1.5 0.5 %collective-permute-start = (bf16[2,2,16,128]{3,2,1,0:T(8,128)(2,1)S(1)}, bf16[2,2,16,128]{3,2,1,0:T(8,128)(2,1)S(1)}, u32[]{:S(2)}, u32[]{:S(2)}) collective-permute-start(bf16[2,2,16,128]{3,2,1,0:T(8,128)(2,1)S(1)} %constant_dynamic-slice_fusion), channel_id=1, source_target_pairs={{0,1},{1,0},{2,3},{3,2},{4,5},{5,4},{6,7},{7,6},{8,9},{9,8},{10,11... | collective-permute-start | bytes 49160 | tf_op jit(solution)/shard_map/ppermute | solution.py:318
  2.0 0.8 %collective-permute-done.by_ref = bf16[2,2,16,128]{3,2,1,0:T(8,128)(2,1)S(1)} collective-permute-done((bf16[2,2,16,128]{3,2,1,0:T(8,128)(2,1)S(1)}, bf16[2,2,16,128]{3,2,1,0:T(8,128)(2,1)S(1)}, u32[]{:S(2)}, u32[]{:S(2)}) %collective-permute-start) | collective-permute-done | bytes 16416 | tf_op jit(solution)/shard_map/ppermute | solution.py:318
  2.9 3.0 %collective-permute-start.2 = (bf16[2,10,16,128]{3,2,1,0:T(8,128)(2,1)S(1)}, bf16[2,10,16,128]{3,2,1,0:T(8,128)(2,1)S(1)}, u32[]{:S(2)}, u32[]{:S(2)}) collective-permute-start(bf16[2,10,16,128]{3,2,1,0:T(8,128)(2,1)S(1)} %pad_maximum_fusion.1), channel_id=1, source_target_pairs={{0,4},{8,12},{4,0},{12,8},{1,5},{9,13},{5,1},{13,9},{2,6},{10,14},... | collective-permute-start | bytes 245768 | tf_op jit(solution)/shard_map/ppermute | solution.py:324
  5.9 0.7 %collective-permute-start.1 = (bf16[2,10,16,128]{3,2,1,0:T(8,128)(2,1)S(1)}, bf16[2,10,16,128]{3,2,1,0:T(8,128)(2,1)S(1)}, u32[]{:S(2)}, u32[]{:S(2)}) collective-permute-start(bf16[2,10,16,128]{3,2,1,0:T(8,128)(2,1)S(1)} %pad_maximum_fusion.1), channel_id=1, source_target_pairs={{4,8},{8,4},{5,9},{9,5},{6,10},{10,6},{7,11},{11,7},{20,24},{24,20... | collective-permute-start | bytes 245768 | tf_op jit(solution)/shard_map/ppermute | solution.py:324
  6.5 0.0 copy-start
  6.5 2.1 %shard_map.109 = (bf16[256,2304]{1,0:T(8,128)(2,1)S(1)}, bf16[256,3456]{1,0:T(8,128)(2,1)S(1)}, bf16[9,384,256]{2,1,0:T(8,128)(2,1)S(1)}, bf16[9,384,128]{2,1,0:T(8,128)(2,1)S(1)}, f32[2,256]{1,0:T(2,128)S(1)}) custom-call(f32[64,864]{1,0:T(8,128)} %bitcast.29, f32[64,1728]{1,0:T(8,128)} %bitcast.28, f32[1,64]{1,0:T(1,128)} %bitcast.30, f32[1,64]{1,0:T(1,128)} %bitcast.31), custom_call_target="tpu_custom_call" | custom-call | flops 2000000000 | bytes 7812500 | tf_op jit(solution)/shard_map/pallas_call | solution.py:350
  8.6 0.0 copy-done
  8.7 0.0 collective-permute-done.2.ev_ref
  8.7 0.0 collective-permute-done.1.od_ref
  8.7 2.7 %shard_map.110 = (bf16[6,12,16,256]{3,2,1,0:T(8,128)(2,1)S(1)}, bf16[4,10,16,384]{3,2,1,0:T(8,128)(2,1)S(1)}, f32[4,10,16,256]{3,2,1,0:T(8,128)S(1)}, bf16[2,8,1...) custom-call(bf16[2,8,16,128]{3,2,1,0:T(8,128)(2,1)S(1)} %copy.17, ...), custom_call_target="tpu_custom_call" | custom-call | flops 4800000000 | bytes 18750000 | tf_op jit(solution)/shard_map/pallas_call | solution.py:371
  11.3 0.1 collective-permute-start.3
  11.4 1.2 %shard_map.111 = (f32[32,1792]{1,0:T(8,128)S(1)}, bf16[32,1792]{1,0:T(8,128)(2,1)S(1)}, f32[4,10,16,256]{3,2,1,0:T(8,128)S(1)}) custom-call(bf16[4,10,16,384]{3,2,1,0:T(8,128)(2,1)S(1)} %get-tuple-element.64.a_ref, bf16[2,8,16,256]{3,2,1,0:T(8,128)(2,1)S(1)} %get-tuple-element.62.g_ref, f32[4,10,16,256]{3,2,1,0:T(8,128)S(1)} %get-tuple-element.65.y_ref), custom_call_target="tpu_custom_call" | custom-call | flops 1800000000 | bytes 7031250 | tf_op jit(solution)/shard_map/pallas_call | solution.py:384
  12.6 0.0 collective-permute-done.3.by_ref
  12.6 4.8 %collective-permute-start.5 = (bf16[2,10,16,256]{3,2,1,0:T(8,128)(2,1)S(1)}, bf16[2,10,16,256]{3,2,1,0:T(8,128)(2,1)S(1)}, u32[]{:S(2)}, u32[]{:S(2)}) collective-permute-start(bf16[2,10,16,256]{3,2,1,0:T(8,128)(2,1)S(1)} %constant_dynamic-update-slice_fusion), channel_id=1, source_target_pairs={{0,4},{8,12},{4,0},{12,8},{1,5},{9,13},{5,1},{13,9},{2,6},{10,14},... | collective-permute-start | bytes 491528 | tf_op jit(solution)/shard_map/ppermute | solution.py:324
  17.4 0.7 %collective-permute-start.4 = (bf16[2,10,16,256]{3,2,1,0:T(8,128)(2,1)S(1)}, bf16[2,10,16,256]{3,2,1,0:T(8,128)(2,1)S(1)}, u32[]{:S(2)}, u32[]{:S(2)}) collective-permute-start(bf16[2,10,16,256]{3,2,1,0:T(8,128)(2,1)S(1)} %constant_dynamic-update-slice_fusion), channel_id=1, source_target_pairs={{4,8},{8,4},{5,9},{9,5},{6,10},{10,6},{7,11},{11,7},{20,24},{24,20... | collective-permute-start | bytes 491528 | tf_op jit(solution)/shard_map/ppermute | solution.py:324
  18.1 1.4 %collective-permute-start.6 = (bf16[32,1792]{1,0:T(8,128)(2,1)S(1)}, bf16[32,1792]{1,0:T(8,128)(2,1)S(1)}, u32[]{:S(2)}, u32[]{:S(2)}) collective-permute-start(bf16[32,1792]{1,0:T(8,128)(2,1)S(1)} %get-tuple-element.71), channel_id=1, source_target_pairs={{0,3},{1,2},{2,1},{3,0},{4,7},{5,6},{6,5},{7,4},{8,11},{9,10},{10,... | collective-permute-start | bytes 344072 | tf_op jit(solution)/shard_map/ppermute | solution.py:341
  19.5 3.8 %collective-permute-done.6.h2_ref = bf16[32,1792]{1,0:T(8,128)(2,1)S(1)} collective-permute-done((bf16[32,1792]{1,0:T(8,128)(2,1)S(1)}, bf16[32,1792]{1,0:T(8,128)(2,1)S(1)}, u32[]{:S(2)}, u32[]{:S(2)}) %collective-permute-start.6) | collective-permute-done | bytes 114720 | tf_op jit(solution)/shard_map/ppermute | solution.py:341
  23.3 0.0 collective-permute-done.5.ev_ref
  23.3 0.0 collective-permute-done.4.od_ref
  23.3 1.9 %shard_map.112 = (f32[64,896]{1,0:T(8,128)S(1)}, bf16[64,896]{1,0:T(8,128)(2,1)S(1)}, bf16[2,8,16,256]{3,2,1,0:T(8,128)(2,1)S(1)}) custom-call(bf16[2,8,16,256]{3,2,1,0:T(8,128)(2,1)S(1)} %get-tuple-element.62.g_ref, bf16[2,2,16,256]{3,2,1,0:T(8,128)(2,1)S(1)} %collective-permute-done.3.by_ref, bf16[2,10,16,256]{3,2,1,0:T(8,128)(2,1)S(1)} %collective-permute-done.5.ev_ref, ...), custom_call_target="tpu_custom_call" | custom-call | flops 5600000000 | bytes 21875000 | tf_op jit(solution)/shard_map/pallas_call | solution.py:393
  25.1 0.2 collective-permute-start.7
  25.3 1.2 %collective-permute-done.7 = bf16[64,896]{1,0:T(8,128)(2,1)S(1)} collective-permute-done((bf16[64,896]{1,0:T(8,128)(2,1)S(1)}, bf16[64,896]{1,0:T(8,128)(2,1)S(1)}, u32[]{:S(2)}, u32[]{:S(2)}) %collective-permute-start.7) | collective-permute-done | bytes 114720 | tf_op jit(solution)/shard_map/ppermute | solution.py:318
  26.6 1.3 %collective-permute-start.8 = (bf16[32,896]{1,0:T(8,128)(2,1)S(1)}, bf16[32,896]{1,0:T(8,128)(2,1)S(1)}, u32[]{:S(2)}, u32[]{:S(2)}) collective-permute-start(bf16[32,896]{1,0:T(8,128)(2,1)S(1)} %get-tuple-element.81), channel_id=1, source_target_pairs={{0,3},{1,2},{2,1},{3,0},{4,7},{5,6},{6,5},{7,4},{8,11},{9,10},{10,... | collective-permute-start | bytes 172040 | tf_op jit(solution)/shard_map/ppermute | solution.py:341
  27.9 3.2 %collective-permute-start.11 = (bf16[32,896]{1,0:T(8,128)(2,1)S(1)}, bf16[32,896]{1,0:T(8,128)(2,1)S(1)}, u32[]{:S(2)}, u32[]{:S(2)}) collective-permute-start(bf16[32,896]{1,0:T(8,128)(2,1)S(1)} %get-tuple-element.90), channel_id=1, source_target_pairs={{0,5},{1,4},{4,1},{5,0},{8,13},{9,12},{12,9},{13,8},{2,7},{3,6},{6... | collective-permute-start | bytes 172040 | tf_op jit(solution)/shard_map/ppermute | solution.py:341
  31.1 1.0 %shard_map.113.t_ref = bf16[4,10,16,384]{3,2,1,0:T(8,128)(2,1)S(1)} custom-call(bf16[2,8,16,256]{3,2,1,0:T(8,128)(2,1)S(1)} %get-tuple-element.62.g_ref, bf16[2,2,16,256]{3,2,1,0:T(8,128)(2,1)S(1)} %collective-permute-done.3.by_ref, bf16[2,10,16,256]{3,2,1,0:T(8,128)(2,1)S(1)} %collective-permute-done.5.ev_ref, ...), custom_call_target="tpu_custom_call" | custom-call | flops 1400000000 | bytes 5468750 | tf_op jit(solution)/shard_map/pallas_call | solution.py:405
  32.1 0.0 collective-permute-done.8
  32.1 1.5 %collective-permute-start.9 = (bf16[32,896]{1,0:T(8,128)(2,1)S(1)}, bf16[32,896]{1,0:T(8,128)(2,1)S(1)}, u32[]{:S(2)}, u32[]{:S(2)}) collective-permute-start(bf16[32,896]{1,0:T(8,128)(2,1)S(1)} %add.23), channel_id=1, source_target_pairs={{0,5},{1,4},{4,1},{5,0},{8,13},{9,12},{12,9},{13,8},{2,7},{3,6},{6... | collective-permute-start | bytes 172040 | tf_op jit(solution)/shard_map/ppermute | solution.py:341
  33.6 0.0 collective-permute-done.11
  33.6 2.0 %collective-permute-start.12 = (bf16[32,896]{1,0:T(8,128)(2,1)S(1)}, bf16[32,896]{1,0:T(8,128)(2,1)S(1)}, u32[]{:S(2)}, u32[]{:S(2)}) collective-permute-start(bf16[32,896]{1,0:T(8,128)(2,1)S(1)} %add.25), channel_id=1, source_target_pairs={{0,9},{1,8},{4,13},{5,12},{8,1},{9,0},{12,5},{13,4},{2,11},{3,10},... | collective-permute-start | bytes 172040 | tf_op jit(solution)/shard_map/ppermute | solution.py:341
  35.6 0.7 %reshape.40 = bf16[1,2,8,4096]{3,2,1,0:T(8,128)(2,1)} reshape(bf16[2,8,16,256]{3,2,1,0:T(8,128)(2,1)S(1)} %get-tuple-element.84) | data formatting | bytes 262144 | tf_op jit(solution)/shard_map/reshape | solution.py:411
  36.4 0.0 collective-permute-done.9
  36.4 2.0 %collective-permute-start.10 = (bf16[32,896]{1,0:T(8,128)(2,1)S(1)}, bf16[32,896]{1,0:T(8,128)(2,1)S(1)}, u32[]{:S(2)}, u32[]{:S(2)}) collective-permute-start(bf16[32,896]{1,0:T(8,128)(2,1)S(1)} %add.24), channel_id=1, source_target_pairs={{0,9},{1,8},{4,13},{5,12},{8,1},{9,0},{12,5},{13,4},{2,11},{3,10},... | collective-permute-start | bytes 172040 | tf_op jit(solution)/shard_map/ppermute | solution.py:341
  38.4 0.0 collective-permute-done.12
  38.4 2.8 %collective-permute-start.13 = (bf16[32,896]{1,0:T(8,128)(2,1)S(1)}, bf16[32,896]{1,0:T(8,128)(2,1)S(1)}, u32[]{:S(2)}, u32[]{:S(2)}) collective-permute-start(bf16[32,896]{1,0:T(8,128)(2,1)S(1)} %add.26), channel_id=1, source_target_pairs={{0,3},{1,2},{2,1},{3,0},{4,7},{5,6},{6,5},{7,4},{8,11},{9,10},{10,... | collective-permute-start | bytes 172040 | tf_op jit(solution)/shard_map/ppermute | solution.py:341
  41.2 0.6 %shard_map.114 = bf16[2,8,16,128]{3,2,1,0:T(8,128)(2,1)S(1)} custom-call(bf16[4,10,16,384]{3,2,1,0:T(8,128)(2,1)S(1)} %shard_map.113.t_ref, bf16[9,384,128]{2,1,0:T(8,128)(2,1)S(1)} %get-tuple-element.88.r1_ref), custom_call_target="tpu_custom_call" | custom-call | flops 1200000000 | bytes 4687500 | tf_op jit(solution)/shard_map/pallas_call | solution.py:420
  41.8 0.7 %reshape.41 = bf16[1,2,8,2048]{3,2,1,0:T(8,128)(2,1)} reshape(bf16[2,8,16,128]{3,2,1,0:T(8,128)(2,1)S(1)} %shard_map.114) | data formatting | bytes 131072 | tf_op jit(solution)/shard_map/reshape | solution.py:421
  42.5 0.0 collective-permute-done.10
  42.5 0.7 %collective-permute-done.13 = bf16[32,896]{1,0:T(8,128)(2,1)S(1)} collective-permute-done((bf16[32,896]{1,0:T(8,128)(2,1)S(1)}, bf16[32,896]{1,0:T(8,128)(2,1)S(1)}, u32[]{:S(2)}, u32[]{:S(2)}) %collective-permute-start.13) | collective-permute-done | bytes 57376 | tf_op jit(solution)/shard_map/ppermute | solution.py:341
  43.2 0.4 collective-permute-start.14
  43.6 1.1 %collective-permute-done.14.h_ref = bf16[96,896]{1,0:T(8,128)(2,1)S(1)} collective-permute-done((bf16[96,896]{1,0:T(8,128)(2,1)S(1)}, bf16[96,896]{1,0:T(8,128)(2,1)S(1)}, u32[]{:S(2)}, u32[]{:S(2)}) %collective-permute-start.14) | collective-permute-done | bytes 172064 | tf_op jit(solution)/shard_map/ppermute | solution.py:318
  44.7 1.0 %shard_map.115 = (f32[64,1728]{1,0:T(8,128)}, f32[1,64]{1,0:T(1,128)}, f32[64,864]{1,0:T(8,128)}, f32[1,64]{1,0:T(1,128)}) custom-call(bf16[96,896]{1,0:T(8,128)(2,1)S(1)} %pad_maximum_fusion.m_ref, bf16[96,896]{1,0:T(8,128)(2,1)S(1)} %collective-permute-done.14.h_ref), custom_call_target="tpu_custom_call" | custom-call | flops 1200000000 | bytes 4687500 | tf_op jit(solution)/shard_map/pallas_call | solution.py:430
  (13 shorter events, 0.2 us)
Async XLA Ops:
  1.5 1.4 %collective-permute-start = (bf16[2,2,16,128]{3,2,1,0:T(8,128)(2,1)S(1)}, bf16[2,2,16,128]{3,2,1,0:T(8,128)(2,1)S(1)}, u32[]{:S(2)}, u32[]{:S(2)}) collective-permute-start(bf16[2,2,16,128]{3,2,1,0:T(8,128)(2,1)S(1)} %constant_dynamic-slice_fusion), channel_id=1, source_target_pairs={{0,1},{1,0},{2,3},{3,2},{4,5},{5,4},{6,7},{7,6},{8,9},{9,8},{10,11... | collective-permute-start | bytes 49160 | tf_op jit(solution)/shard_map/ppermute | solution.py:318
  2.9 5.8 %collective-permute-start.2 = (bf16[2,10,16,128]{3,2,1,0:T(8,128)(2,1)S(1)}, bf16[2,10,16,128]{3,2,1,0:T(8,128)(2,1)S(1)}, u32[]{:S(2)}, u32[]{:S(2)}) collective-permute-start(bf16[2,10,16,128]{3,2,1,0:T(8,128)(2,1)S(1)} %pad_maximum_fusion.1), channel_id=1, source_target_pairs={{0,4},{8,12},{4,0},{12,8},{1,5},{9,13},{5,1},{13,9},{2,6},{10,14},... | collective-permute-start | bytes 245768 | tf_op jit(solution)/shard_map/ppermute | solution.py:324
  5.9 2.8 %collective-permute-start.1 = (bf16[2,10,16,128]{3,2,1,0:T(8,128)(2,1)S(1)}, bf16[2,10,16,128]{3,2,1,0:T(8,128)(2,1)S(1)}, u32[]{:S(2)}, u32[]{:S(2)}) collective-permute-start(bf16[2,10,16,128]{3,2,1,0:T(8,128)(2,1)S(1)} %pad_maximum_fusion.1), channel_id=1, source_target_pairs={{4,8},{8,4},{5,9},{9,5},{6,10},{10,6},{7,11},{11,7},{20,24},{24,20... | collective-permute-start | bytes 245768 | tf_op jit(solution)/shard_map/ppermute | solution.py:324
  6.5 2.1 %copy-start = (bf16[1,2,8,4096]{3,2,1,0:T(8,128)(2,1)S(1)}, bf16[1,2,8,4096]{3,2,1,0:T(8,128)(2,1)}, u32[]{:S(2)}) copy-start(bf16[1,2,8,4096]{3,2,1,0:T(8,128)(2,1)} %param.11) | copy-start | bytes 393220
  11.3 1.3 %collective-permute-start.3 = (bf16[2,2,16,256]{3,2,1,0:T(8,128)(2,1)S(1)}, bf16[2,2,16,256]{3,2,1,0:T(8,128)(2,1)S(1)}, u32[]{:S(2)}, u32[]{:S(2)}) collective-permute-start(bf16[2,2,16,256]{3,2,1,0:T(8,128)(2,1)S(1)} %get-tuple-element.63), channel_id=1, source_target_pairs={{0,1},{1,0},{2,3},{3,2},{4,5},{5,4},{6,7},{7,6},{8,9},{9,8},{10,11... | collective-permute-start | bytes 98312 | tf_op jit(solution)/shard_map/ppermute | solution.py:318
  12.6 10.6 %collective-permute-start.5 = (bf16[2,10,16,256]{3,2,1,0:T(8,128)(2,1)S(1)}, bf16[2,10,16,256]{3,2,1,0:T(8,128)(2,1)S(1)}, u32[]{:S(2)}, u32[]{:S(2)}) collective-permute-start(bf16[2,10,16,256]{3,2,1,0:T(8,128)(2,1)S(1)} %constant_dynamic-update-slice_fusion), channel_id=1, source_target_pairs={{0,4},{8,12},{4,0},{12,8},{1,5},{9,13},{5,1},{13,9},{2,6},{10,14},... | collective-permute-start | bytes 491528 | tf_op jit(solution)/shard_map/ppermute | solution.py:324
  17.4 5.9 %collective-permute-start.4 = (bf16[2,10,16,256]{3,2,1,0:T(8,128)(2,1)S(1)}, bf16[2,10,16,256]{3,2,1,0:T(8,128)(2,1)S(1)}, u32[]{:S(2)}, u32[]{:S(2)}) collective-permute-start(bf16[2,10,16,256]{3,2,1,0:T(8,128)(2,1)S(1)} %constant_dynamic-update-slice_fusion), channel_id=1, source_target_pairs={{4,8},{8,4},{5,9},{9,5},{6,10},{10,6},{7,11},{11,7},{20,24},{24,20... | collective-permute-start | bytes 491528 | tf_op jit(solution)/shard_map/ppermute | solution.py:324
  18.1 5.2 %collective-permute-start.6 = (bf16[32,1792]{1,0:T(8,128)(2,1)S(1)}, bf16[32,1792]{1,0:T(8,128)(2,1)S(1)}, u32[]{:S(2)}, u32[]{:S(2)}) collective-permute-start(bf16[32,1792]{1,0:T(8,128)(2,1)S(1)} %get-tuple-element.71), channel_id=1, source_target_pairs={{0,3},{1,2},{2,1},{3,0},{4,7},{5,6},{6,5},{7,4},{8,11},{9,10},{10,... | collective-permute-start | bytes 344072 | tf_op jit(solution)/shard_map/ppermute | solution.py:341
  25.1 1.4 %collective-permute-start.7 = (bf16[64,896]{1,0:T(8,128)(2,1)S(1)}, bf16[64,896]{1,0:T(8,128)(2,1)S(1)}, u32[]{:S(2)}, u32[]{:S(2)}) collective-permute-start(bf16[64,896]{1,0:T(8,128)(2,1)S(1)} %get-tuple-element.80), channel_id=1, source_target_pairs={{0,1},{1,0},{2,3},{3,2},{4,5},{5,4},{6,7},{7,6},{8,9},{9,8},{10,11... | collective-permute-start | bytes 344072 | tf_op jit(solution)/shard_map/ppermute | solution.py:318
  26.6 5.5 %collective-permute-start.8 = (bf16[32,896]{1,0:T(8,128)(2,1)S(1)}, bf16[32,896]{1,0:T(8,128)(2,1)S(1)}, u32[]{:S(2)}, u32[]{:S(2)}) collective-permute-start(bf16[32,896]{1,0:T(8,128)(2,1)S(1)} %get-tuple-element.81), channel_id=1, source_target_pairs={{0,3},{1,2},{2,1},{3,0},{4,7},{5,6},{6,5},{7,4},{8,11},{9,10},{10,... | collective-permute-start | bytes 172040 | tf_op jit(solution)/shard_map/ppermute | solution.py:341
  27.9 5.7 %collective-permute-start.11 = (bf16[32,896]{1,0:T(8,128)(2,1)S(1)}, bf16[32,896]{1,0:T(8,128)(2,1)S(1)}, u32[]{:S(2)}, u32[]{:S(2)}) collective-permute-start(bf16[32,896]{1,0:T(8,128)(2,1)S(1)} %get-tuple-element.90), channel_id=1, source_target_pairs={{0,5},{1,4},{4,1},{5,0},{8,13},{9,12},{12,9},{13,8},{2,7},{3,6},{6... | collective-permute-start | bytes 172040 | tf_op jit(solution)/shard_map/ppermute | solution.py:341
  32.1 4.3 %collective-permute-start.9 = (bf16[32,896]{1,0:T(8,128)(2,1)S(1)}, bf16[32,896]{1,0:T(8,128)(2,1)S(1)}, u32[]{:S(2)}, u32[]{:S(2)}) collective-permute-start(bf16[32,896]{1,0:T(8,128)(2,1)S(1)} %add.23), channel_id=1, source_target_pairs={{0,5},{1,4},{4,1},{5,0},{8,13},{9,12},{12,9},{13,8},{2,7},{3,6},{6... | collective-permute-start | bytes 172040 | tf_op jit(solution)/shard_map/ppermute | solution.py:341
  33.6 4.7 %collective-permute-start.12 = (bf16[32,896]{1,0:T(8,128)(2,1)S(1)}, bf16[32,896]{1,0:T(8,128)(2,1)S(1)}, u32[]{:S(2)}, u32[]{:S(2)}) collective-permute-start(bf16[32,896]{1,0:T(8,128)(2,1)S(1)} %add.25), channel_id=1, source_target_pairs={{0,9},{1,8},{4,13},{5,12},{8,1},{9,0},{12,5},{13,4},{2,11},{3,10},... | collective-permute-start | bytes 172040 | tf_op jit(solution)/shard_map/ppermute | solution.py:341
  36.4 6.1 %collective-permute-start.10 = (bf16[32,896]{1,0:T(8,128)(2,1)S(1)}, bf16[32,896]{1,0:T(8,128)(2,1)S(1)}, u32[]{:S(2)}, u32[]{:S(2)}) collective-permute-start(bf16[32,896]{1,0:T(8,128)(2,1)S(1)} %add.24), channel_id=1, source_target_pairs={{0,9},{1,8},{4,13},{5,12},{8,1},{9,0},{12,5},{13,4},{2,11},{3,10},... | collective-permute-start | bytes 172040 | tf_op jit(solution)/shard_map/ppermute | solution.py:341
  38.4 4.8 %collective-permute-start.13 = (bf16[32,896]{1,0:T(8,128)(2,1)S(1)}, bf16[32,896]{1,0:T(8,128)(2,1)S(1)}, u32[]{:S(2)}, u32[]{:S(2)}) collective-permute-start(bf16[32,896]{1,0:T(8,128)(2,1)S(1)} %add.26), channel_id=1, source_target_pairs={{0,3},{1,2},{2,1},{3,0},{4,7},{5,6},{6,5},{7,4},{8,11},{9,10},{10,... | collective-permute-start | bytes 172040 | tf_op jit(solution)/shard_map/ppermute | solution.py:341
  43.2 1.5 %collective-permute-start.14 = (bf16[96,896]{1,0:T(8,128)(2,1)S(1)}, bf16[96,896]{1,0:T(8,128)(2,1)S(1)}, u32[]{:S(2)}, u32[]{:S(2)}) collective-permute-start(bf16[96,896]{1,0:T(8,128)(2,1)S(1)} %pad_maximum_fusion.m_ref), channel_id=1, source_target_pairs={{0,1},{1,0},{2,3},{3,2},{4,5},{5,4},{6,7},{7,6},{8,9},{9,8},{10,11... | collective-permute-start | bytes 516104 | tf_op jit(solution)/shard_map/ppermute | solution.py:318

commit v7 on v6

--- a/solution.py
+++ b/solution.py
@@ -180,7 +180,7 @@
     return total
 
 
-def second_weights_body(a_ref, g_ref, y_ref, k_ref, s_ref, d_ref, p_ref):
+def second_weights_body(a_ref, g_ref, k_ref, s_ref, p_ref):
     turned, bias = flipped(g_ref[...].reshape(-1, MID_L))
     narrow = g_ref.shape[1]
     lane = lax.broadcasted_iota(jnp.int32, (64, 384), 1)
@@ -196,6 +196,9 @@
             at = (tap - 1) * TAP2
             p_ref[:, at : at + 384] = jnp.where(lane < TAP2, held, pltpu.roll(found, TAP2, 1))
     k_ref[...], s_ref[...] = halves(p_ref, lax.axis_index("dp") % 2)
+
+
+def slope_body(y_ref, d_ref):
     core = lax.axis_index("ysp")
     space = lax.axis_index("space")
     last = lax.axis_size("space") - 1
@@ -367,7 +370,7 @@
         in_specs=[hbm] * 4,
     )(*[pltpu.with_memory_space_constraint(v, pltpu.HBM) for v in (w_first.T, w_second.T, b_first.reshape(1, C_MID), b_second.reshape(1, C_MID))])
     cot = cotangent.reshape(nx, ny, ROWS, MID_L)
-    odd, even, cot, f1, f2, r2, r1, bias = hold((odd, even, cot, *banded))
+    even, odd, cot, f1, f2, r2, r1, bias = hold((even, odd, cot, *banded))
     wide_in, act, y1, out, g2, edge = call(
         forward_body,
         4800000000,
@@ -381,15 +384,13 @@
         ],
         [pltpu.VMEM(((nx + 2) * (ny + 2) * ROWS, MID_L), F32)],
     )(own, side, even, odd, f1, f2, bias, cot)
-    keep2, send2, slope = call(
-        second_weights_body,
-        1800000000,
-        [((32, PACK2), F32), ((32, PACK2), BF), ((nx + 2, ny + 2, ROWS, MID_L), F32)],
-        [pltpu.VMEM((64, PACK2), F32)],
-    )(act, g2, y1)
-    side, even, odd, keep2, send2, slope = halo(g2, edge, keep2, send2, slope)
+    keep2, send2 = call(
+        second_weights_body, 1800000000, [((32, PACK2), F32), ((32, PACK2), BF)], [pltpu.VMEM((64, PACK2), F32)]
+    )(act, g2)
+    side, even, odd, keep2, send2, y1 = halo(g2, edge, keep2, send2, y1)
     got2 = cross(send2, "dp", 1)
-    odd, even, keep2, got2 = hold((odd, even, keep2, got2))
+    (slope,) = call(slope_body, 1600000000, [((nx + 2, ny + 2, ROWS, MID_L), F32)])(y1)
+    odd, even, keep2, got2, slope = hold((odd, even, keep2, got2, slope))
     keep, send, g1 = call(
         backward_body,
         5600000000,

time: 45.8 us -> 45.5 us (level)
  starting transfers between devices: 24.4 us -> 23.1 us
  waiting for transfers between devices: 7.64 us -> 8.59 us
    ppermute x7, starting transfers between devices: 14.2 us -> 12.7 us  [cross(): return lax.ppermute(cells, (axis, 'ysp'), pairs)]
    ppermute x7, waiting for transfers between devices: 4.52 us -> 5.05 us  [cross(): return lax.ppermute(cells, (axis, 'ysp'), pairs)]
  transfers between devices with their start and end apart: 15 -> 15, of which waited for: 5 -> 9; matrix products, arithmetic and copies ran while one was open for 3% -> 3% of each run, Pallas kernels for 11% -> 11%
where the time goes in v7:
time: 45.5 us; the launch traced here: 45.3 us
  starting transfers between devices  23.1 us (51%)
  Pallas kernels  10.4 us (23%)
  waiting for transfers between devices  8.59 us (19%)
  local copies, waits for them, and re-layouts  2.3 us (5%)
  between operations  0.8 us (2%)
    ppermute x7, starting transfers between devices, cross(): return lax.ppermute(cells, (axis, 'ysp'), pairs)  12.7 us
    ppermute x4, starting transfers between devices, pair_swap(): return lax.ppermute(cells, 'space', pairs + [(j, i) for i, j in pairs])  9.07 us
    ppermute x7, waiting for transfers between devices, cross(): return lax.ppermute(cells, (axis, 'ysp'), pairs)  5.05 us
    ppermute x4, waiting for transfers between devices, swap(): lax.ppermute(cells, axis, [(i, i ^ bit) for i in range(lax.axis_size(axis...  3.19 us
    pallas_call x1, Pallas kernels, on_device(): call(forward_body, 4800000000, [((nx + 4, ny + 4, ROWS, 256), BF), ((nx +...  2.65 us
    pallas_call x1, Pallas kernels, on_device(): call(banded_body, 2000000000, [((256, 9 * 256), BF), ((256, 9 * 384), BF)...  2.08 us
    pallas_call x1, Pallas kernels, on_device(): call(backward_body, 5600000000, [((64, PACK1), F32), ((64, PACK1), BF), (...  1.86 us
    ppermute x4, starting transfers between devices, swap(): lax.ppermute(cells, axis, [(i, i ^ bit) for i in range(lax.axis_size(axis...  1.32 us
  transfers between devices with their start and end apart: 15, of which 9 were waited for; matrix products, arithmetic and copies ran while one was open for 3% of the time, Pallas kernels for 11%

profile of v7, /device:TPU:0, one launch (start us, length us, event | category | flops | bytes accessed | tf_op | source)
XLA Modules:
  0.0 45.3 jit_solution(14977243942907106693)
XLA Ops:
  0.6 0.9 %copy.17 = bf16[2,8,16,128]{3,2,1,0:T(8,128)(2,1)S(1)} copy(bf16[2,8,16,128]{3,1,2,0:T(8,128)(2,1)} %bitcast.27) | data formatting | bytes 131072
  1.5 0.5 %collective-permute-start = (bf16[2,2,16,128]{3,2,1,0:T(8,128)(2,1)S(1)}, bf16[2,2,16,128]{3,2,1,0:T(8,128)(2,1)S(1)}, u32[]{:S(2)}, u32[]{:S(2)}) collective-permute-start(bf16[2,2,16,128]{3,2,1,0:T(8,128)(2,1)S(1)} %constant_dynamic-slice_fusion), channel_id=1, source_target_pairs={{0,1},{1,0},{2,3},{3,2},{4,5},{5,4},{6,7},{7,6},{8,9},{9,8},{10,11... | collective-permute-start | bytes 49160 | tf_op jit(solution)/shard_map/ppermute | solution.py:321
  2.0 0.8 %collective-permute-done.by_ref = bf16[2,2,16,128]{3,2,1,0:T(8,128)(2,1)S(1)} collective-permute-done((bf16[2,2,16,128]{3,2,1,0:T(8,128)(2,1)S(1)}, bf16[2,2,16,128]{3,2,1,0:T(8,128)(2,1)S(1)}, u32[]{:S(2)}, u32[]{:S(2)}) %collective-permute-start) | collective-permute-done | bytes 16416 | tf_op jit(solution)/shard_map/ppermute | solution.py:321
  2.9 0.7 %collective-permute-start.2 = (bf16[2,10,16,128]{3,2,1,0:T(8,128)(2,1)S(1)}, bf16[2,10,16,128]{3,2,1,0:T(8,128)(2,1)S(1)}, u32[]{:S(2)}, u32[]{:S(2)}) collective-permute-start(bf16[2,10,16,128]{3,2,1,0:T(8,128)(2,1)S(1)} %pad_maximum_fusion.1), channel_id=1, source_target_pairs={{4,8},{8,4},{5,9},{9,5},{6,10},{10,6},{7,11},{11,7},{20,24},{24,20... | collective-permute-start | bytes 245768 | tf_op jit(solution)/shard_map/ppermute | solution.py:327
  3.6 5.8 %collective-permute-start.1 = (bf16[2,10,16,128]{3,2,1,0:T(8,128)(2,1)S(1)}, bf16[2,10,16,128]{3,2,1,0:T(8,128)(2,1)S(1)}, u32[]{:S(2)}, u32[]{:S(2)}) collective-permute-start(bf16[2,10,16,128]{3,2,1,0:T(8,128)(2,1)S(1)} %pad_maximum_fusion.1), channel_id=1, source_target_pairs={{0,4},{8,12},{4,0},{12,8},{1,5},{9,13},{5,1},{13,9},{2,6},{10,14},... | collective-permute-start | bytes 245768 | tf_op jit(solution)/shard_map/ppermute | solution.py:327
  9.4 0.0 copy-start
  9.4 2.1 %shard_map.109 = (bf16[256,2304]{1,0:T(8,128)(2,1)S(1)}, bf16[256,3456]{1,0:T(8,128)(2,1)S(1)}, bf16[9,384,256]{2,1,0:T(8,128)(2,1)S(1)}, bf16[9,384,128]{2,1,0:T(8,128)(2,1)S(1)}, f32[2,256]{1,0:T(2,128)S(1)}) custom-call(f32[64,864]{1,0:T(8,128)} %bitcast.29, f32[64,1728]{1,0:T(8,128)} %bitcast.28, f32[1,64]{1,0:T(1,128)} %bitcast.30, f32[1,64]{1,0:T(1,128)} %bitcast.31), custom_call_target="tpu_custom_call" | custom-call | flops 2000000000 | bytes 7812500 | tf_op jit(solution)/shard_map/pallas_call | solution.py:353
  11.4 0.0 copy-done
  11.5 0.0 collective-permute-done.2.od_ref
  11.5 0.4 collective-permute-done.1.ev_ref
  11.8 2.7 %shard_map.110 = (bf16[6,12,16,256]{3,2,1,0:T(8,128)(2,1)S(1)}, bf16[4,10,16,384]{3,2,1,0:T(8,128)(2,1)S(1)}, f32[4,10,16,256]{3,2,1,0:T(8,128)S(1)}, bf16[2,8,1...) custom-call(bf16[2,8,16,128]{3,2,1,0:T(8,128)(2,1)S(1)} %copy.17, ...), custom_call_target="tpu_custom_call" | custom-call | flops 4800000000 | bytes 18750000 | tf_op jit(solution)/shard_map/pallas_call | solution.py:374
  14.5 0.1 collective-permute-start.3
  14.6 1.0 %shard_map.111 = (f32[32,1792]{1,0:T(8,128)S(1)}, bf16[32,1792]{1,0:T(8,128)(2,1)S(1)}) custom-call(bf16[4,10,16,384]{3,2,1,0:T(8,128)(2,1)S(1)} %get-tuple-element.64.a_ref, bf16[2,8,16,256]{3,2,1,0:T(8,128)(2,1)S(1)} %get-tuple-element.62.g_ref), custom_call_target="tpu_custom_call" | custom-call | flops 1800000000 | bytes 7031250 | tf_op jit(solution)/shard_map/pallas_call | solution.py:387
  15.6 0.2 collective-permute-done.3.by_ref
  15.8 1.9 %collective-permute-start.5 = (bf16[2,10,16,256]{3,2,1,0:T(8,128)(2,1)S(1)}, bf16[2,10,16,256]{3,2,1,0:T(8,128)(2,1)S(1)}, u32[]{:S(2)}, u32[]{:S(2)}) collective-permute-start(bf16[2,10,16,256]{3,2,1,0:T(8,128)(2,1)S(1)} %constant_dynamic-update-slice_fusion), channel_id=1, source_target_pairs={{0,4},{8,12},{4,0},{12,8},{1,5},{9,13},{5,1},{13,9},{2,6},{10,14},... | collective-permute-start | bytes 491528 | tf_op jit(solution)/shard_map/ppermute | solution.py:327
  17.7 0.7 %collective-permute-start.4 = (bf16[2,10,16,256]{3,2,1,0:T(8,128)(2,1)S(1)}, bf16[2,10,16,256]{3,2,1,0:T(8,128)(2,1)S(1)}, u32[]{:S(2)}, u32[]{:S(2)}) collective-permute-start(bf16[2,10,16,256]{3,2,1,0:T(8,128)(2,1)S(1)} %constant_dynamic-update-slice_fusion), channel_id=1, source_target_pairs={{4,8},{8,4},{5,9},{9,5},{6,10},{10,6},{7,11},{11,7},{20,24},{24,20... | collective-permute-start | bytes 491528 | tf_op jit(solution)/shard_map/ppermute | solution.py:327
  18.4 1.3 %collective-permute-start.6 = (bf16[32,1792]{1,0:T(8,128)(2,1)S(1)}, bf16[32,1792]{1,0:T(8,128)(2,1)S(1)}, u32[]{:S(2)}, u32[]{:S(2)}) collective-permute-start(bf16[32,1792]{1,0:T(8,128)(2,1)S(1)} %get-tuple-element.70), channel_id=1, source_target_pairs={{0,3},{1,2},{2,1},{3,0},{4,7},{5,6},{6,5},{7,4},{8,11},{9,10},{10,... | collective-permute-start | bytes 344072 | tf_op jit(solution)/shard_map/ppermute | solution.py:344
  19.7 0.2 shard_map.112.d_ref
  19.9 3.6 %collective-permute-done.6.h2_ref = bf16[32,1792]{1,0:T(8,128)(2,1)S(1)} collective-permute-done((bf16[32,1792]{1,0:T(8,128)(2,1)S(1)}, bf16[32,1792]{1,0:T(8,128)(2,1)S(1)}, u32[]{:S(2)}, u32[]{:S(2)}) %collective-permute-start.6) | collective-permute-done | bytes 114720 | tf_op jit(solution)/shard_map/ppermute | solution.py:344
  23.6 0.0 collective-permute-done.5.ev_ref
  23.6 0.0 collective-permute-done.4.od_ref
  23.6 1.9 %shard_map.113 = (f32[64,896]{1,0:T(8,128)S(1)}, bf16[64,896]{1,0:T(8,128)(2,1)S(1)}, bf16[2,8,16,256]{3,2,1,0:T(8,128)(2,1)S(1)}) custom-call(bf16[2,8,16,256]{3,2,1,0:T(8,128)(2,1)S(1)} %get-tuple-element.62.g_ref, bf16[2,2,16,256]{3,2,1,0:T(8,128)(2,1)S(1)} %collective-permute-done.3.by_ref, bf16[2,10,16,256]{3,2,1,0:T(8,128)(2,1)S(1)} %collective-permute-done.5.ev_ref, ...), custom_call_target="tpu_custom_call" | custom-call | flops 5600000000 | bytes 21875000 | tf_op jit(solution)/shard_map/pallas_call | solution.py:394
  25.4 0.2 collective-permute-start.7
  25.7 1.1 %collective-permute-done.7 = bf16[64,896]{1,0:T(8,128)(2,1)S(1)} collective-permute-done((bf16[64,896]{1,0:T(8,128)(2,1)S(1)}, bf16[64,896]{1,0:T(8,128)(2,1)S(1)}, u32[]{:S(2)}, u32[]{:S(2)}) %collective-permute-start.7) | collective-permute-done | bytes 114720 | tf_op jit(solution)/shard_map/ppermute | solution.py:321
  26.9 1.3 %collective-permute-start.8 = (bf16[32,896]{1,0:T(8,128)(2,1)S(1)}, bf16[32,896]{1,0:T(8,128)(2,1)S(1)}, u32[]{:S(2)}, u32[]{:S(2)}) collective-permute-start(bf16[32,896]{1,0:T(8,128)(2,1)S(1)} %get-tuple-element.81), channel_id=1, source_target_pairs={{0,3},{1,2},{2,1},{3,0},{4,7},{5,6},{6,5},{7,4},{8,11},{9,10},{10,... | collective-permute-start | bytes 172040 | tf_op jit(solution)/shard_map/ppermute | solution.py:344
  28.2 2.5 %collective-permute-start.11 = (bf16[32,896]{1,0:T(8,128)(2,1)S(1)}, bf16[32,896]{1,0:T(8,128)(2,1)S(1)}, u32[]{:S(2)}, u32[]{:S(2)}) collective-permute-start(bf16[32,896]{1,0:T(8,128)(2,1)S(1)} %get-tuple-element.90), channel_id=1, source_target_pairs={{0,5},{1,4},{4,1},{5,0},{8,13},{9,12},{12,9},{13,8},{2,7},{3,6},{6... | collective-permute-start | bytes 172040 | tf_op jit(solution)/shard_map/ppermute | solution.py:344
  30.7 1.0 %shard_map.114.t_ref = bf16[4,10,16,384]{3,2,1,0:T(8,128)(2,1)S(1)} custom-call(bf16[2,8,16,256]{3,2,1,0:T(8,128)(2,1)S(1)} %get-tuple-element.62.g_ref, bf16[2,2,16,256]{3,2,1,0:T(8,128)(2,1)S(1)} %collective-permute-done.3.by_ref, bf16[2,10,16,256]{3,2,1,0:T(8,128)(2,1)S(1)} %collective-permute-done.5.ev_ref, ...), custom_call_target="tpu_custom_call" | custom-call | flops 1400000000 | bytes 5468750 | tf_op jit(solution)/shard_map/pallas_call | solution.py:406
  31.7 0.0 collective-permute-done.8
  31.8 1.5 %collective-permute-start.9 = (bf16[32,896]{1,0:T(8,128)(2,1)S(1)}, bf16[32,896]{1,0:T(8,128)(2,1)S(1)}, u32[]{:S(2)}, u32[]{:S(2)}) collective-permute-start(bf16[32,896]{1,0:T(8,128)(2,1)S(1)} %add.23), channel_id=1, source_target_pairs={{0,5},{1,4},{4,1},{5,0},{8,13},{9,12},{12,9},{13,8},{2,7},{3,6},{6... | collective-permute-start | bytes 172040 | tf_op jit(solution)/shard_map/ppermute | solution.py:344
  33.3 0.0 collective-permute-done.11
  33.3 1.5 %collective-permute-start.12 = (bf16[32,896]{1,0:T(8,128)(2,1)S(1)}, bf16[32,896]{1,0:T(8,128)(2,1)S(1)}, u32[]{:S(2)}, u32[]{:S(2)}) collective-permute-start(bf16[32,896]{1,0:T(8,128)(2,1)S(1)} %add.25), channel_id=1, source_target_pairs={{0,9},{1,8},{4,13},{5,12},{8,1},{9,0},{12,5},{13,4},{2,11},{3,10},... | collective-permute-start | bytes 172040 | tf_op jit(solution)/shard_map/ppermute | solution.py:344
  34.8 0.7 %reshape.40 = bf16[1,2,8,4096]{3,2,1,0:T(8,128)(2,1)} reshape(bf16[2,8,16,256]{3,2,1,0:T(8,128)(2,1)S(1)} %get-tuple-element.84) | data formatting | bytes 262144 | tf_op jit(solution)/shard_map/reshape | solution.py:412
  35.5 0.2 collective-permute-done.9
  35.7 1.8 %collective-permute-start.10 = (bf16[32,896]{1,0:T(8,128)(2,1)S(1)}, bf16[32,896]{1,0:T(8,128)(2,1)S(1)}, u32[]{:S(2)}, u32[]{:S(2)}) collective-permute-start(bf16[32,896]{1,0:T(8,128)(2,1)S(1)} %add.24), channel_id=1, source_target_pairs={{0,9},{1,8},{4,13},{5,12},{8,1},{9,0},{12,5},{13,4},{2,11},{3,10},... | collective-permute-start | bytes 172040 | tf_op jit(solution)/shard_map/ppermute | solution.py:344
  37.5 0.5 %collective-permute-done.12 = bf16[32,896]{1,0:T(8,128)(2,1)S(1)} collective-permute-done((bf16[32,896]{1,0:T(8,128)(2,1)S(1)}, bf16[32,896]{1,0:T(8,128)(2,1)S(1)}, u32[]{:S(2)}, u32[]{:S(2)}) %collective-permute-start.12) | collective-permute-done | bytes 57376 | tf_op jit(solution)/shard_map/ppermute | solution.py:344
  38.0 2.7 %collective-permute-start.13 = (bf16[32,896]{1,0:T(8,128)(2,1)S(1)}, bf16[32,896]{1,0:T(8,128)(2,1)S(1)}, u32[]{:S(2)}, u32[]{:S(2)}) collective-permute-start(bf16[32,896]{1,0:T(8,128)(2,1)S(1)} %add.26), channel_id=1, source_target_pairs={{0,3},{1,2},{2,1},{3,0},{4,7},{5,6},{6,5},{7,4},{8,11},{9,10},{10,... | collective-permute-start | bytes 172040 | tf_op jit(solution)/shard_map/ppermute | solution.py:344
  40.8 0.6 %shard_map.115 = bf16[2,8,16,128]{3,2,1,0:T(8,128)(2,1)S(1)} custom-call(bf16[4,10,16,384]{3,2,1,0:T(8,128)(2,1)S(1)} %shard_map.114.t_ref, bf16[9,384,128]{2,1,0:T(8,128)(2,1)S(1)} %get-tuple-element.88.r1_ref), custom_call_target="tpu_custom_call" | custom-call | flops 1200000000 | bytes 4687500 | tf_op jit(solution)/shard_map/pallas_call | solution.py:421
  41.4 0.7 %reshape.41 = bf16[1,2,8,2048]{3,2,1,0:T(8,128)(2,1)} reshape(bf16[2,8,16,128]{3,2,1,0:T(8,128)(2,1)S(1)} %shard_map.115) | data formatting | bytes 131072 | tf_op jit(solution)/shard_map/reshape | solution.py:422
  42.1 0.0 collective-permute-done.10
  42.1 0.7 %collective-permute-done.13 = bf16[32,896]{1,0:T(8,128)(2,1)S(1)} collective-permute-done((bf16[32,896]{1,0:T(8,128)(2,1)S(1)}, bf16[32,896]{1,0:T(8,128)(2,1)S(1)}, u32[]{:S(2)}, u32[]{:S(2)}) %collective-permute-start.13) | collective-permute-done | bytes 57376 | tf_op jit(solution)/shard_map/ppermute | solution.py:344
  42.8 0.5 %collective-permute-start.14 = (bf16[96,896]{1,0:T(8,128)(2,1)S(1)}, bf16[96,896]{1,0:T(8,128)(2,1)S(1)}, u32[]{:S(2)}, u32[]{:S(2)}) collective-permute-start(bf16[96,896]{1,0:T(8,128)(2,1)S(1)} %pad_maximum_fusion.m_ref), channel_id=1, source_target_pairs={{0,1},{1,0},{2,3},{3,2},{4,5},{5,4},{6,7},{7,6},{8,9},{9,8},{10,11... | collective-permute-start | bytes 516104 | tf_op jit(solution)/shard_map/ppermute | solution.py:321
  43.3 1.0 %collective-permute-done.14.h_ref = bf16[96,896]{1,0:T(8,128)(2,1)S(1)} collective-permute-done((bf16[96,896]{1,0:T(8,128)(2,1)S(1)}, bf16[96,896]{1,0:T(8,128)(2,1)S(1)}, u32[]{:S(2)}, u32[]{:S(2)}) %collective-permute-start.14) | collective-permute-done | bytes 172064 | tf_op jit(solution)/shard_map/ppermute | solution.py:321
  44.3 1.0 %shard_map.116 = (f32[64,1728]{1,0:T(8,128)}, f32[1,64]{1,0:T(1,128)}, f32[64,864]{1,0:T(8,128)}, f32[1,64]{1,0:T(1,128)}) custom-call(bf16[96,896]{1,0:T(8,128)(2,1)S(1)} %pad_maximum_fusion.m_ref, bf16[96,896]{1,0:T(8,128)(2,1)S(1)} %collective-permute-done.14.h_ref), custom_call_target="tpu_custom_call" | custom-call | flops 1200000000 | bytes 4687500 | tf_op jit(solution)/shard_map/pallas_call | solution.py:431
  (13 shorter events, 0.2 us)
Async XLA Ops:
  1.5 1.4 %collective-permute-start = (bf16[2,2,16,128]{3,2,1,0:T(8,128)(2,1)S(1)}, bf16[2,2,16,128]{3,2,1,0:T(8,128)(2,1)S(1)}, u32[]{:S(2)}, u32[]{:S(2)}) collective-permute-start(bf16[2,2,16,128]{3,2,1,0:T(8,128)(2,1)S(1)} %constant_dynamic-slice_fusion), channel_id=1, source_target_pairs={{0,1},{1,0},{2,3},{3,2},{4,5},{5,4},{6,7},{7,6},{8,9},{9,8},{10,11... | collective-permute-start | bytes 49160 | tf_op jit(solution)/shard_map/ppermute | solution.py:321
  2.9 8.6 %collective-permute-start.2 = (bf16[2,10,16,128]{3,2,1,0:T(8,128)(2,1)S(1)}, bf16[2,10,16,128]{3,2,1,0:T(8,128)(2,1)S(1)}, u32[]{:S(2)}, u32[]{:S(2)}) collective-permute-start(bf16[2,10,16,128]{3,2,1,0:T(8,128)(2,1)S(1)} %pad_maximum_fusion.1), channel_id=1, source_target_pairs={{4,8},{8,4},{5,9},{9,5},{6,10},{10,6},{7,11},{11,7},{20,24},{24,20... | collective-permute-start | bytes 245768 | tf_op jit(solution)/shard_map/ppermute | solution.py:327
  3.6 8.3 %collective-permute-start.1 = (bf16[2,10,16,128]{3,2,1,0:T(8,128)(2,1)S(1)}, bf16[2,10,16,128]{3,2,1,0:T(8,128)(2,1)S(1)}, u32[]{:S(2)}, u32[]{:S(2)}) collective-permute-start(bf16[2,10,16,128]{3,2,1,0:T(8,128)(2,1)S(1)} %pad_maximum_fusion.1), channel_id=1, source_target_pairs={{0,4},{8,12},{4,0},{12,8},{1,5},{9,13},{5,1},{13,9},{2,6},{10,14},... | collective-permute-start | bytes 245768 | tf_op jit(solution)/shard_map/ppermute | solution.py:327
  9.4 2.1 %copy-start = (bf16[1,2,8,4096]{3,2,1,0:T(8,128)(2,1)S(1)}, bf16[1,2,8,4096]{3,2,1,0:T(8,128)(2,1)}, u32[]{:S(2)}) copy-start(bf16[1,2,8,4096]{3,2,1,0:T(8,128)(2,1)} %param.11) | copy-start | bytes 393220
  14.5 1.3 %collective-permute-start.3 = (bf16[2,2,16,256]{3,2,1,0:T(8,128)(2,1)S(1)}, bf16[2,2,16,256]{3,2,1,0:T(8,128)(2,1)S(1)}, u32[]{:S(2)}, u32[]{:S(2)}) collective-permute-start(bf16[2,2,16,256]{3,2,1,0:T(8,128)(2,1)S(1)} %get-tuple-element.63), channel_id=1, source_target_pairs={{0,1},{1,0},{2,3},{3,2},{4,5},{5,4},{6,7},{7,6},{8,9},{9,8},{10,11... | collective-permute-start | bytes 98312 | tf_op jit(solution)/shard_map/ppermute | solution.py:321
  15.8 7.8 %collective-permute-start.5 = (bf16[2,10,16,256]{3,2,1,0:T(8,128)(2,1)S(1)}, bf16[2,10,16,256]{3,2,1,0:T(8,128)(2,1)S(1)}, u32[]{:S(2)}, u32[]{:S(2)}) collective-permute-start(bf16[2,10,16,256]{3,2,1,0:T(8,128)(2,1)S(1)} %constant_dynamic-update-slice_fusion), channel_id=1, source_target_pairs={{0,4},{8,12},{4,0},{12,8},{1,5},{9,13},{5,1},{13,9},{2,6},{10,14},... | collective-permute-start | bytes 491528 | tf_op jit(solution)/shard_map/ppermute | solution.py:327
  17.7 5.8 %collective-permute-start.4 = (bf16[2,10,16,256]{3,2,1,0:T(8,128)(2,1)S(1)}, bf16[2,10,16,256]{3,2,1,0:T(8,128)(2,1)S(1)}, u32[]{:S(2)}, u32[]{:S(2)}) collective-permute-start(bf16[2,10,16,256]{3,2,1,0:T(8,128)(2,1)S(1)} %constant_dynamic-update-slice_fusion), channel_id=1, source_target_pairs={{4,8},{8,4},{5,9},{9,5},{6,10},{10,6},{7,11},{11,7},{20,24},{24,20... | collective-permute-start | bytes 491528 | tf_op jit(solution)/shard_map/ppermute | solution.py:327
  18.4 5.2 %collective-permute-start.6 = (bf16[32,1792]{1,0:T(8,128)(2,1)S(1)}, bf16[32,1792]{1,0:T(8,128)(2,1)S(1)}, u32[]{:S(2)}, u32[]{:S(2)}) collective-permute-start(bf16[32,1792]{1,0:T(8,128)(2,1)S(1)} %get-tuple-element.70), channel_id=1, source_target_pairs={{0,3},{1,2},{2,1},{3,0},{4,7},{5,6},{6,5},{7,4},{8,11},{9,10},{10,... | collective-permute-start | bytes 344072 | tf_op jit(solution)/shard_map/ppermute | solution.py:344
  25.4 1.4 %collective-permute-start.7 = (bf16[64,896]{1,0:T(8,128)(2,1)S(1)}, bf16[64,896]{1,0:T(8,128)(2,1)S(1)}, u32[]{:S(2)}, u32[]{:S(2)}) collective-permute-start(bf16[64,896]{1,0:T(8,128)(2,1)S(1)} %get-tuple-element.80), channel_id=1, source_target_pairs={{0,1},{1,0},{2,3},{3,2},{4,5},{5,4},{6,7},{7,6},{8,9},{9,8},{10,11... | collective-permute-start | bytes 344072 | tf_op jit(solution)/shard_map/ppermute | solution.py:321
  26.9 4.9 %collective-permute-start.8 = (bf16[32,896]{1,0:T(8,128)(2,1)S(1)}, bf16[32,896]{1,0:T(8,128)(2,1)S(1)}, u32[]{:S(2)}, u32[]{:S(2)}) collective-permute-start(bf16[32,896]{1,0:T(8,128)(2,1)S(1)} %get-tuple-element.81), channel_id=1, source_target_pairs={{0,3},{1,2},{2,1},{3,0},{4,7},{5,6},{6,5},{7,4},{8,11},{9,10},{10,... | collective-permute-start | bytes 172040 | tf_op jit(solution)/shard_map/ppermute | solution.py:344
  28.2 5.1 %collective-permute-start.11 = (bf16[32,896]{1,0:T(8,128)(2,1)S(1)}, bf16[32,896]{1,0:T(8,128)(2,1)S(1)}, u32[]{:S(2)}, u32[]{:S(2)}) collective-permute-start(bf16[32,896]{1,0:T(8,128)(2,1)S(1)} %get-tuple-element.90), channel_id=1, source_target_pairs={{0,5},{1,4},{4,1},{5,0},{8,13},{9,12},{12,9},{13,8},{2,7},{3,6},{6... | collective-permute-start | bytes 172040 | tf_op jit(solution)/shard_map/ppermute | solution.py:344
  31.8 3.9 %collective-permute-start.9 = (bf16[32,896]{1,0:T(8,128)(2,1)S(1)}, bf16[32,896]{1,0:T(8,128)(2,1)S(1)}, u32[]{:S(2)}, u32[]{:S(2)}) collective-permute-start(bf16[32,896]{1,0:T(8,128)(2,1)S(1)} %add.23), channel_id=1, source_target_pairs={{0,5},{1,4},{4,1},{5,0},{8,13},{9,12},{12,9},{13,8},{2,7},{3,6},{6... | collective-permute-start | bytes 172040 | tf_op jit(solution)/shard_map/ppermute | solution.py:344
  33.3 4.7 %collective-permute-start.12 = (bf16[32,896]{1,0:T(8,128)(2,1)S(1)}, bf16[32,896]{1,0:T(8,128)(2,1)S(1)}, u32[]{:S(2)}, u32[]{:S(2)}) collective-permute-start(bf16[32,896]{1,0:T(8,128)(2,1)S(1)} %add.25), channel_id=1, source_target_pairs={{0,9},{1,8},{4,13},{5,12},{8,1},{9,0},{12,5},{13,4},{2,11},{3,10},... | collective-permute-start | bytes 172040 | tf_op jit(solution)/shard_map/ppermute | solution.py:344
  35.7 6.3 %collective-permute-start.10 = (bf16[32,896]{1,0:T(8,128)(2,1)S(1)}, bf16[32,896]{1,0:T(8,128)(2,1)S(1)}, u32[]{:S(2)}, u32[]{:S(2)}) collective-permute-start(bf16[32,896]{1,0:T(8,128)(2,1)S(1)} %add.24), channel_id=1, source_target_pairs={{0,9},{1,8},{4,13},{5,12},{8,1},{9,0},{12,5},{13,4},{2,11},{3,10},... | collective-permute-start | bytes 172040 | tf_op jit(solution)/shard_map/ppermute | solution.py:344
  38.0 4.8 %collective-permute-start.13 = (bf16[32,896]{1,0:T(8,128)(2,1)S(1)}, bf16[32,896]{1,0:T(8,128)(2,1)S(1)}, u32[]{:S(2)}, u32[]{:S(2)}) collective-permute-start(bf16[32,896]{1,0:T(8,128)(2,1)S(1)} %add.26), channel_id=1, source_target_pairs={{0,3},{1,2},{2,1},{3,0},{4,7},{5,6},{6,5},{7,4},{8,11},{9,10},{10,... | collective-permute-start | bytes 172040 | tf_op jit(solution)/shard_map/ppermute | solution.py:344
  42.8 1.5 %collective-permute-start.14 = (bf16[96,896]{1,0:T(8,128)(2,1)S(1)}, bf16[96,896]{1,0:T(8,128)(2,1)S(1)}, u32[]{:S(2)}, u32[]{:S(2)}) collective-permute-start(bf16[96,896]{1,0:T(8,128)(2,1)S(1)} %pad_maximum_fusion.m_ref), channel_id=1, source_target_pairs={{0,1},{1,0},{2,3},{3,2},{4,5},{5,4},{6,7},{7,6},{8,9},{9,8},{10,11... | collective-permute-start | bytes 516104 | tf_op jit(solution)/shard_map/ppermute | solution.py:321

commit v8 on v7

--- a/solution.py
+++ b/solution.py
@@ -144,18 +144,22 @@
     spread(gathered(x_ref, by_ref, ev_ref, od_ref, space), core, e_ref, IN_L)
     wide = x_ref.shape[1] + 2
     narrow = wide - 2
-    acc[...] = dot(taps(lambda a, b: e_ref[a : a + 4, b : b + wide]), f1_ref[...], NT)
-    rows = wide * ROWS
+    at, most = 1 - core, wide - 1
+    acc[...] = dot(taps(lambda a, b: e_ref[a : a + 4, pl.ds(b + at, most)]), f1_ref[...], NT)
+    rows = most * ROWS
     bias1, bias2 = b_ref[0:1], b_ref[1:2]
     for x in range(4):
         y1 = acc[x * rows : (x + 1) * rows, :] + bias1
-        mask = plane_mask(x, rows, space, last, core)
-        sig = sigmoid(y1)
-        d_ref[x] = y1.reshape(wide, ROWS, MID_L)
-        act = (y1 * sig * mask).astype(BF)
-        a_ref[x, :, :, :MID_L] = act.reshape(wide, ROWS, MID_L)
+        act = y1 * sigmoid(y1)
+        if x in (0, 3):
+            act = act * jnp.where((space > 0) if x == 0 else (space < last), 1.0, 0.0)
+        act = act.astype(BF)
+        d_ref[x, pl.ds(at, most)] = y1.reshape(most, ROWS, MID_L)
+        d_ref[x, core * most] = jnp.zeros((ROWS, MID_L), F32)
+        a_ref[x, pl.ds(at, most), :, :MID_L] = act.reshape(most, ROWS, MID_L)
         edge = edges(act.astype(F32), 0, 128)
-        a_ref[x, :, :, MID_L:] = edge.astype(BF).reshape(wide, ROWS, 128)
+        a_ref[x, pl.ds(at, most), :, MID_L:] = edge.astype(BF).reshape(most, ROWS, 128)
+        a_ref[x, core * most] = jnp.zeros((ROWS, 384), BF)
     y2 = dot(taps(lambda a, b: a_ref[a : a + 2, b : b + narrow]), f2_ref[...], NT) + bias2
     sig = sigmoid(y2)
     shape = o_ref.shape
@@ -382,7 +386,7 @@
             ((nx, ny, ROWS, MID_L), BF),
             ((nx, 2, ROWS, MID_L), BF),
         ],
-        [pltpu.VMEM(((nx + 2) * (ny + 2) * ROWS, MID_L), F32)],
+        [pltpu.VMEM(((nx + 2) * (ny + 1) * ROWS, MID_L), F32)],
     )(own, side, even, odd, f1, f2, bias, cot)
     keep2, send2 = call(
         second_weights_body, 1800000000, [((32, PACK2), F32), ((32, PACK2), BF)], [pltpu.VMEM((64, PACK2), F32)]

time: 45.5 us -> 45.4 us (level)
  no operation moved by 1% of the time
where the time goes in v8:
time: 45.4 us; the launch traced here: 45.2 us
  starting transfers between devices  23.1 us (51%)
  Pallas kernels  10.3 us (23%)
  waiting for transfers between devices  8.59 us (19%)
  local copies, waits for them, and re-layouts  2.3 us (5%)
  between operations  0.8 us (2%)
    ppermute x7, starting transfers between devices, cross(): return lax.ppermute(cells, (axis, 'ysp'), pairs)  12.7 us
    ppermute x4, starting transfers between devices, pair_swap(): return lax.ppermute(cells, 'space', pairs + [(j, i) for i, j in pairs])  9.07 us
    ppermute x7, waiting for transfers between devices, cross(): return lax.ppermute(cells, (axis, 'ysp'), pairs)  5.05 us
    ppermute x4, waiting for transfers between devices, swap(): lax.ppermute(cells, axis, [(i, i ^ bit) for i in range(lax.axis_size(axis...  3.19 us
    pallas_call x1, Pallas kernels, on_device(): call(forward_body, 4800000000, [((nx + 4, ny + 4, ROWS, 256), BF), ((nx +...  2.54 us
    pallas_call x1, Pallas kernels, on_device(): call(banded_body, 2000000000, [((256, 9 * 256), BF), ((256, 9 * 384), BF)...  2.08 us
    pallas_call x1, Pallas kernels, on_device(): call(backward_body, 5600000000, [((64, PACK1), F32), ((64, PACK1), BF), (...  1.86 us
    ppermute x4, starting transfers between devices, swap(): lax.ppermute(cells, axis, [(i, i ^ bit) for i in range(lax.axis_size(axis...  1.32 us
  transfers between devices with their start and end apart: 15, of which 9 were waited for; matrix products, arithmetic and copies ran while one was open for 3% of the time, Pallas kernels for 11%

profile of v8, /device:TPU:0, one launch (start us, length us, event | category | flops | bytes accessed | tf_op | source)
XLA Modules:
  0.0 45.2 jit_solution(16827736270865357147)
XLA Ops:
  0.6 0.9 %copy.17 = bf16[2,8,16,128]{3,2,1,0:T(8,128)(2,1)S(1)} copy(bf16[2,8,16,128]{3,1,2,0:T(8,128)(2,1)} %bitcast.27) | data formatting | bytes 131072
  1.5 0.5 %collective-permute-start = (bf16[2,2,16,128]{3,2,1,0:T(8,128)(2,1)S(1)}, bf16[2,2,16,128]{3,2,1,0:T(8,128)(2,1)S(1)}, u32[]{:S(2)}, u32[]{:S(2)}) collective-permute-start(bf16[2,2,16,128]{3,2,1,0:T(8,128)(2,1)S(1)} %constant_dynamic-slice_fusion), channel_id=1, source_target_pairs={{0,1},{1,0},{2,3},{3,2},{4,5},{5,4},{6,7},{7,6},{8,9},{9,8},{10,11... | collective-permute-start | bytes 49160 | tf_op jit(solution)/shard_map/ppermute | solution.py:325
  2.0 0.8 %collective-permute-done.by_ref = bf16[2,2,16,128]{3,2,1,0:T(8,128)(2,1)S(1)} collective-permute-done((bf16[2,2,16,128]{3,2,1,0:T(8,128)(2,1)S(1)}, bf16[2,2,16,128]{3,2,1,0:T(8,128)(2,1)S(1)}, u32[]{:S(2)}, u32[]{:S(2)}) %collective-permute-start) | collective-permute-done | bytes 16416 | tf_op jit(solution)/shard_map/ppermute | solution.py:325
  2.9 0.7 %collective-permute-start.2 = (bf16[2,10,16,128]{3,2,1,0:T(8,128)(2,1)S(1)}, bf16[2,10,16,128]{3,2,1,0:T(8,128)(2,1)S(1)}, u32[]{:S(2)}, u32[]{:S(2)}) collective-permute-start(bf16[2,10,16,128]{3,2,1,0:T(8,128)(2,1)S(1)} %pad_maximum_fusion.1), channel_id=1, source_target_pairs={{4,8},{8,4},{5,9},{9,5},{6,10},{10,6},{7,11},{11,7},{20,24},{24,20... | collective-permute-start | bytes 245768 | tf_op jit(solution)/shard_map/ppermute | solution.py:331
  3.6 5.8 %collective-permute-start.1 = (bf16[2,10,16,128]{3,2,1,0:T(8,128)(2,1)S(1)}, bf16[2,10,16,128]{3,2,1,0:T(8,128)(2,1)S(1)}, u32[]{:S(2)}, u32[]{:S(2)}) collective-permute-start(bf16[2,10,16,128]{3,2,1,0:T(8,128)(2,1)S(1)} %pad_maximum_fusion.1), channel_id=1, source_target_pairs={{0,4},{8,12},{4,0},{12,8},{1,5},{9,13},{5,1},{13,9},{2,6},{10,14},... | collective-permute-start | bytes 245768 | tf_op jit(solution)/shard_map/ppermute | solution.py:331
  9.4 0.0 copy-start
  9.4 2.1 %shard_map.109 = (bf16[256,2304]{1,0:T(8,128)(2,1)S(1)}, bf16[256,3456]{1,0:T(8,128)(2,1)S(1)}, bf16[9,384,256]{2,1,0:T(8,128)(2,1)S(1)}, bf16[9,384,128]{2,1,0:T(8,128)(2,1)S(1)}, f32[2,256]{1,0:T(2,128)S(1)}) custom-call(f32[64,864]{1,0:T(8,128)} %bitcast.29, f32[64,1728]{1,0:T(8,128)} %bitcast.28, f32[1,64]{1,0:T(1,128)} %bitcast.30, f32[1,64]{1,0:T(1,128)} %bitcast.31), custom_call_target="tpu_custom_call" | custom-call | flops 2000000000 | bytes 7812500 | tf_op jit(solution)/shard_map/pallas_call | solution.py:357
  11.4 0.0 copy-done
  11.5 0.0 collective-permute-done.2.od_ref
  11.5 0.4 collective-permute-done.1.ev_ref
  11.8 2.5 %shard_map.110 = (bf16[6,12,16,256]{3,2,1,0:T(8,128)(2,1)S(1)}, bf16[4,10,16,384]{3,2,1,0:T(8,128)(2,1)S(1)}, f32[4,10,16,256]{3,2,1,0:T(8,128)S(1)}, bf16[2,8,1...) custom-call(bf16[2,8,16,128]{3,2,1,0:T(8,128)(2,1)S(1)} %copy.17, ...), custom_call_target="tpu_custom_call" | custom-call | flops 4800000000 | bytes 18750000 | tf_op jit(solution)/shard_map/pallas_call | solution.py:378
  14.4 0.1 collective-permute-start.3
  14.5 1.0 %shard_map.111 = (f32[32,1792]{1,0:T(8,128)S(1)}, bf16[32,1792]{1,0:T(8,128)(2,1)S(1)}) custom-call(bf16[4,10,16,384]{3,2,1,0:T(8,128)(2,1)S(1)} %get-tuple-element.64.a_ref, bf16[2,8,16,256]{3,2,1,0:T(8,128)(2,1)S(1)} %get-tuple-element.62.g_ref), custom_call_target="tpu_custom_call" | custom-call | flops 1800000000 | bytes 7031250 | tf_op jit(solution)/shard_map/pallas_call | solution.py:391
  15.5 0.2 collective-permute-done.3.by_ref
  15.7 1.9 %collective-permute-start.5 = (bf16[2,10,16,256]{3,2,1,0:T(8,128)(2,1)S(1)}, bf16[2,10,16,256]{3,2,1,0:T(8,128)(2,1)S(1)}, u32[]{:S(2)}, u32[]{:S(2)}) collective-permute-start(bf16[2,10,16,256]{3,2,1,0:T(8,128)(2,1)S(1)} %constant_dynamic-update-slice_fusion), channel_id=1, source_target_pairs={{0,4},{8,12},{4,0},{12,8},{1,5},{9,13},{5,1},{13,9},{2,6},{10,14},... | collective-permute-start | bytes 491528 | tf_op jit(solution)/shard_map/ppermute | solution.py:331
  17.6 0.7 %collective-permute-start.4 = (bf16[2,10,16,256]{3,2,1,0:T(8,128)(2,1)S(1)}, bf16[2,10,16,256]{3,2,1,0:T(8,128)(2,1)S(1)}, u32[]{:S(2)}, u32[]{:S(2)}) collective-permute-start(bf16[2,10,16,256]{3,2,1,0:T(8,128)(2,1)S(1)} %constant_dynamic-update-slice_fusion), channel_id=1, source_target_pairs={{4,8},{8,4},{5,9},{9,5},{6,10},{10,6},{7,11},{11,7},{20,24},{24,20... | collective-permute-start | bytes 491528 | tf_op jit(solution)/shard_map/ppermute | solution.py:331
  18.3 1.3 %collective-permute-start.6 = (bf16[32,1792]{1,0:T(8,128)(2,1)S(1)}, bf16[32,1792]{1,0:T(8,128)(2,1)S(1)}, u32[]{:S(2)}, u32[]{:S(2)}) collective-permute-start(bf16[32,1792]{1,0:T(8,128)(2,1)S(1)} %get-tuple-element.70), channel_id=1, source_target_pairs={{0,3},{1,2},{2,1},{3,0},{4,7},{5,6},{6,5},{7,4},{8,11},{9,10},{10,... | collective-permute-start | bytes 344072 | tf_op jit(solution)/shard_map/ppermute | solution.py:348
  19.6 0.2 shard_map.112.d_ref
  19.8 3.6 %collective-permute-done.6.h2_ref = bf16[32,1792]{1,0:T(8,128)(2,1)S(1)} collective-permute-done((bf16[32,1792]{1,0:T(8,128)(2,1)S(1)}, bf16[32,1792]{1,0:T(8,128)(2,1)S(1)}, u32[]{:S(2)}, u32[]{:S(2)}) %collective-permute-start.6) | collective-permute-done | bytes 114720 | tf_op jit(solution)/shard_map/ppermute | solution.py:348
  23.5 0.0 collective-permute-done.5.ev_ref
  23.5 0.0 collective-permute-done.4.od_ref
  23.5 1.9 %shard_map.113 = (f32[64,896]{1,0:T(8,128)S(1)}, bf16[64,896]{1,0:T(8,128)(2,1)S(1)}, bf16[2,8,16,256]{3,2,1,0:T(8,128)(2,1)S(1)}) custom-call(bf16[2,8,16,256]{3,2,1,0:T(8,128)(2,1)S(1)} %get-tuple-element.62.g_ref, bf16[2,2,16,256]{3,2,1,0:T(8,128)(2,1)S(1)} %collective-permute-done.3.by_ref, bf16[2,10,16,256]{3,2,1,0:T(8,128)(2,1)S(1)} %collective-permute-done.5.ev_ref, ...), custom_call_target="tpu_custom_call" | custom-call | flops 5600000000 | bytes 21875000 | tf_op jit(solution)/shard_map/pallas_call | solution.py:398
  25.3 0.2 collective-permute-start.7
  25.6 1.1 %collective-permute-done.7 = bf16[64,896]{1,0:T(8,128)(2,1)S(1)} collective-permute-done((bf16[64,896]{1,0:T(8,128)(2,1)S(1)}, bf16[64,896]{1,0:T(8,128)(2,1)S(1)}, u32[]{:S(2)}, u32[]{:S(2)}) %collective-permute-start.7) | collective-permute-done | bytes 114720 | tf_op jit(solution)/shard_map/ppermute | solution.py:325
  26.8 1.3 %collective-permute-start.8 = (bf16[32,896]{1,0:T(8,128)(2,1)S(1)}, bf16[32,896]{1,0:T(8,128)(2,1)S(1)}, u32[]{:S(2)}, u32[]{:S(2)}) collective-permute-start(bf16[32,896]{1,0:T(8,128)(2,1)S(1)} %get-tuple-element.81), channel_id=1, source_target_pairs={{0,3},{1,2},{2,1},{3,0},{4,7},{5,6},{6,5},{7,4},{8,11},{9,10},{10,... | collective-permute-start | bytes 172040 | tf_op jit(solution)/shard_map/ppermute | solution.py:348
  28.1 2.5 %collective-permute-start.11 = (bf16[32,896]{1,0:T(8,128)(2,1)S(1)}, bf16[32,896]{1,0:T(8,128)(2,1)S(1)}, u32[]{:S(2)}, u32[]{:S(2)}) collective-permute-start(bf16[32,896]{1,0:T(8,128)(2,1)S(1)} %get-tuple-element.90), channel_id=1, source_target_pairs={{0,5},{1,4},{4,1},{5,0},{8,13},{9,12},{12,9},{13,8},{2,7},{3,6},{6... | collective-permute-start | bytes 172040 | tf_op jit(solution)/shard_map/ppermute | solution.py:348
  30.6 1.0 %shard_map.114.t_ref = bf16[4,10,16,384]{3,2,1,0:T(8,128)(2,1)S(1)} custom-call(bf16[2,8,16,256]{3,2,1,0:T(8,128)(2,1)S(1)} %get-tuple-element.62.g_ref, bf16[2,2,16,256]{3,2,1,0:T(8,128)(2,1)S(1)} %collective-permute-done.3.by_ref, bf16[2,10,16,256]{3,2,1,0:T(8,128)(2,1)S(1)} %collective-permute-done.5.ev_ref, ...), custom_call_target="tpu_custom_call" | custom-call | flops 1400000000 | bytes 5468750 | tf_op jit(solution)/shard_map/pallas_call | solution.py:410
  31.6 0.0 collective-permute-done.8
  31.7 1.5 %collective-permute-start.9 = (bf16[32,896]{1,0:T(8,128)(2,1)S(1)}, bf16[32,896]{1,0:T(8,128)(2,1)S(1)}, u32[]{:S(2)}, u32[]{:S(2)}) collective-permute-start(bf16[32,896]{1,0:T(8,128)(2,1)S(1)} %add.23), channel_id=1, source_target_pairs={{0,5},{1,4},{4,1},{5,0},{8,13},{9,12},{12,9},{13,8},{2,7},{3,6},{6... | collective-permute-start | bytes 172040 | tf_op jit(solution)/shard_map/ppermute | solution.py:348
  33.2 0.0 collective-permute-done.11
  33.2 1.5 %collective-permute-start.12 = (bf16[32,896]{1,0:T(8,128)(2,1)S(1)}, bf16[32,896]{1,0:T(8,128)(2,1)S(1)}, u32[]{:S(2)}, u32[]{:S(2)}) collective-permute-start(bf16[32,896]{1,0:T(8,128)(2,1)S(1)} %add.25), channel_id=1, source_target_pairs={{0,9},{1,8},{4,13},{5,12},{8,1},{9,0},{12,5},{13,4},{2,11},{3,10},... | collective-permute-start | bytes 172040 | tf_op jit(solution)/shard_map/ppermute | solution.py:348
  34.7 0.7 %reshape.40 = bf16[1,2,8,4096]{3,2,1,0:T(8,128)(2,1)} reshape(bf16[2,8,16,256]{3,2,1,0:T(8,128)(2,1)S(1)} %get-tuple-element.84) | data formatting | bytes 262144 | tf_op jit(solution)/shard_map/reshape | solution.py:416
  35.4 0.2 collective-permute-done.9
  35.6 1.8 %collective-permute-start.10 = (bf16[32,896]{1,0:T(8,128)(2,1)S(1)}, bf16[32,896]{1,0:T(8,128)(2,1)S(1)}, u32[]{:S(2)}, u32[]{:S(2)}) collective-permute-start(bf16[32,896]{1,0:T(8,128)(2,1)S(1)} %add.24), channel_id=1, source_target_pairs={{0,9},{1,8},{4,13},{5,12},{8,1},{9,0},{12,5},{13,4},{2,11},{3,10},... | collective-permute-start | bytes 172040 | tf_op jit(solution)/shard_map/ppermute | solution.py:348
  37.4 0.5 %collective-permute-done.12 = bf16[32,896]{1,0:T(8,128)(2,1)S(1)} collective-permute-done((bf16[32,896]{1,0:T(8,128)(2,1)S(1)}, bf16[32,896]{1,0:T(8,128)(2,1)S(1)}, u32[]{:S(2)}, u32[]{:S(2)}) %collective-permute-start.12) | collective-permute-done | bytes 57376 | tf_op jit(solution)/shard_map/ppermute | solution.py:348
  37.9 2.7 %collective-permute-start.13 = (bf16[32,896]{1,0:T(8,128)(2,1)S(1)}, bf16[32,896]{1,0:T(8,128)(2,1)S(1)}, u32[]{:S(2)}, u32[]{:S(2)}) collective-permute-start(bf16[32,896]{1,0:T(8,128)(2,1)S(1)} %add.26), channel_id=1, source_target_pairs={{0,3},{1,2},{2,1},{3,0},{4,7},{5,6},{6,5},{7,4},{8,11},{9,10},{10,... | collective-permute-start | bytes 172040 | tf_op jit(solution)/shard_map/ppermute | solution.py:348
  40.7 0.6 %shard_map.115 = bf16[2,8,16,128]{3,2,1,0:T(8,128)(2,1)S(1)} custom-call(bf16[4,10,16,384]{3,2,1,0:T(8,128)(2,1)S(1)} %shard_map.114.t_ref, bf16[9,384,128]{2,1,0:T(8,128)(2,1)S(1)} %get-tuple-element.88.r1_ref), custom_call_target="tpu_custom_call" | custom-call | flops 1200000000 | bytes 4687500 | tf_op jit(solution)/shard_map/pallas_call | solution.py:425
  41.3 0.7 %reshape.41 = bf16[1,2,8,2048]{3,2,1,0:T(8,128)(2,1)} reshape(bf16[2,8,16,128]{3,2,1,0:T(8,128)(2,1)S(1)} %shard_map.115) | data formatting | bytes 131072 | tf_op jit(solution)/shard_map/reshape | solution.py:426
  41.9 0.0 collective-permute-done.10
  42.0 0.7 %collective-permute-done.13 = bf16[32,896]{1,0:T(8,128)(2,1)S(1)} collective-permute-done((bf16[32,896]{1,0:T(8,128)(2,1)S(1)}, bf16[32,896]{1,0:T(8,128)(2,1)S(1)}, u32[]{:S(2)}, u32[]{:S(2)}) %collective-permute-start.13) | collective-permute-done | bytes 57376 | tf_op jit(solution)/shard_map/ppermute | solution.py:348
  42.7 0.5 %collective-permute-start.14 = (bf16[96,896]{1,0:T(8,128)(2,1)S(1)}, bf16[96,896]{1,0:T(8,128)(2,1)S(1)}, u32[]{:S(2)}, u32[]{:S(2)}) collective-permute-start(bf16[96,896]{1,0:T(8,128)(2,1)S(1)} %pad_maximum_fusion.m_ref), channel_id=1, source_target_pairs={{0,1},{1,0},{2,3},{3,2},{4,5},{5,4},{6,7},{7,6},{8,9},{9,8},{10,11... | collective-permute-start | bytes 516104 | tf_op jit(solution)/shard_map/ppermute | solution.py:325
  43.2 1.0 %collective-permute-done.14.h_ref = bf16[96,896]{1,0:T(8,128)(2,1)S(1)} collective-permute-done((bf16[96,896]{1,0:T(8,128)(2,1)S(1)}, bf16[96,896]{1,0:T(8,128)(2,1)S(1)}, u32[]{:S(2)}, u32[]{:S(2)}) %collective-permute-start.14) | collective-permute-done | bytes 172064 | tf_op jit(solution)/shard_map/ppermute | solution.py:325
  44.2 1.0 %shard_map.116 = (f32[64,1728]{1,0:T(8,128)}, f32[1,64]{1,0:T(1,128)}, f32[64,864]{1,0:T(8,128)}, f32[1,64]{1,0:T(1,128)}) custom-call(bf16[96,896]{1,0:T(8,128)(2,1)S(1)} %pad_maximum_fusion.m_ref, bf16[96,896]{1,0:T(8,128)(2,1)S(1)} %collective-permute-done.14.h_ref), custom_call_target="tpu_custom_call" | custom-call | flops 1200000000 | bytes 4687500 | tf_op jit(solution)/shard_map/pallas_call | solution.py:435
  (13 shorter events, 0.2 us)
Async XLA Ops:
  1.5 1.4 %collective-permute-start = (bf16[2,2,16,128]{3,2,1,0:T(8,128)(2,1)S(1)}, bf16[2,2,16,128]{3,2,1,0:T(8,128)(2,1)S(1)}, u32[]{:S(2)}, u32[]{:S(2)}) collective-permute-start(bf16[2,2,16,128]{3,2,1,0:T(8,128)(2,1)S(1)} %constant_dynamic-slice_fusion), channel_id=1, source_target_pairs={{0,1},{1,0},{2,3},{3,2},{4,5},{5,4},{6,7},{7,6},{8,9},{9,8},{10,11... | collective-permute-start | bytes 49160 | tf_op jit(solution)/shard_map/ppermute | solution.py:325
  2.9 8.6 %collective-permute-start.2 = (bf16[2,10,16,128]{3,2,1,0:T(8,128)(2,1)S(1)}, bf16[2,10,16,128]{3,2,1,0:T(8,128)(2,1)S(1)}, u32[]{:S(2)}, u32[]{:S(2)}) collective-permute-start(bf16[2,10,16,128]{3,2,1,0:T(8,128)(2,1)S(1)} %pad_maximum_fusion.1), channel_id=1, source_target_pairs={{4,8},{8,4},{5,9},{9,5},{6,10},{10,6},{7,11},{11,7},{20,24},{24,20... | collective-permute-start | bytes 245768 | tf_op jit(solution)/shard_map/ppermute | solution.py:331
  3.6 8.3 %collective-permute-start.1 = (bf16[2,10,16,128]{3,2,1,0:T(8,128)(2,1)S(1)}, bf16[2,10,16,128]{3,2,1,0:T(8,128)(2,1)S(1)}, u32[]{:S(2)}, u32[]{:S(2)}) collective-permute-start(bf16[2,10,16,128]{3,2,1,0:T(8,128)(2,1)S(1)} %pad_maximum_fusion.1), channel_id=1, source_target_pairs={{0,4},{8,12},{4,0},{12,8},{1,5},{9,13},{5,1},{13,9},{2,6},{10,14},... | collective-permute-start | bytes 245768 | tf_op jit(solution)/shard_map/ppermute | solution.py:331
  9.4 2.1 %copy-start = (bf16[1,2,8,4096]{3,2,1,0:T(8,128)(2,1)S(1)}, bf16[1,2,8,4096]{3,2,1,0:T(8,128)(2,1)}, u32[]{:S(2)}) copy-start(bf16[1,2,8,4096]{3,2,1,0:T(8,128)(2,1)} %param.11) | copy-start | bytes 393220
  14.4 1.3 %collective-permute-start.3 = (bf16[2,2,16,256]{3,2,1,0:T(8,128)(2,1)S(1)}, bf16[2,2,16,256]{3,2,1,0:T(8,128)(2,1)S(1)}, u32[]{:S(2)}, u32[]{:S(2)}) collective-permute-start(bf16[2,2,16,256]{3,2,1,0:T(8,128)(2,1)S(1)} %get-tuple-element.63), channel_id=1, source_target_pairs={{0,1},{1,0},{2,3},{3,2},{4,5},{5,4},{6,7},{7,6},{8,9},{9,8},{10,11... | collective-permute-start | bytes 98312 | tf_op jit(solution)/shard_map/ppermute | solution.py:325
  15.7 7.8 %collective-permute-start.5 = (bf16[2,10,16,256]{3,2,1,0:T(8,128)(2,1)S(1)}, bf16[2,10,16,256]{3,2,1,0:T(8,128)(2,1)S(1)}, u32[]{:S(2)}, u32[]{:S(2)}) collective-permute-start(bf16[2,10,16,256]{3,2,1,0:T(8,128)(2,1)S(1)} %constant_dynamic-update-slice_fusion), channel_id=1, source_target_pairs={{0,4},{8,12},{4,0},{12,8},{1,5},{9,13},{5,1},{13,9},{2,6},{10,14},... | collective-permute-start | bytes 491528 | tf_op jit(solution)/shard_map/ppermute | solution.py:331
  17.6 5.8 %collective-permute-start.4 = (bf16[2,10,16,256]{3,2,1,0:T(8,128)(2,1)S(1)}, bf16[2,10,16,256]{3,2,1,0:T(8,128)(2,1)S(1)}, u32[]{:S(2)}, u32[]{:S(2)}) collective-permute-start(bf16[2,10,16,256]{3,2,1,0:T(8,128)(2,1)S(1)} %constant_dynamic-update-slice_fusion), channel_id=1, source_target_pairs={{4,8},{8,4},{5,9},{9,5},{6,10},{10,6},{7,11},{11,7},{20,24},{24,20... | collective-permute-start | bytes 491528 | tf_op jit(solution)/shard_map/ppermute | solution.py:331
  18.3 5.2 %collective-permute-start.6 = (bf16[32,1792]{1,0:T(8,128)(2,1)S(1)}, bf16[32,1792]{1,0:T(8,128)(2,1)S(1)}, u32[]{:S(2)}, u32[]{:S(2)}) collective-permute-start(bf16[32,1792]{1,0:T(8,128)(2,1)S(1)} %get-tuple-element.70), channel_id=1, source_target_pairs={{0,3},{1,2},{2,1},{3,0},{4,7},{5,6},{6,5},{7,4},{8,11},{9,10},{10,... | collective-permute-start | bytes 344072 | tf_op jit(solution)/shard_map/ppermute | solution.py:348
  25.3 1.4 %collective-permute-start.7 = (bf16[64,896]{1,0:T(8,128)(2,1)S(1)}, bf16[64,896]{1,0:T(8,128)(2,1)S(1)}, u32[]{:S(2)}, u32[]{:S(2)}) collective-permute-start(bf16[64,896]{1,0:T(8,128)(2,1)S(1)} %get-tuple-element.80), channel_id=1, source_target_pairs={{0,1},{1,0},{2,3},{3,2},{4,5},{5,4},{6,7},{7,6},{8,9},{9,8},{10,11... | collective-permute-start | bytes 344072 | tf_op jit(solution)/shard_map/ppermute | solution.py:325
  26.8 4.9 %collective-permute-start.8 = (bf16[32,896]{1,0:T(8,128)(2,1)S(1)}, bf16[32,896]{1,0:T(8,128)(2,1)S(1)}, u32[]{:S(2)}, u32[]{:S(2)}) collective-permute-start(bf16[32,896]{1,0:T(8,128)(2,1)S(1)} %get-tuple-element.81), channel_id=1, source_target_pairs={{0,3},{1,2},{2,1},{3,0},{4,7},{5,6},{6,5},{7,4},{8,11},{9,10},{10,... | collective-permute-start | bytes 172040 | tf_op jit(solution)/shard_map/ppermute | solution.py:348
  28.1 5.1 %collective-permute-start.11 = (bf16[32,896]{1,0:T(8,128)(2,1)S(1)}, bf16[32,896]{1,0:T(8,128)(2,1)S(1)}, u32[]{:S(2)}, u32[]{:S(2)}) collective-permute-start(bf16[32,896]{1,0:T(8,128)(2,1)S(1)} %get-tuple-element.90), channel_id=1, source_target_pairs={{0,5},{1,4},{4,1},{5,0},{8,13},{9,12},{12,9},{13,8},{2,7},{3,6},{6... | collective-permute-start | bytes 172040 | tf_op jit(solution)/shard_map/ppermute | solution.py:348
  31.7 3.9 %collective-permute-start.9 = (bf16[32,896]{1,0:T(8,128)(2,1)S(1)}, bf16[32,896]{1,0:T(8,128)(2,1)S(1)}, u32[]{:S(2)}, u32[]{:S(2)}) collective-permute-start(bf16[32,896]{1,0:T(8,128)(2,1)S(1)} %add.23), channel_id=1, source_target_pairs={{0,5},{1,4},{4,1},{5,0},{8,13},{9,12},{12,9},{13,8},{2,7},{3,6},{6... | collective-permute-start | bytes 172040 | tf_op jit(solution)/shard_map/ppermute | solution.py:348
  33.2 4.7 %collective-permute-start.12 = (bf16[32,896]{1,0:T(8,128)(2,1)S(1)}, bf16[32,896]{1,0:T(8,128)(2,1)S(1)}, u32[]{:S(2)}, u32[]{:S(2)}) collective-permute-start(bf16[32,896]{1,0:T(8,128)(2,1)S(1)} %add.25), channel_id=1, source_target_pairs={{0,9},{1,8},{4,13},{5,12},{8,1},{9,0},{12,5},{13,4},{2,11},{3,10},... | collective-permute-start | bytes 172040 | tf_op jit(solution)/shard_map/ppermute | solution.py:348
  35.6 6.3 %collective-permute-start.10 = (bf16[32,896]{1,0:T(8,128)(2,1)S(1)}, bf16[32,896]{1,0:T(8,128)(2,1)S(1)}, u32[]{:S(2)}, u32[]{:S(2)}) collective-permute-start(bf16[32,896]{1,0:T(8,128)(2,1)S(1)} %add.24), channel_id=1, source_target_pairs={{0,9},{1,8},{4,13},{5,12},{8,1},{9,0},{12,5},{13,4},{2,11},{3,10},... | collective-permute-start | bytes 172040 | tf_op jit(solution)/shard_map/ppermute | solution.py:348
  37.9 4.8 %collective-permute-start.13 = (bf16[32,896]{1,0:T(8,128)(2,1)S(1)}, bf16[32,896]{1,0:T(8,128)(2,1)S(1)}, u32[]{:S(2)}, u32[]{:S(2)}) collective-permute-start(bf16[32,896]{1,0:T(8,128)(2,1)S(1)} %add.26), channel_id=1, source_target_pairs={{0,3},{1,2},{2,1},{3,0},{4,7},{5,6},{6,5},{7,4},{8,11},{9,10},{10,... | collective-permute-start | bytes 172040 | tf_op jit(solution)/shard_map/ppermute | solution.py:348
  42.7 1.5 %collective-permute-start.14 = (bf16[96,896]{1,0:T(8,128)(2,1)S(1)}, bf16[96,896]{1,0:T(8,128)(2,1)S(1)}, u32[]{:S(2)}, u32[]{:S(2)}) collective-permute-start(bf16[96,896]{1,0:T(8,128)(2,1)S(1)} %pad_maximum_fusion.m_ref), channel_id=1, source_target_pairs={{0,1},{1,0},{2,3},{3,2},{4,5},{5,4},{6,7},{7,6},{8,9},{9,8},{10,11... | collective-permute-start | bytes 516104 | tf_op jit(solution)/shard_map/ppermute | solution.py:325
